TPU v7x, 32 devices: a whole 2x2x4 slice. The times are simulated.
32 devices in a mesh: tp: 4 (over x, core), sp: 8 (over z, y).
Axes of the slice: x: 2, y: 2, z: 4, core: 2. Of those that a mesh axis runs over, the one named last changes fastest.
Arguments:
- tokens: bfloat16 [16384, 768], P('sp'), may hold values from -6 to 6
- condition: float32 [4, 768], replicated, may hold values from -6 to 6
- clip_ids: int32 [64], replicated, may hold values from 0 to 3, as said below
- w_mod: bfloat16 [768, 6912], P('sp'), may hold values from -0.21875 to 0.21875
- w_qkv_s: bfloat16 [3, 768, 768], P(None, 'sp', 'tp'), may hold values from -0.21875 to 0.21875
- w_o_s: bfloat16 [768, 768], P('tp', 'sp'), may hold values from -2.5 to 2.5
- w_qkv_t: bfloat16 [3, 768, 768], P(None, 'sp', 'tp'), may hold values from -0.21875 to 0.21875
- w_o_t: bfloat16 [768, 768], P('tp', 'sp'), may hold values from -0.875 to 0.875
- w_up: bfloat16 [768, 3072], P('sp', 'tp'), may hold values from -0.21875 to 0.21875
- w_down: bfloat16 [3072, 768], P('tp', 'sp'), may hold values from -0.109375 to 0.109375
- grad_out: bfloat16 [16384, 768], P('sp'), may hold values from -6 to 6
Outputs:
- block_out: bfloat16 [16384, 768], P('sp')
- grad_tokens: bfloat16 [16384, 768], P('sp')
- grad_condition: float32 [4, 768], replicated
- grad_w_mod: float32 [768, 6912], P('sp')
- grad_w_qkv_s: float32 [3, 768, 768], P(None, 'sp', 'tp')
- grad_w_o_s: float32 [768, 768], P('tp', 'sp')
- grad_w_qkv_t: float32 [3, 768, 768], P(None, 'sp', 'tp')
- grad_w_o_t: float32 [768, 768], P('tp', 'sp')
- grad_w_up: float32 [768, 3072], P('sp', 'tp')
- grad_w_down: float32 [3072, 768], P('tp', 'sp')
Inputs may be any that keep to these rules, and one draw needn't show every extreme that they name: `clip_ids`: each of the 4 clips holds 1 to 32 frames, which need not be consecutive, and one holds exactly 32; the first and the last frame belong to the same clip.
All inputs are finite; a program needn't handle non-finite values.
Results may differ from a plain program's by a relative error of at most 0.025.
Values may be sent and summed in bfloat16 or wider, within the bound.
No kernel may reach another device: no remote copies, remote signals or barrier semaphores. Data moves between devices by JAX's collectives and lax.ppermute only.
A program may use at most 256 MiB of HBM per device.

v0:
```python
import jax
import jax.numpy as jnp
from jax import lax
from jax.sharding import PartitionSpec as P

HD = 64
PATCHES = 256


EPSILON = 1e-06
HIGHEST_PRECISION = lax.Precision.HIGHEST


def norm_rows(operand):
    row_mean = jnp.mean(operand, axis=-1, keepdims=True)
    centred = operand - row_mean
    inverse = lax.rsqrt(jnp.mean(centred * centred, axis=-1, keepdims=True) + EPSILON)
    return (centred * inverse, inverse)


def norm_back(incoming, normed, inverse):
    first_mean = jnp.mean(incoming, axis=-1, keepdims=True)
    second_mean = jnp.mean(incoming * normed, axis=-1, keepdims=True)
    return inverse * (incoming - first_mean - normed * second_mean)


def gelu_tanh(operand):
    return jax.nn.gelu(operand, approximate=True)


def heads_sum(term_value):
    return lax.psum(term_value, "tp").astype(jnp.float32)


def grads_sum(term_value):
    return lax.psum(term_value.astype(jnp.bfloat16), "tp").astype(jnp.float32)


def attend(query_rows, key_rows, value_rows, score_form, mix_form, same_clip):
    scores = (
        jnp.einsum(score_form, query_rows, key_rows, preferred_element_type=jnp.float32) * 0.125
    )
    if same_clip is not None:
        scores = jnp.where(same_clip, scores, -1e30)
    log_total = jax.nn.logsumexp(scores, axis=-1, keepdims=True)
    weights = jnp.exp(scores - log_total).astype(jnp.bfloat16)
    mix_out = jnp.einsum(mix_form, weights, value_rows, preferred_element_type=jnp.float32)
    return (mix_out.astype(jnp.bfloat16), log_total)


def attend_back(
    query_rows,
    key_rows,
    value_rows,
    log_total,
    grad_mixed,
    score_form,
    mix_form,
    pair_form,
    same_clip,
):
    scores = (
        jnp.einsum(score_form, query_rows, key_rows, preferred_element_type=jnp.float32) * 0.125
    )
    if same_clip is not None:
        scores = jnp.where(same_clip, scores, -1e30)
    probabilities = jnp.exp(scores - log_total)
    weights = probabilities.astype(jnp.bfloat16)
    grad_weights = jnp.einsum(
        score_form, grad_mixed, value_rows, preferred_element_type=jnp.float32
    )
    grad_values = jnp.einsum(pair_form, weights, grad_mixed, preferred_element_type=jnp.float32)
    row_terms = jnp.sum(probabilities * grad_weights, axis=-1, keepdims=True)
    grad_scores = (probabilities * (grad_weights - row_terms)).astype(jnp.bfloat16)
    grad_queries = (
        jnp.einsum(mix_form, grad_scores, key_rows, preferred_element_type=jnp.float32) * 0.125
    )
    grad_keys = (
        jnp.einsum(pair_form, grad_scores, query_rows, preferred_element_type=jnp.float32) * 0.125
    )
    return (
        grad_queries.astype(jnp.bfloat16),
        grad_keys.astype(jnp.bfloat16),
        grad_values.astype(jnp.bfloat16),
    )


def shards(
    tokens, condition, clip_ids, w_mod, w_qkv_s, w_o_s, w_qkv_t, w_o_t, w_up, w_down, grad_out
):
    full_qs, full_os, full_qt, full_ot, full_up, full_down = (
        lax.all_gather(w_qkv_s, "sp", axis=1, tiled=True),
        lax.all_gather(w_o_s, "sp", axis=1, tiled=True),
        lax.all_gather(w_qkv_t, "sp", axis=1, tiled=True),
        lax.all_gather(w_o_t, "sp", axis=1, tiled=True),
        lax.all_gather(w_up, "sp", axis=0, tiled=True),
        lax.all_gather(w_down, "sp", axis=1, tiled=True),
    )
    model_width = tokens.shape[1]
    frame_count = tokens.shape[0] // PATCHES
    head_local = full_qs.shape[2] // HD
    first_frame = lax.axis_index("sp") * frame_count
    local_ids = lax.dynamic_slice_in_dim(clip_ids, first_frame, frame_count)
    clip_count = condition.shape[0]
    selector = (local_ids[:, None] == jnp.arange(clip_count, dtype=jnp.int32)[None, :]).astype(
        jnp.float32
    )
    cond_act = jax.nn.silu(condition).astype(jnp.bfloat16)
    row_count = w_mod.shape[0]
    cond_rows = lax.dynamic_slice_in_dim(
        cond_act, lax.axis_index("sp") * row_count, row_count, axis=1
    )
    modulation = lax.psum(jnp.dot(cond_rows, w_mod, preferred_element_type=jnp.float32), "sp")
    frame_mod = jnp.dot(selector, modulation, precision=HIGHEST_PRECISION)[:, None, :]
    mod_parts = [
        frame_mod[:, :, member * model_width : (member + 1) * model_width] for member in range(9)
    ]
    residual = tokens.astype(jnp.float32).reshape(frame_count, PATCHES, model_width)
    normed_one, inverse_one = norm_rows(residual)
    input_one = (normed_one * (1.0 + mod_parts[1]) + mod_parts[0]).astype(jnp.bfloat16)
    proj_one = jnp.einsum(
        "fpd,sde->sfpe", input_one, full_qs, preferred_element_type=jnp.float32
    ).astype(jnp.bfloat16)
    heads_one = proj_one.reshape(3, frame_count, PATCHES, head_local, HD)
    mix_one, total_one = attend(
        heads_one[0], heads_one[1], heads_one[2], "aqhe,akhe->ahqk", "ahqk,akhe->aqhe", None
    )
    flat_one = mix_one.reshape(frame_count, PATCHES, -1)
    branch_one = heads_sum(
        jnp.einsum("fpe,ed->fpd", flat_one, full_os, preferred_element_type=jnp.float32).astype(
            jnp.bfloat16
        )
    )
    after_one = residual + mod_parts[2] * branch_one
    normed_two, inverse_two = norm_rows(after_one)
    input_two = (normed_two * (1.0 + mod_parts[4]) + mod_parts[3]).astype(jnp.bfloat16)
    proj_two = jnp.einsum(
        "fpd,sde->sfpe", input_two, full_qt, preferred_element_type=jnp.float32
    ).astype(jnp.bfloat16)
    positions = lax.all_to_all(proj_two, "sp", split_axis=2, concat_axis=1, tiled=True)
    all_frames = positions.shape[1]
    patch_local = positions.shape[2]
    heads_two = positions.reshape(3, all_frames, patch_local, head_local, HD)
    same_clip = clip_ids[:, None] == clip_ids[None, :]
    mix_two, total_two = attend(
        heads_two[0], heads_two[1], heads_two[2], "qahe,kahe->ahqk", "ahqk,kahe->qahe", same_clip
    )
    back_two = lax.all_to_all(
        mix_two.reshape(all_frames, patch_local, -1), "sp", split_axis=0, concat_axis=1, tiled=True
    )
    branch_two = heads_sum(
        jnp.einsum("fpe,ed->fpd", back_two, full_ot, preferred_element_type=jnp.float32).astype(
            jnp.bfloat16
        )
    )
    after_two = after_one + mod_parts[5] * branch_two
    normed_three, inverse_three = norm_rows(after_two)
    input_three = (normed_three * (1.0 + mod_parts[7]) + mod_parts[6]).astype(jnp.bfloat16)
    hidden_pre = jnp.einsum("fpd,dh->fph", input_three, full_up, preferred_element_type=jnp.float32)
    hidden = gelu_tanh(hidden_pre).astype(jnp.bfloat16)
    branch_three = heads_sum(
        jnp.einsum("fph,hd->fpd", hidden, full_down, preferred_element_type=jnp.float32).astype(
            jnp.bfloat16
        )
    )
    output = after_two + mod_parts[8] * branch_three
    block_out = output.reshape(-1, model_width).astype(jnp.bfloat16)
    mod_grads = [None] * 9
    grad_res = grad_out.astype(jnp.float32).reshape(frame_count, PATCHES, model_width)
    mod_grads[8] = jnp.sum(grad_res * branch_three, axis=1)
    grad_branch = (mod_parts[8] * grad_res).astype(jnp.bfloat16)
    grad_down = jnp.einsum("fph,fpd->hd", hidden, grad_branch, preferred_element_type=jnp.float32)
    grad_hidden = jnp.einsum(
        "fpd,hd->fph", grad_branch, full_down, preferred_element_type=jnp.float32
    )
    unused_value, gelu_pull = jax.vjp(gelu_tanh, hidden_pre)
    grad_pre = gelu_pull(grad_hidden)[0].astype(jnp.bfloat16)
    grad_up = jnp.einsum("fpd,fph->dh", input_three, grad_pre, preferred_element_type=jnp.float32)
    grad_in3 = grads_sum(
        jnp.einsum("fph,dh->fpd", grad_pre, full_up, preferred_element_type=jnp.float32)
    )
    mod_grads[6] = jnp.sum(grad_in3, axis=1)
    mod_grads[7] = jnp.sum(grad_in3 * normed_three, axis=1)
    grad_res = grad_res + norm_back(grad_in3 * (1.0 + mod_parts[7]), normed_three, inverse_three)
    mod_grads[5] = jnp.sum(grad_res * branch_two, axis=1)
    grad_branch = (mod_parts[5] * grad_res).astype(jnp.bfloat16)
    grad_ot = jnp.einsum("fpe,fpd->ed", back_two, grad_branch, preferred_element_type=jnp.float32)
    grad_mix = jnp.einsum(
        "fpd,ed->fpe", grad_branch, full_ot, preferred_element_type=jnp.float32
    ).astype(jnp.bfloat16)
    grad_pos = lax.all_to_all(grad_mix, "sp", split_axis=1, concat_axis=0, tiled=True).reshape(
        all_frames, patch_local, head_local, HD
    )
    grads_two = attend_back(
        heads_two[0],
        heads_two[1],
        heads_two[2],
        total_two,
        grad_pos,
        "qahe,kahe->ahqk",
        "ahqk,kahe->qahe",
        "ahqk,qahe->kahe",
        same_clip,
    )
    stacked = jnp.stack(grads_two).reshape(3, all_frames, patch_local, -1)
    grad_proj_two = lax.all_to_all(stacked, "sp", split_axis=1, concat_axis=2, tiled=True)
    grad_qt = jnp.einsum(
        "fpd,sfpe->sde", input_two, grad_proj_two, preferred_element_type=jnp.float32
    )
    grad_in2 = grads_sum(
        jnp.einsum("sfpe,sde->fpd", grad_proj_two, full_qt, preferred_element_type=jnp.float32)
    )
    mod_grads[3] = jnp.sum(grad_in2, axis=1)
    mod_grads[4] = jnp.sum(grad_in2 * normed_two, axis=1)
    grad_res = grad_res + norm_back(grad_in2 * (1.0 + mod_parts[4]), normed_two, inverse_two)
    mod_grads[2] = jnp.sum(grad_res * branch_one, axis=1)
    grad_branch = (mod_parts[2] * grad_res).astype(jnp.bfloat16)
    grad_os = jnp.einsum("fpe,fpd->ed", flat_one, grad_branch, preferred_element_type=jnp.float32)
    grad_mix_one = jnp.einsum(
        "fpd,ed->fpe", grad_branch, full_os, preferred_element_type=jnp.float32
    ).astype(jnp.bfloat16)
    grads_one = attend_back(
        heads_one[0],
        heads_one[1],
        heads_one[2],
        total_one,
        grad_mix_one.reshape(frame_count, PATCHES, head_local, HD),
        "aqhe,akhe->ahqk",
        "ahqk,akhe->aqhe",
        "ahqk,aqhe->akhe",
        None,
    )
    grad_proj_one = jnp.stack(grads_one).reshape(3, frame_count, PATCHES, -1)
    grad_qs = jnp.einsum(
        "fpd,sfpe->sde", input_one, grad_proj_one, preferred_element_type=jnp.float32
    )
    grad_in1 = grads_sum(
        jnp.einsum("sfpe,sde->fpd", grad_proj_one, full_qs, preferred_element_type=jnp.float32)
    )
    mod_grads[0] = jnp.sum(grad_in1, axis=1)
    mod_grads[1] = jnp.sum(grad_in1 * normed_one, axis=1)
    grad_res = grad_res + norm_back(grad_in1 * (1.0 + mod_parts[1]), normed_one, inverse_one)
    grad_tokens = grad_res.reshape(-1, model_width).astype(jnp.bfloat16)
    frame_grads = jnp.concatenate(mod_grads, axis=-1)
    clip_grads = lax.psum(jnp.dot(selector.T, frame_grads, precision=HIGHEST_PRECISION), "sp")
    clip_low = clip_grads.astype(jnp.bfloat16)
    grad_mod = jnp.dot(cond_rows.T, clip_low, preferred_element_type=jnp.float32)
    grad_act = lax.all_gather(
        jnp.dot(clip_low, w_mod.T, preferred_element_type=jnp.float32), "sp", axis=1, tiled=True
    )
    unused_act, silu_pull = jax.vjp(jax.nn.silu, condition)
    grad_condition = silu_pull(grad_act)[0]
    sum_qs, sum_os, sum_qt, sum_ot, sum_up, sum_down = (
        lax.psum_scatter(grad_qs, "sp", scatter_dimension=1, tiled=True),
        lax.psum_scatter(grad_os, "sp", scatter_dimension=1, tiled=True),
        lax.psum_scatter(grad_qt, "sp", scatter_dimension=1, tiled=True),
        lax.psum_scatter(grad_ot, "sp", scatter_dimension=1, tiled=True),
        lax.psum_scatter(grad_up, "sp", scatter_dimension=0, tiled=True),
        lax.psum_scatter(grad_down, "sp", scatter_dimension=1, tiled=True),
    )
    return (
        block_out,
        grad_tokens,
        grad_condition,
        grad_mod,
        sum_qs,
        sum_os,
        sum_qt,
        sum_ot,
        sum_up,
        sum_down,
    )


def solution(mesh):
    placed = (
        P("sp", None),
        P(),
        P(),
        P("sp", None),
        P(None, "sp", "tp"),
        P("tp", "sp"),
        P(None, "sp", "tp"),
        P("tp", "sp"),
        P("sp", "tp"),
        P("tp", "sp"),
        P("sp", None),
    )
    return jax.shard_map(
        shards,
        mesh=mesh,
        in_specs=placed,
        out_specs=(
            P("sp", None),
            P("sp", None),
            P(),
            P("sp", None),
            P(None, "sp", "tp"),
            P("tp", "sp"),
            P(None, "sp", "tp"),
            P("tp", "sp"),
            P("sp", "tp"),
            P("tp", "sp"),
        ),
        check_vma=False,
    )
```

profile of v0, /device:TPU:0, one launch (start us, length us, event | category | flops | bytes accessed | tf_op | source)
XLA Modules:
  0.0 1388.4 jit_solution(1560362934817548284)
XLA Ops:
  15.6 39.2 %all_gather.21 = bf16[3,768,192]{2,0,1:T(4,128)(2,1)S(1)} all-gather(bf16[3,96,192]{2,0,1:T(4,128)(2,1)S(1)} %copy.155), channel_id=1, replica_groups=mesh['tp'=4,'sp'=8] {'sp'}, dimensions={1}, use_global_device_ids=true | all-gather | bytes 995328 | tf_op jit(solution)/shard_map/all_gather | solution.py:92
  57.0 31.3 %all_gather.22 = bf16[192,768]{0,1:T(8,128)(2,1)S(1)} all-gather(bf16[192,96]{0,1:T(8,128)(2,1)S(1)} %copy.158), channel_id=1, replica_groups=mesh['tp'=4,'sp'=8] {'sp'}, dimensions={1}, use_global_device_ids=true | all-gather | bytes 331776 | tf_op jit(solution)/shard_map/all_gather | solution.py:93
  103.1 35.4 %all_gather.23 = bf16[3,768,192]{2,0,1:T(4,128)(2,1)S(1)} all-gather(bf16[3,96,192]{2,0,1:T(4,128)(2,1)S(1)} %copy.160), channel_id=1, replica_groups=mesh['tp'=4,'sp'=8] {'sp'}, dimensions={1}, use_global_device_ids=true | all-gather | bytes 995328 | tf_op jit(solution)/shard_map/all_gather | solution.py:94
  140.7 29.7 %all-reduce.10.cloned.1.call-done = bf16[8,256,768]{2,1,0:T(8,128)(2,1)} async-done(((bf16[8,256,768]{2,1,0:T(8,128)(2,1)}), bf16[8,256,768]{2,1,0:T(8,128)(2,1)}) %all-reduce.10.cloned.1.call-update) | async-done | bytes 3145744 | tf_op jit(solution)/shard_map/psum | solution.py:32
  200.1 70.6 %all-to-all-done = bf16[3,8,256,192]{3,1,0,2:T(8,128)(2,1)} async-done(((bf16[3,8,256,192]{3,1,0,2:T(8,128)(2,1)}), bf16[3,8,256,192]{3,1,0,2:T(8,128)(2,1)}, u32[]{:S(2)}, u32[]{:S(2)}) %all-to-all-start) | async-done | bytes 2359328 | tf_op jit(solution)/shard_map/all_to_all | solution.py:140
  315.2 47.3 %all_gather.24 = bf16[192,768]{0,1:T(8,128)(2,1)} all-gather(bf16[192,96]{0,1:T(8,128)(2,1)S(1)} %copy.173), channel_id=1, replica_groups=mesh['tp'=4,'sp'=8] {'sp'}, dimensions={1}, use_global_device_ids=true | all-gather | bytes 331776 | tf_op jit(solution)/shard_map/all_gather | solution.py:95
  369.7 9.1 all-reduce.14.cloned.1.call-start
  378.8 57.0 %all-reduce.12.cloned.1.call-done = bf16[8,256,768]{2,1,0:T(8,128)(2,1)} async-done(((bf16[8,256,768]{2,1,0:T(8,128)(2,1)}), bf16[8,256,768]{2,1,0:T(8,128)(2,1)}) %all-reduce.12.cloned.1.call-update) | async-done | bytes 3145744 | tf_op jit(solution)/shard_map/psum | solution.py:32
  443.9 35.3 %all-gather.4.cloned.1.call-done = bf16[768,768]{1,0:T(8,128)(2,1)} async-done(((bf16[96,768]{1,0:T(8,128)(2,1)}), bf16[768,768]{1,0:T(8,128)(2,1)}) %all-gather.4.cloned.1.call-update) | async-done | bytes 1179664 | tf_op jit(solution)/shard_map/all_gather | solution.py:96
  479.2 8.7 fusion.65
  488.0 33.4 %all-gather.6.cloned.1.call-done = bf16[768,768]{0,1:T(8,128)(2,1)} async-done(((bf16[768,96]{0,1:T(8,128)(2,1)}), bf16[768,768]{0,1:T(8,128)(2,1)}) %all-gather.6.cloned.1.call-update) | async-done | bytes 1179664 | tf_op jit(solution)/shard_map/all_gather | solution.py:97
  521.4 8.9 fusion.33
  535.9 67.3 %all-reduce.14.cloned.1.call-done = bf16[8,256,768]{2,1,0:T(8,128)(2,1)} async-done(((bf16[8,256,768]{2,1,0:T(8,128)(2,1)}), bf16[8,256,768]{2,1,0:T(8,128)(2,1)}) %all-reduce.14.cloned.1.call-update) | async-done | bytes 3145744 | tf_op jit(solution)/shard_map/psum | solution.py:36
  623.2 31.4 %all_to_all.66 = bf16[8,256,192]{2,0,1:T(8,128)(2,1)S(1)} all-to-all(bf16[8,256,192]{2,0,1:T(8,128)(2,1)} %copy.177), channel_id=1, replica_groups=mesh['tp'=4,'sp'=8] {'sp'}, dimensions={1} | all-to-all | bytes 1572864 | tf_op jit(solution)/shard_map/all_to_all | solution.py:191
  695.4 74.1 %all_to_all.67 = bf16[3,64,32,192]{3,2,0,1:T(8,128)(2,1)S(1)} all-to-all(bf16[3,64,32,192]{3,2,0,1:T(8,128)(2,1)} %copy.192), channel_id=1, replica_groups=mesh['tp'=4,'sp'=8] {'sp'}, dimensions={1} | all-to-all | bytes 4718592 | tf_op jit(solution)/shard_map/all_to_all | solution.py:206
  781.1 61.3 %all-reduce.16.cloned.1.call-done = bf16[8,256,768]{2,1,0:T(8,128)(2,1)} async-done(((bf16[8,256,768]{2,1,0:T(8,128)(2,1)}), bf16[8,256,768]{2,1,0:T(8,128)(2,1)}) %all-reduce.16.cloned.1.call-update) | async-done | bytes 3145744 | tf_op jit(solution)/shard_map/psum | solution.py:36
  918.4 8.5 fusion.51
  937.3 36.3 %reduce-scatter.21.cloned.1.call-done = f32[96,192]{1,0:T(8,128)} async-done(((f32[768,192]{1,0:T(8,128)}), f32[96,192]{1,0:T(8,128)}) %reduce-scatter.21.cloned.1.call-update) | async-done | bytes 73744
  975.2 68.4 %reduce-scatter.23.cloned.1.call-done = f32[96,576]{1,0:T(8,128)} async-done(((f32[768,576]{1,0:T(8,128)}), f32[96,576]{1,0:T(8,128)}) %reduce-scatter.23.cloned.1.call-update) | async-done | bytes 221200
  1045.4 119.8 %all-reduce.18.cloned.1.call-done = (bf16[8,256,768]{2,1,0:T(8,128)(2,1)}, bf16[8,256,768]{2,1,0:T(8,128)(2,1)}) async-done(((bf16[8,256,768]{2,1,0:T(8,128)(2,1)}, bf16[8,256,768]{2,1,0:T(8,128)(2,1)}), (bf16[8,256,768]{2,1,0:T(8,128)(2,1)}, bf16[8,256,768]{2,1,0:T(8,128)(2,1)})) %all-reduce.18.cloned.1.call-update) | async-done | bytes 6291472 | tf_op jit(solution)/shard_map/psum | solution.py:32
  1178.9 39.0 %psum.63 = bf16[4,6912]{1,0:T(4,128)(2,1)S(1)} all-reduce(f32[4,6912]{1,0:T(4,128)S(1)} %fusion.89), channel_id=1, replica_groups=mesh['tp'=4,'sp'=8] {'sp'}, use_global_device_ids=true, to_apply=%region_34.35 | all-reduce | flops 27648 | bytes 165888 | tf_op jit(solution)/shard_map/psum | solution.py:245
  1218.4 26.2 %all-gather = f32[8,96,4]{1,2,0:T(4,128)S(1)} all-gather(f32[1,96,4]{1,2,0:T(4,128)S(1)} %convolution_bitcast_fusion.5), channel_id=1, replica_groups=mesh['tp'=4,'sp'=8] {'sp'}, dimensions={0}, use_global_device_ids=true | all-gather | bytes 13824 | tf_op jit(solution)/shard_map/all_gather | solution.py:248
  1256.1 52.9 %reduce-scatter.17.cloned.1.call-done = f32[768,96]{0,1:T(8,128)} async-done(((f32[768,768]{0,1:T(8,128)}), f32[768,96]{0,1:T(8,128)}) %reduce-scatter.17.cloned.1.call-update) | async-done | bytes 294928 | tf_op jit(solution)/shard_map/reduce_scatter | solution.py:259
  1309.0 72.4 %reduce-scatter.15.cloned.1.call-done = f32[96,768]{1,0:T(8,128)} async-done(((f32[768,768]{1,0:T(8,128)}), f32[96,768]{1,0:T(8,128)}) %reduce-scatter.15.cloned.1.call-update) | async-done | bytes 294928 | tf_op jit(solution)/shard_map/reduce_scatter | solution.py:258
  (301 shorter events, 309.5 us)
Async XLA Ops:
  7.2 81.1 %all-reduce.8.cloned.1.call-start = ((), (), s32[]{:S(2)}) async-start(), calls=%async_computation.10 | async-start | bytes 221184 | tf_op jit(solution)/shard_map/psum | solution.py:113
  9.8 160.6 %all-reduce.10.cloned.1.call-start = ((), (), s32[]{:S(2)}) async-start(), calls=%async_computation.11 | async-start | bytes 6291456 | tf_op jit(solution)/shard_map/psum | solution.py:32
  12.3 44.7 %copy-start.66 = (s32[64]{0:T(128)S(1)}, s32[64]{0:T(128)}, u32[]{:S(2)}) copy-start(s32[64]{0:T(128)} %param.13) | copy-start | bytes 772
  12.3 82.2 %copy-start.51 = (f32[8,256]{1,0:T(8,128)}, f32[8,256]{1,0:T(8,128)S(1)}, u32[]{:S(2)}) copy-start(f32[8,256]{1,0:T(8,128)S(1)} %div.46) | copy-start | bytes 24580
  15.3 79.2 %copy-start.53 = (f32[8,256]{1,0:T(8,128)}, f32[8,256]{1,0:T(8,128)S(1)}, u32[]{:S(2)}) copy-start(f32[8,256]{1,0:T(8,128)S(1)} %rsqrt.28) | copy-start | bytes 24580
  90.1 93.5 %copy-start.60 = (f32[8,768]{1,0:T(8,128)}, f32[8,768]{1,0:T(8,128)S(1)}, u32[]{:S(2)}) copy-start(f32[8,768]{1,0:T(8,128)S(1)} %get-tuple-element.81) | copy-start | bytes 73732
  194.5 76.2 %all-to-all-start = ((bf16[3,8,256,192]{3,1,0,2:T(8,128)(2,1)}), bf16[3,8,256,192]{3,1,0,2:T(8,128)(2,1)}, u32[]{:S(2)}, u32[]{:S(2)}) async-start(bf16[3,8,256,192]{3,1,0,2:T(8,128)(2,1)} %copy.162), calls=%async_computation | async-start | bytes 6291456 | tf_op jit(solution)/shard_map/all_to_all | solution.py:140
  310.0 52.5 %all-to-all-start.1 = ((bf16[64,32,192]{2,1,0:T(8,128)(2,1)}), bf16[64,32,192]{2,1,0:T(8,128)(2,1)}, u32[]{:S(2)}, u32[]{:S(2)}) async-start(bf16[64,32,192]{2,1,0:T(8,128)(2,1)} %copy.171), calls=%async_computation.1 | async-start | bytes 2097152 | tf_op jit(solution)/shard_map/all_to_all | solution.py:148
  314.2 121.5 %all-reduce.12.cloned.1.call-start = ((), (), s32[]{:S(2)}) async-start(), calls=%async_computation.12 | async-start | bytes 6291456 | tf_op jit(solution)/shard_map/psum | solution.py:32
  368.5 110.8 %all-gather.4.cloned.1.call-start = ((), (), s32[]{:S(2)}) async-start(), calls=%async_computation.13 | async-start | bytes 1327104 | tf_op jit(solution)/shard_map/all_gather | solution.py:96
  369.1 152.3 %all-gather.6.cloned.1.call-start = ((), (), s32[]{:S(2)}) async-start(), calls=%async_computation.14 | async-start | bytes 1327104 | tf_op jit(solution)/shard_map/all_gather | solution.py:97
  369.7 233.6 %all-reduce.14.cloned.1.call-start = ((), (), s32[]{:S(2)}) async-start(), calls=%async_computation.15 | async-start | bytes 6291456 | tf_op jit(solution)/shard_map/psum | solution.py:36
  479.2 42.1 %copy-start.45 = (f32[8,768]{1,0:T(8,128)S(1)}, f32[8,768]{1,0:T(8,128)}, u32[]{:S(2)}) copy-start(f32[8,768]{1,0:T(8,128)} %get-tuple-element.78) | copy-start | bytes 73732
  535.9 306.5 %all-reduce.16.cloned.1.call-start = ((), (), s32[]{:S(2)}) async-start(), calls=%async_computation.16 | async-start | bytes 6291456 | tf_op jit(solution)/shard_map/psum | solution.py:36
  775.5 66.9 %copy-start.50 = (f32[8,256]{1,0:T(8,128)S(1)}, f32[8,256]{1,0:T(8,128)}, u32[]{:S(2)}) copy-start(f32[8,256]{1,0:T(8,128)} %copy-done.49) | copy-start | bytes 24580
  775.5 160.1 %reduce-scatter.25.cloned.1.call-start = ((), (), s32[]{:S(2)}) async-start(), calls=%async_computation.22 | async-start | bytes 884736
  781.0 192.5 %reduce-scatter.21.cloned.1.call-start = ((), (), s32[]{:S(2)}) async-start(), calls=%async_computation.20 | async-start | bytes 884736
  859.8 183.7 %reduce-scatter.23.cloned.1.call-start = ((), (), s32[]{:S(2)}) async-start(), calls=%async_computation.21 | async-start | bytes 2211840
  876.3 288.9 %all-reduce.18.cloned.1.call-start = ((), (), s32[]{:S(2)}) async-start(), calls=%async_computation.23 | async-start | bytes 12582912 | tf_op jit(solution)/shard_map/psum | solution.py:32
  905.1 349.1 %reduce-scatter.19.cloned.1.call-start = ((), (), s32[]{:S(2)}) async-start(), calls=%async_computation.19 | async-start | bytes 2211840
  918.3 390.6 %reduce-scatter.17.cloned.1.call-start = ((), (), s32[]{:S(2)}) async-start(), calls=%async_computation.18 | async-start | bytes 2654208 | tf_op jit(solution)/shard_map/reduce_scatter | solution.py:259
  926.9 454.5 %reduce-scatter.15.cloned.1.call-start = ((), (), s32[]{:S(2)}) async-start(), calls=%async_computation.17 | async-start | bytes 2654208 | tf_op jit(solution)/shard_map/reduce_scatter | solution.py:258
  1172.5 72.1 %copy-start.55 = (f32[4,768]{1,0:T(4,128)S(1)}, f32[4,768]{1,0:T(4,128)}, u32[]{:S(2)}) copy-start(f32[4,768]{1,0:T(4,128)} %param.12) | copy-start | bytes 36868
  1172.5 72.7 %copy-start.63 = (bf16[4,96]{1,0:T(4,128)(2,1)S(1)}, bf16[4,96]{1,0:T(4,128)(2,1)}, u32[]{:S(2)}) copy-start(bf16[4,96]{1,0:T(4,128)(2,1)} %copy-done.62) | copy-start | bytes 2308
  (64 other events, 377.8 us)
Sparse Core Ops, SparseCore 0:
  12.0 73.8 all-reduce.7
  103.1 67.2 all-reduce.9
  368.6 67.1 all-reduce.11
  438.0 41.1 all-gather.3
  481.5 39.8 all-gather.5
  536.0 67.1 all-reduce.13
  775.6 66.7 all-reduce.15
  846.0 62.6 reduce-scatter.24
  912.1 61.4 reduce-scatter.20
  977.8 65.6 reduce-scatter.22
  1046.5 118.7 all-reduce.17
  1168.6 67.5 reduce-scatter.18
  1240.7 68.2 reduce-scatter.16
  1313.3 68.0 reduce-scatter.14
where the time goes:
time: 1400 us; the launch traced here: 1390 us
  waiting for transfers between devices  706 us (50%)
  blocking collectives  324 us (23%)
  matrix products  130 us (9%)
  local copies, waits for them, and re-layouts  113 us (8%)
  other arithmetic  80 us (6%)
  starting transfers between devices  20.5 us (1%)
  between operations  15.4 us (1%)
    psum x3, waiting for transfers between devices, heads_sum(): return lax.psum(term_value, 'tp').astype(jnp.float32)  207 us
    psum x2, waiting for transfers between devices, grads_sum(): return lax.psum(term_value.astype(jnp.bfloat16), 'tp').astype(jnp.float32)  129 us
    unnamed x18, waiting for transfers between devices  106 us
    all_to_all x1, blocking collectives, shards(): lax.all_to_all(stacked, 'sp', split_axis=1, concat_axis=2, tiled=True)  74.1 us
    reduce_scatter x1, waiting for transfers between devices, shards(): lax.psum_scatter(grad_up, 'sp', scatter_dimension=0, tiled=True)  72.4 us
    all_to_all x1, waiting for transfers between devices, shards(): lax.all_to_all(proj_two, 'sp', split_axis=2, concat_axis=1, tiled=True)  70.6 us
    reduce_scatter x1, waiting for transfers between devices, shards(): lax.psum_scatter(grad_down, 'sp', scatter_dimension=1, tiled=True)  52.9 us
    all_gather x1, blocking collectives, shards(): lax.all_gather(w_o_t, 'sp', axis=1, tiled=True)  47.3 us
  transfers between devices with their start and end apart: 16, of which 12 were waited for; matrix products, arithmetic and copies ran while one was open for 11% of the time, Pallas kernels for 0%

commit v1 on v0

v1 whole, which is shorter than its diff:
```python
import jax
import jax.numpy as jnp
from jax import lax
from jax.sharding import PartitionSpec as P

HD = 64
PATCHES = 256
BLOCK_ROWS = 256
EPSILON = 1e-06
HIGHEST = lax.Precision.HIGHEST
BF = jnp.bfloat16
F32 = jnp.float32


def bits_of(size):
    return size.bit_length() - 1


def swap(value, axis, bit):
    size = lax.axis_size(axis)
    return lax.ppermute(value, axis, [(i, i ^ (1 << bit)) for i in range(size)])


def my_bit(axis, bit):
    return (lax.axis_index(axis) >> bit) & 1


def cube_sum(value, dims):
    for axis, bit in dims:
        value = value + swap(value, axis, bit)
    return value


def cube_gather(block, dims):
    held = block[None]
    for axis, bit in dims:
        other = swap(held, axis, bit)
        high = my_bit(axis, bit) == 1
        held = jnp.concatenate([jnp.where(high, other, held), jnp.where(high, held, other)])
    return held


def cube_scatter(parts, dims):
    for axis, bit in reversed(dims):
        half = parts.shape[0] // 2
        mine = my_bit(axis, bit)
        send = lax.dynamic_slice_in_dim(parts, (1 - mine) * half, half)
        keep = lax.dynamic_slice_in_dim(parts, mine * half, half)
        got = swap(send, axis, bit)
        parts = keep.astype(F32) + got.astype(F32)
        if half > 1:
            parts = parts.astype(BF)
    return parts[0]


def cube_dims(order):
    return [("sp", bit) for bit in order[0]] + order[1]


def in_device_order(gathered, dims, back=False):
    count = len(dims)
    want = [("tp", b) for b in reversed(range(bits_of(lax.axis_size("tp"))))]
    want += [("sp", b) for b in reversed(range(bits_of(lax.axis_size("sp"))))]
    have = list(reversed(dims))
    tail = gathered.shape[1:]
    if back:
        have, want = want, have
    split = gathered.reshape((2,) * count + tail)
    order = [have.index(w) for w in want]
    split = split.transpose(order + [count + i for i in range(len(tail))])
    return split.reshape((2**count,) + tail)


def norm_rows(operand):
    centred = operand - jnp.mean(operand, axis=-1, keepdims=True)
    inverse = lax.rsqrt(jnp.mean(centred * centred, axis=-1, keepdims=True) + EPSILON)
    return (centred * inverse, inverse)


def norm_back(incoming, normed, inverse):
    first_mean = jnp.mean(incoming, axis=-1, keepdims=True)
    second_mean = jnp.mean(incoming * normed, axis=-1, keepdims=True)
    return inverse * (incoming - first_mean - normed * second_mean)


def gelu_tanh(operand):
    return jax.nn.gelu(operand, approximate=True)


def mm(form, left, right):
    return jnp.einsum(form, left, right, preferred_element_type=F32)


def attend(qkv, mask):
    heads = qkv.reshape(qkv.shape[0], qkv.shape[1], 3, -1, HD)
    q, k, v = heads[:, :, 0], heads[:, :, 1], heads[:, :, 2]
    scores = mm("aqhe,akhe->ahqk", q, k) * 0.125
    if mask is not None:
        scores = jnp.where(mask, scores, -1e30)
    lse = jax.nn.logsumexp(scores, axis=-1, keepdims=True)
    weights = jnp.exp(scores - lse).astype(BF)
    out = mm("ahqk,akhe->aqhe", weights, v).astype(BF)
    return out.reshape(qkv.shape[0], qkv.shape[1], -1), lse


def attend_back(qkv, lse, grad, mask):
    heads = qkv.reshape(qkv.shape[0], qkv.shape[1], 3, -1, HD)
    q, k, v = heads[:, :, 0], heads[:, :, 1], heads[:, :, 2]
    grad = grad.reshape(q.shape)
    scores = mm("aqhe,akhe->ahqk", q, k) * 0.125
    if mask is not None:
        scores = jnp.where(mask, scores, -1e30)
    prob = jnp.exp(scores - lse)
    grad_p = mm("aqhe,akhe->ahqk", grad, v)
    grad_v = mm("ahqk,aqhe->akhe", prob.astype(BF), grad)
    rows = jnp.sum(prob * grad_p, axis=-1, keepdims=True)
    grad_s = (prob * (grad_p - rows)).astype(BF)
    grad_q = mm("ahqk,akhe->aqhe", grad_s, k) * 0.125
    grad_k = mm("ahqk,aqhe->akhe", grad_s, q) * 0.125
    out = jnp.stack([grad_q, grad_k, grad_v], axis=2).astype(BF)
    return out.reshape(qkv.shape)


def shards(
    tokens, condition, clip_ids, w_mod, w_qkv_s, w_o_s, w_qkv_t, w_o_t, w_up, w_down, grad_out
):
    n_tp, n_sp = lax.axis_size("tp"), lax.axis_size("sp")
    devices = n_tp * n_sp
    my_tp, my_sp = lax.axis_index("tp"), lax.axis_index("sp")
    width = tokens.shape[1]
    sp_frames = tokens.shape[0] // PATCHES
    frames = sp_frames // n_tp
    all_frames = sp_frames * n_sp
    places = PATCHES // devices
    per_block = max(1, min(places, BLOCK_ROWS // all_frames))
    blocks = places // per_block
    rows = all_frames * per_block
    clips = condition.shape[0]
    unit_tp = w_up.shape[1]
    head_tp = w_o_s.shape[0]
    row_sp = w_up.shape[0]

    sp_bits = bits_of(n_sp)
    tp_bits = bits_of(n_tp)
    far_sp = [("sp", b) for b in reversed(range(1, sp_bits))]
    dims_s = far_sp + [("sp", 0), ("tp", 1), ("tp", 0)]
    dims_t = far_sp + [("tp", 1), ("sp", 0), ("tp", 0)]
    every = [("tp", b) for b in range(tp_bits)] + [("sp", b) for b in range(sp_bits)]

    def pack(w_qkv, w_o):
        flat = w_qkv.transpose(1, 0, 2).reshape(row_sp, -1)
        return jnp.concatenate([flat, w_o.T], axis=1)

    def unpack(gathered, dims):
        full = in_device_order(gathered, dims).reshape(n_tp, width, 4, head_tp)
        full = full.transpose(1, 2, 0, 3).reshape(width, 4 * width)
        return full[:, : 3 * width], full[:, 3 * width :]

    cond_act = jax.nn.silu(condition).astype(BF)
    cond_rows = lax.dynamic_slice_in_dim(cond_act, my_sp * row_sp, row_sp, axis=1)
    modulation = cube_sum(
        jnp.dot(cond_rows, w_mod, preferred_element_type=F32),
        [("sp", b) for b in range(sp_bits)],
    )
    qkv_s, out_s = unpack(cube_gather(pack(w_qkv_s, w_o_s), dims_s), dims_s)
    qkv_t, out_t = unpack(cube_gather(pack(w_qkv_t, w_o_t), dims_t), dims_t)
    feed = lax.all_gather(jnp.stack([w_up, w_down.T]), ("tp", "sp"), axis=0)
    feed = feed.reshape(n_tp, n_sp, 2, row_sp, unit_tp).transpose(2, 0, 1, 3, 4)
    feed = feed.reshape(2, n_tp, width, unit_tp)
    up, down = feed[0], feed[1]

    hot_all = clip_ids[:, None] == jnp.arange(clips, dtype=jnp.int32)[None, :]
    first = my_sp * sp_frames + my_tp * frames
    hot_frames = lax.dynamic_slice_in_dim(hot_all, first, frames).astype(F32)
    mod_frames = jnp.dot(hot_frames, modulation, precision=HIGHEST)[:, None, :]
    mod_s = [mod_frames[:, :, i * width : (i + 1) * width] for i in range(3)]
    row_ids = jnp.repeat(clip_ids, per_block)
    mod_rows = jnp.dot(
        jnp.repeat(hot_all, per_block, axis=0).astype(F32), modulation, precision=HIGHEST
    )[None]
    mod_t = [mod_rows[:, :, i * width : (i + 1) * width] for i in range(9)]
    key = row_ids * per_block + jnp.tile(jnp.arange(per_block, dtype=jnp.int32), all_frames)
    mask = key[:, None] == key[None, :]

    def to_places(value):
        split = value.reshape(frames, devices, blocks, per_block, width).transpose(1, 2, 0, 3, 4)
        got = lax.all_to_all(split, ("sp", "tp"), 0, 0, tiled=True)
        return got.transpose(1, 0, 2, 3, 4).reshape(blocks, rows, width)

    def to_frames(value):
        split = value.reshape(blocks, devices, frames, per_block, width).transpose(1, 0, 2, 3, 4)
        got = lax.all_to_all(split, ("sp", "tp"), 0, 0, tiled=True)
        return got.transpose(2, 0, 1, 3, 4).reshape(frames, PATCHES, width)

    def input_to_places(value):
        split = value.reshape(sp_frames, n_sp, n_tp, blocks, per_block, width)
        split = lax.dynamic_slice_in_dim(split, my_tp, 1, axis=2)[:, :, 0]
        got = lax.all_to_all(split.transpose(1, 2, 0, 3, 4), "sp", 0, 0, tiled=True)
        return got.transpose(1, 0, 2, 3, 4).reshape(blocks, rows, width)

    def places_to_output(value):
        split = value.reshape(blocks, n_sp, sp_frames, per_block, width).transpose(1, 0, 2, 3, 4)
        got = lax.all_to_all(split, "sp", 0, 0, tiled=True)
        got = lax.all_gather(got, "tp", axis=0)
        return got.transpose(3, 1, 0, 2, 4, 5).reshape(-1, width)

    grad_rows = input_to_places(grad_out).astype(F32)

    own = lax.dynamic_slice_in_dim(tokens, my_tp * frames * PATCHES, frames * PATCHES)
    res0 = own.astype(F32).reshape(frames, PATCHES, width)
    n1, r1 = norm_rows(res0)
    h1 = (n1 * (1.0 + mod_s[1]) + mod_s[0]).astype(BF)
    qkv1 = mm("frd,de->fre", h1, qkv_s).astype(BF)
    o1, lse1 = attend(qkv1, None)
    a1 = mm("fre,de->frd", o1, out_s)
    x1_frames = res0 + mod_s[2] * a1
    x1 = to_places(x1_frames.astype(BF)).astype(F32)

    n2, r2 = norm_rows(x1)
    h2 = (n2 * (1.0 + mod_t[4]) + mod_t[3]).astype(BF)
    qkv2 = mm("brd,de->bre", h2, qkv_t).astype(BF)
    o2, lse2 = attend(qkv2, mask)
    a2 = mm("bre,de->brd", o2, out_t)
    x2 = x1 + mod_t[5] * a2
    n3, r3 = norm_rows(x2)
    h3 = (n3 * (1.0 + mod_t[7]) + mod_t[6]).astype(BF)

    da3 = (mod_t[8] * grad_rows).astype(BF)
    u = mm("brd,tdh->tbrh", h3, up)
    g32, gelu_pull = jax.vjp(gelu_tanh, u)
    g = g32.astype(BF)
    a3 = mm("tbrh,tdh->brd", g, down)
    dg = mm("brd,tdh->tbrh", da3, down)
    du = gelu_pull(dg)[0].astype(BF)
    grad_down = mm("brd,tbrh->tdh", da3, g).astype(BF)
    grad_up = mm("brd,tbrh->tdh", h3, du).astype(BF)
    dh3 = mm("tbrh,tdh->brd", du, up)
    block_out = places_to_output((x2 + mod_t[8] * a3).astype(BF))
    feed_grad = jnp.stack([grad_up, grad_down], axis=2).reshape(
        n_tp, n_sp, row_sp, 2, unit_tp
    )
    feed_grad = lax.psum_scatter(
        feed_grad.reshape(devices, row_sp, 2, unit_tp), ("tp", "sp"), scatter_dimension=0
    ).astype(F32)

    hot_rows = jnp.repeat(hot_all, per_block, axis=0).astype(BF)

    def clip_sum(value):
        return mm("rc,brd->cd", hot_rows, value.astype(BF))

    dm = [None] * 9
    dm[8] = clip_sum(grad_rows * a3)
    dm[6] = clip_sum(dh3)
    dm[7] = clip_sum(dh3 * n3)
    dx2 = grad_rows + norm_back(dh3 * (1.0 + mod_t[7]), n3, r3)

    dm[5] = clip_sum(dx2 * a2)
    da2 = (mod_t[5] * dx2).astype(BF)
    grad_ot = mm("brd,bre->de", da2, o2)
    do2 = mm("brd,de->bre", da2, out_t).astype(BF)
    dqkv2 = attend_back(qkv2, lse2, do2, mask)
    grad_qt = mm("brd,bre->de", h2, dqkv2)
    dh2 = mm("bre,de->brd", dqkv2, qkv_t)
    dm[3] = clip_sum(dh2)
    dm[4] = clip_sum(dh2 * n2)
    dx1 = dx2 + norm_back(dh2 * (1.0 + mod_t[4]), n2, r2)

    def scatter_grads(grad_q, grad_o, dims):
        both = jnp.concatenate([grad_q.astype(BF), grad_o.astype(BF)], axis=1)
        both = both.reshape(n_sp, row_sp, 4, n_tp, head_tp).transpose(3, 0, 1, 2, 4)
        both = both.reshape(devices, row_sp, 4 * head_tp)
        mine = cube_scatter(in_device_order(both, dims, back=True), dims)
        mine = mine.reshape(row_sp, 4, head_tp)
        return mine[:, :3].transpose(1, 0, 2), mine[:, 3].T

    sum_qt, sum_ot = scatter_grads(grad_qt, grad_ot, dims_t)
    dx1_frames = to_frames(dx1.astype(BF)).astype(F32)

    frame_sum = [None] * 3
    frame_sum[2] = jnp.sum(dx1_frames * a1, axis=1)
    da1 = (mod_s[2] * dx1_frames).astype(BF)
    grad_os = mm("frd,fre->de", da1, o1)
    do1 = mm("frd,de->fre", da1, out_s).astype(BF)
    dqkv1 = attend_back(qkv1, lse1, do1, None)
    grad_qs = mm("frd,fre->de", h1, dqkv1)
    dh1 = mm("fre,de->frd", dqkv1, qkv_s)
    frame_sum[0] = jnp.sum(dh1, axis=1)
    frame_sum[1] = jnp.sum(dh1 * n1, axis=1)
    dx0 = dx1_frames + norm_back(dh1 * (1.0 + mod_s[1]), n1, r1)
    sum_qs, sum_os = scatter_grads(grad_qs, grad_os, dims_s)
    grad_tokens = lax.all_gather(
        dx0.reshape(-1, width).astype(BF), "tp", axis=0, tiled=True
    )

    dm_s = jnp.dot(hot_frames.T, jnp.concatenate(frame_sum, axis=-1), precision=HIGHEST)
    dm_t = cube_sum(jnp.concatenate(dm[3:], axis=-1), every)
    dm_s = cube_sum(dm_s, every)
    dm_low = jnp.concatenate([dm_s, dm_t], axis=-1).astype(BF)
    grad_mod = jnp.dot(cond_rows.T, dm_low, preferred_element_type=F32)
    grad_act = jnp.dot(dm_low, w_mod.T, preferred_element_type=F32)
    sp_dims = [("sp", b) for b in range(sp_bits)]
    grad_act = cube_gather(grad_act, sp_dims).transpose(1, 0, 2).reshape(clips, width)
    unused, silu_pull = jax.vjp(jax.nn.silu, condition)
    grad_condition = silu_pull(grad_act)[0]
    return (
        block_out,
        grad_tokens,
        grad_condition,
        grad_mod,
        sum_qs,
        sum_os,
        sum_qt,
        sum_ot,
        feed_grad[:, 0],
        feed_grad[:, 1].T,
    )


def solution(mesh):
    placed = (
        P("sp", None),
        P(),
        P(),
        P("sp", None),
        P(None, "sp", "tp"),
        P("tp", "sp"),
        P(None, "sp", "tp"),
        P("tp", "sp"),
        P("sp", "tp"),
        P("tp", "sp"),
        P("sp", None),
    )
    return jax.shard_map(
        shards,
        mesh=mesh,
        in_specs=placed,
        out_specs=(
            P("sp", None),
            P("sp", None),
            P(),
            P("sp", None),
            P(None, "sp", "tp"),
            P("tp", "sp"),
            P(None, "sp", "tp"),
            P("tp", "sp"),
            P("sp", "tp"),
            P("tp", "sp"),
        ),
        check_vma=False,
    )
```

time: 1400 us -> 747 us (0.53)
  waiting for transfers between devices: 706 us -> 162 us
  blocking collectives: 324 us -> 0 us
  local copies, waits for them, and re-layouts: 113 us -> 272 us
  starting transfers between devices: 20.5 us -> 71.2 us
  other arithmetic: 80 us -> 95.7 us
    psum x6 -> x0, waiting for transfers between devices: 335 us -> none  [the longest x3 207 us: heads_sum(): return lax.psum(term_value, 'tp').astype(jnp.float32)]
    all_gather x5 -> x0, blocking collectives: 179 us -> none  [the longest x1 47.3 us: shards(): lax.all_gather(w_o_t, 'sp', axis=1, tiled=True)]
    ppermute x0 -> x36, waiting for transfers between devices: none -> 132 us  [swap(): return lax.ppermute(value, axis, [(i, i ^ 1 << bit) for i in range(size)])]
    reduce_scatter x2 -> x1, waiting for transfers between devices: 125 us -> 0.01 us  [shards(): lax.psum_scatter(feed_grad.reshape(devices, row_sp, 2, unit_tp), ('tp', '...]
    unnamed x18 -> x4, waiting for transfers between devices: 106 us -> 0.07 us
    all_to_all x2 -> x0, blocking collectives: 105 us -> none  [the longest x1 74.1 us: shards(): lax.all_to_all(stacked, 'sp', split_axis=1, concat_axis=2, tiled=True)]
    all_gather x2 -> x3, waiting for transfers between devices: 68.7 us -> 0.01 us  [the longest x1 0.01 us: shards(): feed = lax.all_gather(jnp.stack([w_up, w_down.T]), ('tp', 'sp'), axis=0)]
    reshape x3 -> x15, local copies, waits for them, and re-layouts: 12.9 us -> 80.6 us  [the longest x4 44.5 us: scatter_grads(): both = both.reshape(n_sp, row_sp, 4, n_tp, head_tp).transpose(3, 0, 1, 2, 4)]
  transfers between devices with their start and end apart: 16 -> 44, of which waited for: 12 -> 24; matrix products, arithmetic and copies ran while one was open for 11% -> 55% of each run, Pallas kernels for 0% -> 0%
where the time goes in v1:
time: 747 us; the launch traced here: 738 us
  local copies, waits for them, and re-layouts  272 us (36%)
  waiting for transfers between devices  162 us (22%)
  matrix products  122 us (16%)
  other arithmetic  95.7 us (13%)
  starting transfers between devices  71.2 us (10%)
  between operations  15.8 us (2%)
    ppermute x36, waiting for transfers between devices, swap(): return lax.ppermute(value, axis, [(i, i ^ 1 << bit) for i in range(size)])  132 us
    dot_general x36, matrix products, mm(): return jnp.einsum(form, left, right, preferred_element_type=F32)  113 us
    reshape x4, local copies, waits for them, and re-layouts, scatter_grads(): both = both.reshape(n_sp, row_sp, 4, n_tp, head_tp).transpose(3, 0, 1, 2, 4)  44.5 us
    ppermute x36, starting transfers between devices, swap(): return lax.ppermute(value, axis, [(i, i ^ 1 << bit) for i in range(size)])  43.6 us
    unnamed x227, local copies, waits for them, and re-layouts  27.3 us
    another operation x2, local copies, waits for them, and re-layouts, unpack(): full = in_device_order(gathered, dims).reshape(n_tp, width, 4, head_tp)  26.3 us
    another operation x2, local copies, waits for them, and re-layouts, in_device_order(): split = gathered.reshape((2,) * count + tail)  23.8 us
    transpose x2, local copies, waits for them, and re-layouts, unpack(): full = full.transpose(1, 2, 0, 3).reshape(width, 4 * width)  20.7 us
  transfers between devices with their start and end apart: 44, of which 24 were waited for; matrix products, arithmetic and copies ran while one was open for 55% of the time, Pallas kernels for 0%

profile of v1, /device:TPU:0, one launch (start us, length us, event | category | flops | bytes accessed | tf_op | source)
XLA Modules:
  0.0 737.8 jit_solution(9956251952700723522)
XLA Ops:
  17.1 16.3 %collective-permute-done.3 = bf16[1,96,768]{1,2,0:T(8,128)(2,1)S(1)} collective-permute-done((bf16[1,96,768]{1,2,0:T(8,128)(2,1)S(1)}, bf16[1,96,768]{1,2,0:T(8,128)(2,1)S(1)}, u32[]{:S(2)}, u32[]{:S(2)}) %collective-permute-start.3) | collective-permute-done | bytes 147488 | tf_op jit(solution)/shard_map/ppermute | solution.py:21
  40.9 15.6 %collective-permute-done.4 = bf16[2,96,768]{1,2,0:T(8,128)(2,1)} collective-permute-done((bf16[2,96,768]{1,2,0:T(8,128)(2,1)S(1)}, bf16[2,96,768]{1,2,0:T(8,128)(2,1)}, u32[]{:S(2)}, u32[]{:S(2)}) %collective-permute-start.4) | collective-permute-done | bytes 294944 | tf_op jit(solution)/shard_map/ppermute | solution.py:21
  70.5 13.2 %all-to-all-start.2 = ((bf16[8,2,8,4,768]{4,3,2,1,0:T(4,128)(2,1)}), bf16[8,2,8,4,768]{4,3,2,1,0:T(4,128)(2,1)}, u32[]{:S(2)}, u32[]{:S(2)}) async-start(bf16[8,2,8,4,768]{4,3,2,1,0:T(4,128)(2,1)} %copy_bitcast_fusion.2), calls=%async_computation.2 | async-start | bytes 1572864 | tf_op jit(solution)/shard_map/all_to_all | solution.py:198
  94.2 25.2 %collective-permute-done.9 = bf16[2,96,768]{1,2,0:T(8,128)(2,1)S(1)} collective-permute-done((bf16[2,96,768]{1,2,0:T(8,128)(2,1)S(1)}, bf16[2,96,768]{1,2,0:T(8,128)(2,1)S(1)}, u32[]{:S(2)}, u32[]{:S(2)}) %collective-permute-start.9) | collective-permute-done | bytes 294944 | tf_op jit(solution)/shard_map/ppermute | solution.py:21
  198.5 8.1 %copy.477 = bf16[2,2,2,2,2,96,768]{6,5,2,3,4,0,1:T(8,128)(2,1)} copy(bf16[2,2,2,2,2,96,768]{5,6,4,3,2,1,0:T(8,128)(2,1)} %bitcast.416) | data formatting | bytes 9437184 | tf_op jit(solution)/shard_map/reshape | solution.py:68
  206.6 13.4 %reshape_reshape.13 = bf16[4,768,4,192]{3,2,1,0:T(4,128)(2,1)} reshape(bf16[2,2,2,2,2,96,768]{6,5,4,3,2,1,0:T(8,128)(2,1)} %bitcast.435) | data formatting | bytes 9437184 | tf_op jit(solution)/shard_map/reshape;reshape | solution.py:155
  220.0 10.4 %copy.478 = bf16[768,4,4,192]{0,3,2,1:T(8,128)(2,1)} copy(bf16[768,4,4,192]{3,1,0,2:T(4,128)(2,1)} %bitcast.420) | data formatting | bytes 9437184 | tf_op jit(solution)/shard_map/transpose | solution.py:156
  285.2 8.0 %copy.504 = bf16[2,2,2,2,2,96,768]{6,5,1,3,4,0,2:T(8,128)(2,1)} copy(bf16[2,2,2,2,2,96,768]{5,6,4,3,2,1,0:T(8,128)(2,1)} %bitcast.417) | data formatting | bytes 9437184 | tf_op jit(solution)/shard_map/reshape | solution.py:68
  293.2 12.9 %reshape_reshape.14 = bf16[4,768,4,192]{3,2,1,0:T(4,128)(2,1)} reshape(bf16[2,2,2,2,2,96,768]{6,5,4,3,2,1,0:T(8,128)(2,1)} %bitcast.436) | data formatting | bytes 9437184 | tf_op jit(solution)/shard_map/reshape;reshape | solution.py:155
  306.1 10.3 %copy.505 = bf16[768,4,4,192]{0,3,2,1:T(8,128)(2,1)} copy(bf16[768,4,4,192]{3,1,0,2:T(4,128)(2,1)} %bitcast.421) | data formatting | bytes 9437184 | tf_op jit(solution)/shard_map/transpose | solution.py:156
  344.9 6.9 fusion.80
  370.1 8.9 %convert_reduce_fusion = (bf16[256,768]{1,0:T(8,128)(2,1)}, bf16[2,256,768]{2,1,0:T(8,128)(2,1)}, bf16[256,768]{1,0:T(8,128)(2,1)}, f32[2,256,768]{2,1,0:T(8,128)S(1)}) fusion(f32[2,256,768]{2,1,0:T(8,128)S(1)} %copy-done.51, f32[2,256,768]{2,1,0:T(8,128)S(1)} %get-tuple-element.45, f32[256,768]{1,0:T(8,128)S(1)} %copy-done.57, ...), kind=kOutput, calls=%fused_computation.86 | convolution fusion | flops 2437152768 | bytes 22028288 | tf_op jit(solution)/shard_map/tbrh,tdh->brd/dot_general | solution.py:91
  421.1 11.0 %all-to-all-done.1 = bf16[8,2,8,4,768]{4,3,2,1,0:T(4,128)(2,1)} async-done(((bf16[8,2,8,4,768]{4,3,2,1,0:T(4,128)(2,1)}), bf16[8,2,8,4,768]{4,3,2,1,0:T(4,128)(2,1)}, u32[]{:S(2)}, u32[]{:S(2)}) %all-to-all-start.1) | async-done | bytes 786464 | tf_op jit(solution)/shard_map/all_to_all | solution.py:203
  437.9 18.3 %all-to-all-done.3 = bf16[32,2,2,4,768]{4,3,1,2,0:T(4,128)(2,1)S(1)} async-done(((bf16[32,2,2,4,768]{4,3,1,2,0:T(4,128)(2,1)}), bf16[32,2,2,4,768]{4,3,1,2,0:T(4,128)(2,1)S(1)}, u32[]{:S(2)}, u32[]{:S(2)}) %all-to-all-start.3) | async-done | bytes 786464 | tf_op jit(solution)/shard_map/all_to_all | solution.py:192
  484.5 7.0 bitcast_convert_fusion.1
  491.5 8.0 %bitcast_convert_fusion = bf16[4,768,768]{1,2,0:T(8,128)(2,1)} fusion(f32[2,256,768]{2,1,0:T(8,128)S(1)} %copy-done.52, f32[256,768]{1,0:T(8,128)S(1)} %copy-done.58, f32[4,768,2,256]{3,1,2,0:T(8,128)} %copy-done.97), kind=kOutput, calls=%fused_computation.2 | convolution fusion | flops 2433220608 | bytes 13369344 | tf_op jit(solution)/shard_map/brd,tbrh->tdh/dot_general | solution.py:91
  499.6 8.4 %pad_maximum_fusion = bf16[32,96,2,768]{3,1,2,0:T(8,128)(2,1)} fusion(bf16[32,96,1,768]{3,1,2,0:T(8,128)(2,1)} %bitcast.468, bf16[32,96,1,768]{3,1,2,0:T(8,128)(2,1)} %bitcast.467), kind=kLoop, calls=%fused_computation.1 | loop fusion | flops 4718592 | bytes 18874368 | tf_op jit(solution)/shard_map/stack | solution.py:239
  533.1 13.3 %reshape.336 = bf16[8,96,4,4,192]{4,3,2,1,0:T(4,128)(2,1)} reshape(bf16[768,3072]{1,0:T(8,128)(2,1)} %pad_maximum_fusion.4) | data formatting | bytes 9437184 | tf_op jit(solution)/shard_map/reshape | solution.py:270
  546.4 9.1 %copy.644 = bf16[8,96,4,4,192]{4,2,1,0,3:T(4,128)(2,1)} copy(bf16[8,96,4,4,192]{4,3,2,1,0:T(4,128)(2,1)} %reshape.336) | data formatting | bytes 9437184 | tf_op jit(solution)/shard_map/reshape | solution.py:270
  555.5 11.9 %reshape_reshape.16 = bf16[2,2,2,2,2,96,768]{6,5,4,3,2,1,0:T(8,128)(2,1)} reshape(bf16[4,8,96,4,192]{4,3,2,1,0:T(4,128)(2,1)} %bitcast.418) | data formatting | bytes 9437184 | tf_op jit(solution)/shard_map/reshape;reshape | solution.py:68
  591.6 13.2 %reshape.334 = bf16[8,96,4,4,192]{4,3,2,1,0:T(4,128)(2,1)} reshape(bf16[768,3072]{1,0:T(8,128)(2,1)} %pad_maximum_fusion.3) | data formatting | bytes 9437184 | tf_op jit(solution)/shard_map/reshape | solution.py:270
  604.8 8.8 %copy.645 = bf16[8,96,4,4,192]{4,2,1,0,3:T(4,128)(2,1)} copy(bf16[8,96,4,4,192]{4,3,2,1,0:T(4,128)(2,1)} %reshape.334) | data formatting | bytes 9437184 | tf_op jit(solution)/shard_map/reshape | solution.py:270
  613.7 11.9 %reshape_reshape.15 = bf16[2,2,2,2,2,96,768]{6,5,4,3,2,1,0:T(8,128)(2,1)} reshape(bf16[4,8,96,4,192]{4,3,2,1,0:T(4,128)(2,1)} %bitcast.419) | data formatting | bytes 9437184 | tf_op jit(solution)/shard_map/reshape;reshape | solution.py:68
  660.5 13.2 %collective-permute-done.32 = bf16[8,96,768]{2,1,0:T(8,128)(2,1)} collective-permute-done((bf16[8,96,768]{2,1,0:T(8,128)(2,1)S(1)}, bf16[8,96,768]{2,1,0:T(8,128)(2,1)}, u32[]{:S(2)}, u32[]{:S(2)}) %collective-permute-start.32) | collective-permute-done | bytes 1179680 | tf_op jit(solution)/shard_map/ppermute | solution.py:21
  (528 shorter events, 438.5 us)
Async XLA Ops:
  7.2 337.7 %all-gather.8.cloned.1.call-start = ((), (), s32[]{:S(2)}) async-start(), calls=%async_computation.7 | async-start | bytes 9732096 | tf_op jit(solution)/shard_map/all_gather | solution.py:167
  11.0 22.4 %collective-permute-start.3 = (bf16[1,96,768]{1,2,0:T(8,128)(2,1)S(1)}, bf16[1,96,768]{1,2,0:T(8,128)(2,1)S(1)}, u32[]{:S(2)}, u32[]{:S(2)}) collective-permute-start(bf16[1,96,768]{1,2,0:T(8,128)(2,1)S(1)} %maximum_bitcast_fusion), channel_id=1, source_target_pairs={{0,4},{1,5},{2,6},{3,7},{4,0},{5,1},{6,2},{7,3},{8,12},{9,13},{10,... | collective-permute-start | bytes 442376 | tf_op jit(solution)/shard_map/ppermute | solution.py:21
  17.0 21.9 %collective-permute-start.8 = (bf16[1,96,768]{1,2,0:T(8,128)(2,1)S(1)}, bf16[1,96,768]{1,2,0:T(8,128)(2,1)S(1)}, u32[]{:S(2)}, u32[]{:S(2)}) collective-permute-start(bf16[1,96,768]{1,2,0:T(8,128)(2,1)S(1)} %maximum_bitcast_fusion.1), channel_id=1, source_target_pairs={{0,4},{1,5},{2,6},{3,7},{4,0},{5,1},{6,2},{7,3},{8,12},{9,13},{10,... | collective-permute-start | bytes 442376 | tf_op jit(solution)/shard_map/ppermute | solution.py:21
  58.9 24.9 %collective-permute-start.5 = (bf16[4,96,768]{2,1,0:T(8,128)(2,1)}, bf16[4,96,768]{2,1,0:T(8,128)(2,1)}, u32[]{:S(2)}, u32[]{:S(2)}) collective-permute-start(bf16[4,96,768]{2,1,0:T(8,128)(2,1)} %copy.468), channel_id=1, source_target_pairs={{0,1},{1,0},{2,3},{3,2},{4,5},{5,4},{6,7},{7,6},{8,9},{9,8},{10,11... | collective-permute-start | bytes 1769480 | tf_op jit(solution)/shard_map/ppermute | solution.py:21
  61.6 87.2 %collective-permute-start = (f32[4,6912]{1,0:T(4,128)}, f32[4,6912]{1,0:T(4,128)}, u32[]{:S(2)}, u32[]{:S(2)}) collective-permute-start(f32[4,6912]{1,0:T(4,128)} %fusion.81), channel_id=1, source_target_pairs={{0,1},{1,0},{2,3},{3,2},{4,5},{5,4},{6,7},{7,6},{8,9},{9,8},{10,11... | collective-permute-start | bytes 331784 | tf_op jit(solution)/shard_map/ppermute | solution.py:21
  70.5 182.6 %all-to-all-start.2 = ((bf16[8,2,8,4,768]{4,3,2,1,0:T(4,128)(2,1)}), bf16[8,2,8,4,768]{4,3,2,1,0:T(4,128)(2,1)}, u32[]{:S(2)}, u32[]{:S(2)}) async-start(bf16[8,2,8,4,768]{4,3,2,1,0:T(4,128)(2,1)} %copy_bitcast_fusion.2), calls=%async_computation.2 | async-start | bytes 1572864 | tf_op jit(solution)/shard_map/all_to_all | solution.py:198
  88.3 35.6 %collective-permute-start.6 = (bf16[8,96,768]{2,1,0:T(8,128)(2,1)}, bf16[8,96,768]{2,1,0:T(8,128)(2,1)}, u32[]{:S(2)}, u32[]{:S(2)}) collective-permute-start(bf16[8,96,768]{2,1,0:T(8,128)(2,1)} %copy.471), channel_id=1, source_target_pairs={{0,16},{8,24},{16,0},{24,8},{1,17},{9,25},{17,1},{25,9},{2,18},{10... | collective-permute-start | bytes 3538952 | tf_op jit(solution)/shard_map/ppermute | solution.py:21
  89.9 29.4 %collective-permute-start.9 = (bf16[2,96,768]{1,2,0:T(8,128)(2,1)S(1)}, bf16[2,96,768]{1,2,0:T(8,128)(2,1)S(1)}, u32[]{:S(2)}, u32[]{:S(2)}) collective-permute-start(bf16[2,96,768]{1,2,0:T(8,128)(2,1)S(1)} %pad_maximum_fusion.12), channel_id=1, source_target_pairs={{0,2},{1,3},{2,0},{3,1},{4,6},{5,7},{6,4},{7,5},{8,10},{9,11},{10,... | collective-permute-start | bytes 884744 | tf_op jit(solution)/shard_map/ppermute | solution.py:21
  136.6 50.8 %collective-permute-start.7 = (bf16[16,96,768]{2,1,0:T(8,128)(2,1)}, bf16[16,96,768]{2,1,0:T(8,128)(2,1)}, u32[]{:S(2)}, u32[]{:S(2)}) collective-permute-start(bf16[16,96,768]{2,1,0:T(8,128)(2,1)} %copy.474), channel_id=1, source_target_pairs={{0,8},{8,0},{16,24},{24,16},{1,9},{9,1},{17,25},{25,17},{2,10},{10... | collective-permute-start | bytes 7077896 | tf_op jit(solution)/shard_map/ppermute | solution.py:21
  145.8 28.5 %collective-permute-start.11 = (bf16[8,96,768]{2,1,0:T(8,128)(2,1)}, bf16[8,96,768]{2,1,0:T(8,128)(2,1)}, u32[]{:S(2)}, u32[]{:S(2)}) collective-permute-start(bf16[8,96,768]{2,1,0:T(8,128)(2,1)} %copy.498), channel_id=1, source_target_pairs={{0,1},{1,0},{2,3},{3,2},{4,5},{5,4},{6,7},{7,6},{8,9},{9,8},{10,11... | collective-permute-start | bytes 3538952 | tf_op jit(solution)/shard_map/ppermute | solution.py:21
  187.5 86.1 %collective-permute-start.12 = (bf16[16,96,768]{2,1,0:T(8,128)(2,1)}, bf16[16,96,768]{2,1,0:T(8,128)(2,1)}, u32[]{:S(2)}, u32[]{:S(2)}) collective-permute-start(bf16[16,96,768]{2,1,0:T(8,128)(2,1)} %copy.501), channel_id=1, source_target_pairs={{0,8},{8,0},{16,24},{24,16},{1,9},{9,1},{17,25},{25,17},{2,10},{10... | collective-permute-start | bytes 7077896 | tf_op jit(solution)/shard_map/ppermute | solution.py:21
  253.1 63.3 %all-to-all-start = ((bf16[32,2,2,4,768]{4,1,3,2,0:T(2,128)(2,1)}), bf16[32,2,2,4,768]{4,1,3,2,0:T(2,128)(2,1)S(1)}, u32[]{:S(2)}, u32[]{:S(2)}) async-start(bf16[32,2,2,4,768]{4,1,3,2,0:T(2,128)(2,1)} %bitcast.407), calls=%async_computation | async-start | bytes 1572864 | tf_op jit(solution)/shard_map/all_to_all | solution.py:187
  405.3 26.7 %all-to-all-start.1 = ((bf16[8,2,8,4,768]{4,3,2,1,0:T(4,128)(2,1)}), bf16[8,2,8,4,768]{4,3,2,1,0:T(4,128)(2,1)}, u32[]{:S(2)}, u32[]{:S(2)}) async-start(bf16[8,2,8,4,768]{4,3,2,1,0:T(4,128)(2,1)} %bitcast.472), calls=%async_computation.1 | async-start | bytes 1572864 | tf_op jit(solution)/shard_map/all_to_all | solution.py:203
  432.0 24.2 %all-to-all-start.3 = ((bf16[32,2,2,4,768]{4,3,1,2,0:T(4,128)(2,1)}), bf16[32,2,2,4,768]{4,3,1,2,0:T(4,128)(2,1)S(1)}, u32[]{:S(2)}, u32[]{:S(2)}) async-start(bf16[32,2,2,4,768]{4,3,1,2,0:T(4,128)(2,1)} %bitcast.405), calls=%async_computation.3 | async-start | bytes 1572864 | tf_op jit(solution)/shard_map/all_to_all | solution.py:192
  435.6 276.6 %all-gather.10.cloned.1.call-start = ((), (), s32[]{:S(2)}) async-start(), calls=%async_computation.8 | async-start | bytes 3932160 | tf_op jit(solution)/shard_map/all_gather | solution.py:204
  437.9 287.6 %all-gather.6.cloned.1.call-start = ((), (), s32[]{:S(2)}) async-start(), calls=%async_computation.5 | async-start | bytes 3932160 | tf_op jit(solution)/shard_map/all_gather | solution.py:291
  484.1 241.4 %reduce-scatter.2.cloned.1.call-start = ((), (), s32[]{:S(2)}) async-start(), calls=%async_computation.6 | async-start | bytes 9732096 | tf_op jit(solution)/shard_map/reduce_scatter | solution.py:242
  528.6 41.8 %collective-permute-start.20 = (f32[4,4608]{1,0:T(4,128)S(1)}, f32[4,4608]{1,0:T(4,128)S(1)}, u32[]{:S(2)}, u32[]{:S(2)}) collective-permute-start(f32[4,4608]{1,0:T(4,128)S(1)} %add.320), channel_id=1, source_target_pairs={{0,1},{1,0},{2,3},{3,2},{4,5},{5,4},{6,7},{7,6},{8,9},{9,8},{10,11... | collective-permute-start | bytes 221192 | tf_op jit(solution)/shard_map/ppermute | solution.py:21
  573.4 71.8 %collective-permute-start.31 = (bf16[16,96,768]{2,1,0:T(8,128)(2,1)}, bf16[16,96,768]{2,1,0:T(8,128)(2,1)}, u32[]{:S(2)}, u32[]{:S(2)}) collective-permute-start(bf16[16,96,768]{2,1,0:T(8,128)(2,1)} %constant_dynamic-slice_fusion.5), channel_id=1, source_target_pairs={{0,8},{8,0},{16,24},{24,16},{1,9},{9,1},{17,25},{25,17},{2,10},{10... | collective-permute-start | bytes 7077896 | tf_op jit(solution)/shard_map/ppermute | solution.py:21
  579.8 55.9 %collective-permute-start.22 = (f32[4,4608]{1,0:T(4,128)S(1)}, f32[4,4608]{1,0:T(4,128)S(1)}, u32[]{:S(2)}, u32[]{:S(2)}) collective-permute-start(f32[4,4608]{1,0:T(4,128)S(1)} %add.322), channel_id=1, source_target_pairs={{0,4},{1,5},{2,6},{3,7},{4,0},{5,1},{6,2},{7,3},{8,12},{9,13},{10,... | collective-permute-start | bytes 221192 | tf_op jit(solution)/shard_map/ppermute | solution.py:21
  588.7 39.7 %collective-permute-start.15 = (f32[4,2304]{1,0:T(4,128)S(1)}, f32[4,2304]{1,0:T(4,128)S(1)}, u32[]{:S(2)}, u32[]{:S(2)}) collective-permute-start(f32[4,2304]{1,0:T(4,128)S(1)} %add.315), channel_id=1, source_target_pairs={{0,1},{1,0},{2,3},{3,2},{4,5},{5,4},{6,7},{7,6},{8,9},{9,8},{10,11... | collective-permute-start | bytes 110600 | tf_op jit(solution)/shard_map/ppermute | solution.py:21
  632.6 18.1 %collective-permute-start.26 = (bf16[16,96,768]{2,1,0:T(8,128)(2,1)}, bf16[16,96,768]{2,1,0:T(8,128)(2,1)}, u32[]{:S(2)}, u32[]{:S(2)}) collective-permute-start(bf16[16,96,768]{2,1,0:T(8,128)(2,1)} %constant_dynamic-slice_fusion.10), channel_id=1, source_target_pairs={{0,8},{8,0},{16,24},{24,16},{1,9},{9,1},{17,25},{25,17},{2,10},{10... | collective-permute-start | bytes 7077896 | tf_op jit(solution)/shard_map/ppermute | solution.py:21
  648.6 25.1 %collective-permute-start.32 = (bf16[8,96,768]{2,1,0:T(8,128)(2,1)S(1)}, bf16[8,96,768]{2,1,0:T(8,128)(2,1)}, u32[]{:S(2)}, u32[]{:S(2)}) collective-permute-start(bf16[8,96,768]{2,1,0:T(8,128)(2,1)S(1)} %constant_dynamic-slice_fusion.4), channel_id=1, source_target_pairs={{0,1},{1,0},{2,3},{3,2},{4,5},{5,4},{6,7},{7,6},{8,9},{9,8},{10,11... | collective-permute-start | bytes 3538952 | tf_op jit(solution)/shard_map/ppermute | solution.py:21
  654.3 28.0 %collective-permute-start.27 = (bf16[8,96,768]{2,1,0:T(8,128)(2,1)}, bf16[8,96,768]{2,1,0:T(8,128)(2,1)}, u32[]{:S(2)}, u32[]{:S(2)}) collective-permute-start(bf16[8,96,768]{2,1,0:T(8,128)(2,1)} %constant_dynamic-slice_fusion.9), channel_id=1, source_target_pairs={{0,16},{8,24},{16,0},{24,8},{1,17},{9,25},{17,1},{25,9},{2,18},{10... | collective-permute-start | bytes 3538952 | tf_op jit(solution)/shard_map/ppermute | solution.py:21
  (131 other events, 1255.1 us)
Sparse Core Ops, SparseCore 0:
  11.5 106.0 all-gather.7
  438.1 31.3 all-gather.9
  484.2 27.5 all-gather.5
  517.5 141.2 reduce-scatter.1

commit v2 on v1

v2 whole, which is shorter than its diff:
```python
import functools

import jax
import jax.numpy as jnp
from jax import lax
from jax.experimental import pallas as pl
from jax.experimental.pallas import tpu as pltpu
from jax.sharding import PartitionSpec as P

HD = 64
PATCHES = 256
BLOCK_ROWS = 256
EPSILON = 1e-06
HIGHEST = lax.Precision.HIGHEST
BF = jnp.bfloat16
F32 = jnp.float32


def bits_of(size):
    return size.bit_length() - 1


def swap(value, axis, bit):
    size = lax.axis_size(axis)
    return lax.ppermute(value, axis, [(i, i ^ (1 << bit)) for i in range(size)])


def my_bit(axis, bit):
    return (lax.axis_index(axis) >> bit) & 1


def cube_sum(value, dims):
    for axis, bit in dims:
        value = value + swap(value, axis, bit)
    return value


def cube_gather(block, dims):
    held = block[None]
    for axis, bit in dims:
        other = swap(held, axis, bit)
        high = my_bit(axis, bit) == 1
        held = jnp.concatenate([jnp.where(high, other, held), jnp.where(high, held, other)])
    return held


def cube_scatter(parts, dims):
    for axis, bit in reversed(dims):
        half = parts.shape[0] // 2
        mine = my_bit(axis, bit)
        send = lax.dynamic_slice_in_dim(parts, (1 - mine) * half, half)
        keep = lax.dynamic_slice_in_dim(parts, mine * half, half)
        got = swap(send, axis, bit)
        parts = keep.astype(F32) + got.astype(F32)
        if half > 1:
            parts = parts.astype(BF)
    return parts[0]


def cube_dims(order):
    return [("sp", bit) for bit in order[0]] + order[1]


def in_device_order(gathered, dims, back=False):
    count = len(dims)
    want = [("tp", b) for b in reversed(range(bits_of(lax.axis_size("tp"))))]
    want += [("sp", b) for b in reversed(range(bits_of(lax.axis_size("sp"))))]
    have = list(reversed(dims))
    tail = gathered.shape[1:]
    if back:
        have, want = want, have
    split = gathered.reshape((2,) * count + tail)
    order = [have.index(w) for w in want]
    split = split.transpose(order + [count + i for i in range(len(tail))])
    return split.reshape((2**count,) + tail)


VMEM_BYTES = 52 * 1024 * 1024


def near_gather(block, dims):
    held = block[None]
    for axis, bit in dims[:-1]:
        held = jnp.concatenate([held, swap(held, axis, bit)])
    return held, swap(held, *dims[-1])


def near_scatter(low, high, dims):
    got = swap(high, *dims[-1])
    for axis, bit in reversed(dims[:-1]):
        half = low.shape[0] // 2
        total = low.astype(F32) + got.astype(F32)
        low, high = total[:half].astype(BF), total[half:].astype(BF)
        got = swap(high, axis, bit)
    return (low.astype(F32) + got.astype(F32))[0]


def dims_masks(dims):
    masks = []
    for m in range(2 ** len(dims)):
        flip = {"tp": 0, "sp": 0}
        for place, (axis, bit) in enumerate(dims):
            flip[axis] |= ((m >> place) & 1) << bit
        masks.append((flip["tp"], flip["sp"]))
    return masks


def dot(left, right, left_dim, right_dim):
    return lax.dot_general(
        left, right, (((left_dim,), (right_dim,)), ((), ())), preferred_element_type=F32
    )


def norm_rows(operand):
    centred = operand - jnp.mean(operand, axis=-1, keepdims=True)
    inverse = lax.rsqrt(jnp.mean(centred * centred, axis=-1, keepdims=True) + EPSILON)
    return (centred * inverse, inverse)


def norm_back(incoming, normed, inverse):
    first_mean = jnp.mean(incoming, axis=-1, keepdims=True)
    second_mean = jnp.mean(incoming * normed, axis=-1, keepdims=True)
    return inverse * (incoming - first_mean - normed * second_mean)


def params(count=1):
    return pltpu.CompilerParams(
        dimension_semantics=("arbitrary",) * count, vmem_limit_bytes=VMEM_BYTES
    )


def whole(shape):
    zeros = (0,) * len(shape)
    return pl.BlockSpec(shape, lambda g, meta: zeros, pipeline_mode=pl.Buffered(1))


def place_weights(meta, pieces, masks, target):
    if masks is None:
        target[...] = pieces[0][...]
        return
    rows = pieces[0].shape[1]
    half = pieces[0].shape[0]
    for m, (tp_flip, sp_flip) in enumerate(masks):
        at = pl.multiple_of((meta[2] ^ sp_flip) * rows, rows)
        target[meta[1] ^ tp_flip, pl.ds(at, rows), :] = pieces[m // half][m % half]


def forward_kernel(masks, heads, masked, meta, x, hot, mst, key_r, key_c, *refs):
    pieces = refs[: 1 if masks is None else 2]
    x_out, h_out, qkv_out, p_out, o_out, a_out, w = refs[len(pieces) :]
    width = x.shape[2]
    head_tp = heads * HD

    @pl.when(pl.program_id(0) == 0)
    def _():
        place_weights(meta, pieces, masks, w)

    def modulation(i):
        return dot(hot[0], mst[:, i * width : (i + 1) * width], 1, 0)

    xin = x[0].astype(F32)
    normed = norm_rows(xin)[0]
    h = (normed * (1.0 + modulation(1)) + modulation(0)).astype(BF)
    h_out[0] = h
    bias = jnp.where(key_r[...] == key_c[...], 0.0, -1e30) if masked else None
    total = None
    for t in range(w.shape[0]):
        proj = dot(h, w[t, :, : 3 * head_tp], 1, 0).astype(BF)
        qkv_out[0, t] = proj
        outs = []
        for j in range(heads):
            q, k, v = (
                proj[:, i * head_tp + j * HD : i * head_tp + (j + 1) * HD] for i in range(3)
            )
            scores = dot(k, q * jnp.asarray(0.125, BF), 1, 1)
            if masked:
                scores = scores + bias
            e = jnp.exp(scores - jnp.max(scores, axis=0, keepdims=True))
            p = (e * (1.0 / jnp.sum(e, axis=0, keepdims=True))).astype(BF)
            p_out[0, t * heads + j] = p
            outs.append(dot(v, p, 0, 0))
        o = jnp.concatenate(outs, axis=0).T.astype(BF)
        o_out[0, t] = o
        part = dot(o, w[t, :, 3 * head_tp :], 1, 1)
        total = part if total is None else total + part
    a_out[0] = total.astype(BF)
    x_out[0] = (xin + modulation(2) * total).astype(x_out.dtype)


def weight_specs(pieces):
    return [whole(p.shape) for p in pieces]


def forward(meta, x, groups, hot, mst, keys, pieces, masks, n_tp, heads, out_dtype):
    rows, width = x.shape[1], x.shape[2]
    lanes = 4 * heads * HD
    same = hot.shape[0] == 1
    masked = keys is not None
    if keys is None:
        keys = jnp.zeros((rows, 1), jnp.int32), jnp.zeros((1, rows), jnp.int32)

    def out(*shape, dtype=BF):
        zeros = (0,) * (len(shape))
        return (
            jax.ShapeDtypeStruct((groups,) + shape, dtype),
            pl.BlockSpec((1,) + shape, lambda g, meta: (g,) + zeros),
        )

    outs = [
        out(rows, width, dtype=out_dtype),
        out(rows, width),
        out(n_tp, rows, 3 * heads * HD),
        out(n_tp * heads, rows, rows),
        out(n_tp, rows, heads * HD),
        out(rows, width),
    ]
    flops = 2 * groups * rows * width * n_tp * lanes + 4 * groups * rows * rows * n_tp * heads * HD
    return pl.pallas_call(
        functools.partial(forward_kernel, masks, heads, masked),
        out_shape=[o[0] for o in outs],
        grid_spec=pltpu.PrefetchScalarGridSpec(
            num_scalar_prefetch=1,
            grid=(groups,),
            in_specs=[
                pl.BlockSpec((1, rows, width), lambda g, meta: (g + meta[0], 0, 0)),
                pl.BlockSpec(
                    (1, rows, hot.shape[2]), lambda g, meta: (0 if same else g, 0, 0)
                ),
                whole(mst.shape),
                whole(keys[0].shape),
                whole(keys[1].shape),
            ]
            + weight_specs(pieces),
            out_specs=[o[1] for o in outs],
            scratch_shapes=[pltpu.VMEM((n_tp, width, lanes), BF)],
        ),
        compiler_params=params(),
        cost_estimate=pl.CostEstimate(
            flops=flops, bytes_accessed=16 * 2**20, transcendentals=groups * 12 * rows * rows
        ),
    )(meta, x, hot, mst, *keys, *pieces)


def backward_kernel(masks, heads, meta, dx, x, hot, hot_t, mst, a, qkv, p, *refs):
    pieces = refs[: 1 if masks is None else 2]
    dx_out, dqkv_out, da_out, dm_out, w = refs[len(pieces) :]
    width = x.shape[2]
    head_tp = heads * HD
    step = pl.program_id(0)

    @pl.when(step == 0)
    def _():
        place_weights(meta, pieces, masks, w)

    def modulation(i):
        return dot(hot[0], mst[:, i * width : (i + 1) * width], 1, 0)

    grad = dx[0].astype(F32)
    da = (modulation(2) * grad).astype(BF)
    da_out[0] = da
    dh = None
    for t in range(w.shape[0]):
        do = dot(da, w[t, :, 3 * head_tp :], 1, 0).astype(BF)
        got = [[], [], []]
        for j in range(heads):
            q, k, v = (
                qkv[0, t, :, i * head_tp + j * HD : i * head_tp + (j + 1) * HD]
                for i in range(3)
            )
            dop = do[:, j * HD : (j + 1) * HD]
            prob = p[0, t * heads + j]
            dp = dot(v, dop, 1, 1)
            prob32 = prob.astype(F32)
            prod = prob32 * dp
            ds = (prod - prob32 * jnp.sum(prod, axis=0, keepdims=True)).astype(BF)
            got[0].append(dot(k, ds, 0, 0))
            got[1].append(dot(ds, q, 1, 0))
            got[2].append(dot(prob, dop, 1, 0))
        dq = jnp.concatenate(got[0], axis=0).T * 0.125
        dk = jnp.concatenate(got[1], axis=1) * 0.125
        dqkv = jnp.concatenate([dq, dk] + got[2], axis=1).astype(BF)
        dqkv_out[0, t] = dqkv
        part = dot(dqkv, w[t, :, : 3 * head_tp], 1, 1)
        dh = part if dh is None else dh + part
    normed, inverse = norm_rows(x[0].astype(F32))
    dx_out[0] = (grad + norm_back(dh * (1.0 + modulation(1)), normed, inverse)).astype(BF)

    def clip_sum(value):
        return dot(hot_t[0], value.astype(BF), 1, 0)

    sums = [clip_sum(dh), clip_sum(dh * normed), clip_sum(grad * a[0].astype(F32))]

    @pl.when(step == 0)
    def _():
        for i in range(3):
            dm_out[:, i * width : (i + 1) * width] = sums[i]

    @pl.when(step > 0)
    def _():
        for i in range(3):
            dm_out[:, i * width : (i + 1) * width] += sums[i]


def backward(meta, dx, x, hot, hot_t, mst, a, qkv, p, pieces, masks, heads):
    groups, rows, width = dx.shape
    n_tp = qkv.shape[1]
    lanes = 4 * heads * HD
    same = hot.shape[0] == 1
    clips = hot_t.shape[1]

    def blocked(shape, offset=False, fixed=False):
        zeros = (0,) * (len(shape) - 1)
        return pl.BlockSpec(
            (1,) + shape[1:],
            lambda g, meta: (0 if fixed else g + meta[0] if offset else g,) + zeros,
        )

    flops = 2 * groups * rows * width * n_tp * lanes + 8 * groups * rows * rows * n_tp * heads * HD
    return pl.pallas_call(
        functools.partial(backward_kernel, masks, heads),
        out_shape=[
            jax.ShapeDtypeStruct((groups, rows, width), BF),
            jax.ShapeDtypeStruct(qkv.shape, BF),
            jax.ShapeDtypeStruct((groups, rows, width), BF),
            jax.ShapeDtypeStruct((clips, 3 * width), F32),
        ],
        grid_spec=pltpu.PrefetchScalarGridSpec(
            num_scalar_prefetch=1,
            grid=(groups,),
            in_specs=[
                blocked(dx.shape),
                blocked(x.shape, offset=True),
                blocked(hot.shape, fixed=same),
                blocked(hot_t.shape, fixed=same),
                whole(mst.shape),
                blocked(a.shape),
                blocked(qkv.shape),
                blocked(p.shape),
            ]
            + weight_specs(pieces),
            out_specs=[
                blocked((groups, rows, width)),
                blocked(qkv.shape),
                blocked((groups, rows, width)),
                pl.BlockSpec((clips, 3 * width), lambda g, meta: (0, 0)),
            ],
            scratch_shapes=[pltpu.VMEM((n_tp, width, lanes), BF)],
        ),
        compiler_params=params(),
        cost_estimate=pl.CostEstimate(
            flops=flops, bytes_accessed=16 * 2**20, transcendentals=0
        ),
    )(meta, dx, x, hot, hot_t, mst, a, qkv, p, *pieces)


def grads_kernel(masks, row_sp, meta, h, dqkv, da, o, *refs):
    outs, scratch = refs[:-1], refs[-1]
    groups = h.shape[0]
    wide = dqkv.shape[3]
    first, second = None, None
    for g in range(groups):
        one = dot(h[g], dqkv[g, 0], 0, 0)
        two = dot(da[g], o[g, 0], 0, 0)
        first = one if first is None else first + one
        second = two if second is None else second + two
    if masks is None:
        outs[0][0, :, :wide] = first.astype(BF)
        outs[0][0, :, wide:] = second.astype(BF)
        return
    scratch[:, :wide] = first
    scratch[:, wide:] = second
    for place in range(outs[0].shape[1]):
        at = pl.multiple_of((meta[2] ^ masks[place][1]) * row_sp, row_sp)
        outs[0][0, place] = scratch[pl.ds(at, row_sp), :].astype(BF)


def weight_grads(meta, h, dqkv, da, o, masks, row_sp):
    groups, rows, width = h.shape
    n_tp, wide, narrow = dqkv.shape[1], dqkv.shape[3], o.shape[3]
    lanes = wide + narrow
    if masks is None:
        flips = list(range(n_tp))
        shape = (n_tp, width, lanes)
        index = lambda g, meta: (g, 0, 0)
    else:
        flips = [masks[i * (len(masks) // n_tp)][0] for i in range(n_tp)]
        shape = (n_tp, len(masks) // n_tp, row_sp, lanes)
        index = lambda g, meta: (g, 0, 0, 0)

    def tp_of(g, meta):
        if masks is None:
            return g
        flip = 0
        for i, value in enumerate(flips):
            flip = jnp.where(g == i, value, flip)
        return meta[1] ^ flip

    return pl.pallas_call(
        functools.partial(grads_kernel, masks, row_sp),
        out_shape=[jax.ShapeDtypeStruct(shape, BF)],
        grid_spec=pltpu.PrefetchScalarGridSpec(
            num_scalar_prefetch=1,
            grid=(n_tp,),
            in_specs=[
                whole(h.shape),
                pl.BlockSpec((groups, 1, rows, wide), lambda g, m: (0, tp_of(g, m), 0, 0)),
                whole(da.shape),
                pl.BlockSpec((groups, 1, rows, narrow), lambda g, m: (0, tp_of(g, m), 0, 0)),
            ],
            out_specs=[pl.BlockSpec((1,) + shape[1:], index)],
            scratch_shapes=[pltpu.VMEM((width, lanes), F32)],
        ),
        compiler_params=params(),
        cost_estimate=pl.CostEstimate(
            flops=2 * groups * rows * width * n_tp * lanes,
            bytes_accessed=8 * 2**20,
            transcendentals=0,
        ),
    )(meta, h, dqkv, da, o)[0]


GELU_A = 0.7978845608028654
GELU_B = 0.044715


def feed_kernel(
    meta, x2, dy, hot, hot_t, mst, up, down, out, dx_out, dm_out, gup, gdown, h3, da3, acc, dh
):
    width = x2.shape[1]
    step = pl.program_id(0)

    def modulation(i):
        return dot(hot[...], mst[:, i * width : (i + 1) * width], 1, 0)

    @pl.when(step == 0)
    def _():
        normed = norm_rows(x2[...])[0]
        h3[...] = (normed * (1.0 + modulation(1)) + modulation(0)).astype(BF)
        da3[...] = (modulation(2) * dy[...].astype(F32)).astype(BF)
        acc[...] = jnp.zeros_like(acc)
        dh[...] = jnp.zeros_like(dh)

    wu = up[...].reshape(width, -1)
    wd = down[...].reshape(width, -1)
    u = dot(h3[...], wu, 1, 0)
    square = u * u
    th = jnp.tanh(GELU_A * (u + GELU_B * (square * u)))
    g = (0.5 * u * (1.0 + th)).astype(BF)
    slope = 0.5 * (1.0 + th) + (0.5 * GELU_A) * u * (1.0 - th * th) * (
        1.0 + (3.0 * GELU_B) * square
    )
    dg = dot(da3[...], wd, 1, 0)
    du = (dg * slope).astype(BF)
    acc[...] += dot(g, wd, 1, 1)
    dh[...] += dot(du, wu, 1, 1)
    gup[...] = dot(h3[...], du, 0, 0).astype(BF).reshape(gup.shape)
    gdown[...] = dot(da3[...], g, 0, 0).astype(BF).reshape(gdown.shape)

    @pl.when(step == pl.num_programs(0) - 1)
    def _():
        grad = dy[...].astype(F32)
        a3 = acc[...]
        xin = x2[...]
        normed, inverse = norm_rows(xin)
        out[...] = (xin + modulation(2) * a3).astype(BF)
        dh3 = dh[...]
        dx_out[...] = grad + norm_back(dh3 * (1.0 + modulation(1)), normed, inverse)
        for i, value in enumerate([dh3, dh3 * normed, grad * a3]):
            dm_out[:, i * width : (i + 1) * width] = dot(hot_t[...], value.astype(BF), 1, 0)


def feed_forward(meta, x2, dy, hot, hot_t, mst, feed):
    rows, width = x2.shape
    n_tp, n_sp, unused, row_sp, units = feed.shape
    clips = hot_t.shape[0]
    if row_sp % 16:
        blocked = feed.transpose(2, 0, 1, 3, 4).reshape(2, n_tp, width, units)
        up, down = blocked[0], blocked[1]
        specs = [pl.BlockSpec((1, width, units), lambda g, meta: (g, 0, 0))] * 2
        shape = (n_tp, width, units)
    else:
        up = down = feed
        specs = [
            pl.BlockSpec((1, n_sp, 1, row_sp, units), lambda g, meta, i=i: (g, 0, i, 0, 0))
            for i in range(2)
        ]
        shape = (n_tp, n_sp, 1, row_sp, units)
    zeros = (0,) * (len(shape) - 1)
    grad_spec = pl.BlockSpec((1,) + shape[1:], lambda g, meta: (g,) + zeros)
    plain = lambda s: pl.BlockSpec(s, lambda g, meta: (0, 0))
    block_out, dx2, dm, gup, gdown = pl.pallas_call(
        feed_kernel,
        out_shape=[
            jax.ShapeDtypeStruct((rows, width), BF),
            jax.ShapeDtypeStruct((rows, width), F32),
            jax.ShapeDtypeStruct((clips, 3 * width), F32),
            jax.ShapeDtypeStruct(shape, BF),
            jax.ShapeDtypeStruct(shape, BF),
        ],
        grid_spec=pltpu.PrefetchScalarGridSpec(
            num_scalar_prefetch=1,
            grid=(n_tp,),
            in_specs=[
                whole(x2.shape),
                whole(dy.shape),
                whole(hot.shape),
                whole(hot_t.shape),
                whole(mst.shape),
            ]
            + specs,
            out_specs=[
                plain((rows, width)),
                plain((rows, width)),
                plain((clips, 3 * width)),
                grad_spec,
                grad_spec,
            ],
            scratch_shapes=[
                pltpu.VMEM((rows, width), BF),
                pltpu.VMEM((rows, width), BF),
                pltpu.VMEM((rows, width), F32),
                pltpu.VMEM((rows, width), F32),
            ],
        ),
        compiler_params=params(),
        cost_estimate=pl.CostEstimate(
            flops=12 * rows * width * units * n_tp,
            bytes_accessed=40 * 2**20,
            transcendentals=rows * units * n_tp,
        ),
    )(meta, x2, dy, hot, hot_t, mst, up, down)
    both = jnp.concatenate(
        [v.reshape(n_tp, n_sp, 1, row_sp, units) for v in (gup, gdown)], axis=2
    )
    return block_out, dx2, dm, both


def shards(
    tokens, condition, clip_ids, w_mod, w_qkv_s, w_o_s, w_qkv_t, w_o_t, w_up, w_down, grad_out
):
    n_tp, n_sp = lax.axis_size("tp"), lax.axis_size("sp")
    devices = n_tp * n_sp
    my_tp, my_sp = lax.axis_index("tp"), lax.axis_index("sp")
    width = tokens.shape[1]
    sp_frames = tokens.shape[0] // PATCHES
    frames = sp_frames // n_tp
    all_frames = sp_frames * n_sp
    places = PATCHES // devices
    per_block = max(1, min(places, BLOCK_ROWS // all_frames))
    blocks = places // per_block
    rows = all_frames * per_block
    clips = condition.shape[0]
    head_tp = w_o_s.shape[0]
    heads = head_tp // HD
    row_sp = w_up.shape[0]

    sp_bits = bits_of(n_sp)
    tp_bits = bits_of(n_tp)
    far_sp = [("sp", b) for b in reversed(range(1, sp_bits))]
    dims_s = far_sp + [("sp", 0), ("tp", 1), ("tp", 0)]
    dims_t = far_sp + [("tp", 1), ("sp", 0), ("tp", 0)]
    every = [("tp", b) for b in range(tp_bits)] + [("sp", b) for b in range(sp_bits)]
    near = row_sp % 16 == 0

    def gather(w_qkv, w_o, dims):
        flat = w_qkv.transpose(1, 0, 2).reshape(row_sp, -1)
        packed = jnp.concatenate([flat, w_o.T], axis=1)
        if near:
            return near_gather(packed, dims), dims_masks(dims)
        full = in_device_order(cube_gather(packed, dims), dims)
        return [full.reshape(n_tp, width, 4 * head_tp)], None

    def scatter(h, dqkv, da, o):
        if near:
            terms = weight_grads(meta0, h, dqkv, da, o, dims_masks(dims_s), row_sp)
            terms = terms.reshape(2, devices // 2, row_sp, 4 * head_tp)
            mine = near_scatter(terms[0], terms[1], dims_s)
        else:
            terms = weight_grads(meta0, h, dqkv, da, o, None, row_sp)
            terms = terms.reshape(devices, row_sp, 4 * head_tp)
            mine = cube_scatter(in_device_order(terms, dims_s, back=True), dims_s)
        mine = mine.reshape(row_sp, 4, head_tp)
        return mine[:, :3].transpose(1, 0, 2), mine[:, 3].T

    feed = lax.all_gather(jnp.stack([w_up, w_down.T]), ("tp", "sp"), axis=0)
    feed = feed.reshape(n_tp, n_sp, 2, row_sp, -1)

    cond_act = jax.nn.silu(condition).astype(BF)
    cond_rows = lax.dynamic_slice_in_dim(cond_act, my_sp * row_sp, row_sp, axis=1)
    modulation = cube_sum(
        jnp.dot(cond_rows, w_mod, preferred_element_type=F32),
        [("sp", b) for b in range(sp_bits)],
    )
    pieces_s, masks_s = gather(w_qkv_s, w_o_s, dims_s)
    pieces_t, masks_t = gather(w_qkv_t, w_o_t, dims_t)
    coarse = lax.reduce_precision(modulation, 8, 7)
    mst = jnp.concatenate([coarse, modulation - coarse]).astype(BF)
    mst_s, mst_t, mst_f = (
        mst[:, i * 3 * width : (i + 1) * 3 * width] for i in range(3)
    )

    def hot_of(ids):
        hot = (ids[..., None] == jnp.arange(clips, dtype=jnp.int32)).astype(BF)
        return jnp.concatenate([hot, hot], axis=-1), jnp.swapaxes(hot, -1, -2)

    first = my_sp * sp_frames + my_tp * frames
    ids_s = lax.dynamic_slice_in_dim(clip_ids, first, frames)
    hot_s, hot_s_t = hot_of(jnp.repeat(ids_s[:, None], PATCHES, axis=1))
    ids_t = jnp.repeat(clip_ids, per_block)
    hot_t, hot_t_t = hot_of(ids_t[None])
    hot_f, hot_f_t = hot_of(jnp.tile(ids_t, blocks))
    key = ids_t * per_block + jnp.tile(jnp.arange(per_block, dtype=jnp.int32), all_frames)
    keys = key[:, None], key[None, :]
    meta0 = jnp.stack([0 * my_tp, my_tp, my_sp]).astype(jnp.int32)
    meta_s = jnp.stack([my_tp * frames, my_tp, my_sp]).astype(jnp.int32)

    def to_places(value):
        split = value.reshape(frames, devices, blocks, per_block, width).transpose(1, 2, 0, 3, 4)
        got = lax.all_to_all(split, ("sp", "tp"), 0, 0, tiled=True)
        return got.transpose(1, 0, 2, 3, 4).reshape(blocks, rows, width)

    def to_frames(value):
        split = value.reshape(blocks, devices, frames, per_block, width).transpose(1, 0, 2, 3, 4)
        got = lax.all_to_all(split, ("sp", "tp"), 0, 0, tiled=True)
        return got.transpose(2, 0, 1, 3, 4).reshape(frames, PATCHES, width)

    def input_to_places(value):
        split = value.reshape(sp_frames, n_sp, n_tp, blocks, per_block, width)
        split = lax.dynamic_slice_in_dim(split, my_tp, 1, axis=2)[:, :, 0]
        got = lax.all_to_all(split.transpose(1, 2, 0, 3, 4), "sp", 0, 0, tiled=True)
        return got.transpose(1, 0, 2, 3, 4).reshape(blocks * rows, width)

    def places_to_output(value):
        split = value.reshape(blocks, n_sp, sp_frames, per_block, width).transpose(1, 0, 2, 3, 4)
        got = lax.all_to_all(split, "sp", 0, 0, tiled=True)
        got = lax.all_gather(got, "tp", axis=0)
        return got.transpose(3, 1, 0, 2, 4, 5).reshape(-1, width)

    grad_rows = input_to_places(grad_out)

    own = tokens.reshape(sp_frames, PATCHES, width)
    x1_frames, h1, qkv1, p1, o1, a1 = forward(
        meta_s, own, frames, hot_s, mst_s, None, pieces_s, masks_s, n_tp, heads, BF
    )
    x1 = to_places(x1_frames)
    x2, h2, qkv2, p2, o2, a2 = forward(
        meta0, x1, blocks, hot_t, mst_t, keys, pieces_t, masks_t, n_tp, heads, F32
    )

    block_out, dx2, dm_f, feed_grad = feed_forward(
        meta0, x2.reshape(blocks * rows, width), grad_rows, hot_f, hot_f_t, mst_f, feed
    )
    feed_grad = lax.psum_scatter(
        feed_grad.reshape(devices, 2, row_sp, -1), ("tp", "sp"), scatter_dimension=0
    ).astype(F32)

    dx1, dqkv2, da2, dm_t = backward(
        meta0, dx2.reshape(blocks, rows, width), x1, hot_t, hot_t_t, mst_t, a2, qkv2, p2,
        pieces_t, masks_t, heads,
    )
    dx1_frames = to_frames(dx1)
    sum_qt, sum_ot = scatter(h2, dqkv2, da2, o2)
    block_out = places_to_output(block_out)

    dx0, dqkv1, da1, dm_s = backward(
        meta_s, dx1_frames, own, hot_s, hot_s_t, mst_s, a1, qkv1, p1, pieces_s, masks_s, heads
    )
    sum_qs, sum_os = scatter(h1, dqkv1, da1, o1)
    grad_tokens = lax.all_gather(dx0.reshape(-1, width), "tp", axis=0, tiled=True)

    dm_rest = cube_sum(jnp.concatenate([dm_t, dm_f], axis=-1), every)
    dm_s = cube_sum(dm_s, every)
    dm_low = jnp.concatenate([dm_s, dm_rest], axis=-1).astype(BF)
    grad_mod = jnp.dot(cond_rows.T, dm_low, preferred_element_type=F32)
    grad_act = jnp.dot(dm_low, w_mod.T, preferred_element_type=F32)
    sp_dims = [("sp", b) for b in range(sp_bits)]
    grad_act = cube_gather(grad_act, sp_dims).transpose(1, 0, 2).reshape(clips, width)
    unused, silu_pull = jax.vjp(jax.nn.silu, condition)
    grad_condition = silu_pull(grad_act)[0]
    return (
        block_out,
        grad_tokens,
        grad_condition,
        grad_mod,
        sum_qs,
        sum_os,
        sum_qt,
        sum_ot,
        feed_grad[0],
        feed_grad[1].T,
    )


def solution(mesh):
    placed = (
        P("sp", None),
        P(),
        P(),
        P("sp", None),
        P(None, "sp", "tp"),
        P("tp", "sp"),
        P(None, "sp", "tp"),
        P("tp", "sp"),
        P("sp", "tp"),
        P("tp", "sp"),
        P("sp", None),
    )
    return jax.shard_map(
        shards,
        mesh=mesh,
        in_specs=placed,
        out_specs=(
            P("sp", None),
            P("sp", None),
            P(),
            P("sp", None),
            P(None, "sp", "tp"),
            P("tp", "sp"),
            P(None, "sp", "tp"),
            P("tp", "sp"),
            P("sp", "tp"),
            P("tp", "sp"),
        ),
        check_vma=False,
    )
```

time: 747 us -> 538 us (0.72)
  local copies, waits for them, and re-layouts: 272 us -> 83.3 us
  matrix products: 122 us -> 2.75 us
  Pallas kernels: 0 us -> 114 us
  other arithmetic: 95.7 us -> 23.6 us
  waiting for transfers between devices: 162 us -> 196 us
  blocking collectives: 0 us -> 24 us
    dot_general x39 -> x0, matrix products: 119 us -> none  [the longest x36 113 us: mm(): return jnp.einsum(form, left, right, preferred_element_type=F32)]
    pallas_call x0 -> x7, Pallas kernels: none -> 114 us  [the longest x2 40 us: backward(): pl.pallas_call(functools.partial(backward_kernel, masks, heads), out_shap...]
    reshape x6 -> x5, local copies, waits for them, and re-layouts: 60.6 us -> 7.33 us  [the longest x1 2.45 us: to_frames(): return got.transpose(2, 0, 1, 3, 4).reshape(frames, PATCHES, width)]
    another operation x6 -> x0, local copies, waits for them, and re-layouts: 50.7 us -> none  [the longest x2 26.3 us: unpack(): full = in_device_order(gathered, dims).reshape(n_tp, width, 4, head_tp)]
    convert_element_type x23 -> x3, other arithmetic: 31 us -> 1.08 us  [the longest x1 1 us: shards(): feed_grad = lax.psum_scatter(feed_grad.reshape(devices, 2, row_sp, -1), (...]
    all_to_all x0 -> x1, blocking collectives: none -> 24 us  [places_to_output(): got = lax.all_to_all(split, 'sp', 0, 0, tiled=True)]
    convert_element_type x12 -> x0, local copies, waits for them, and re-layouts: 22.1 us -> none  [the longest x1 4.48 us: shards(): qkv2 = mm('brd,de->bre', h2, qkv_t).astype(BF)]
    transpose x7 -> x9, local copies, waits for them, and re-layouts: 29.4 us -> 8.56 us  [the longest x1 2.31 us: input_to_places(): return got.transpose(1, 0, 2, 3, 4).reshape(blocks * rows, width)]
  transfers between devices with their start and end apart: 44 -> 43, of which waited for: 24 -> 18; matrix products, arithmetic and copies ran while one was open for 55% -> 17% of each run, Pallas kernels for 0% -> 17%
where the time goes in v2:
time: 538 us; the launch traced here: 530 us
  waiting for transfers between devices  196 us (36%)
  Pallas kernels  114 us (21%)
  local copies, waits for them, and re-layouts  83.3 us (15%)
  starting transfers between devices  70.8 us (13%)
  blocking collectives  24 us (4%)
  other arithmetic  23.6 us (4%)
  between operations  14.8 us (3%)
    ppermute x36, waiting for transfers between devices, swap(): return lax.ppermute(value, axis, [(i, i ^ 1 << bit) for i in range(size)])  145 us
    ppermute x36, starting transfers between devices, swap(): return lax.ppermute(value, axis, [(i, i ^ 1 << bit) for i in range(size)])  54.4 us
    pallas_call x2, Pallas kernels, backward(): pl.pallas_call(functools.partial(backward_kernel, masks, heads), out_shap...  40 us
    pallas_call x2, Pallas kernels, forward(): pl.pallas_call(functools.partial(forward_kernel, masks, heads, masked), o...  34 us
    all_to_all x1, blocking collectives, places_to_output(): got = lax.all_to_all(split, 'sp', 0, 0, tiled=True)  24 us
    pallas_call x1, Pallas kernels, feed_forward(): pl.pallas_call(feed_kernel, out_shape=[jax.ShapeDtypeStruct((rows, width)...  23.6 us
    unnamed x44, local copies, waits for them, and re-layouts  21 us
    all_to_all x1, waiting for transfers between devices, to_frames(): got = lax.all_to_all(split, ('sp', 'tp'), 0, 0, tiled=True)  20.5 us
  transfers between devices with their start and end apart: 43, of which 18 were waited for; matrix products, arithmetic and copies ran while one was open for 17% of the time, Pallas kernels for 17%

profile of v2, /device:TPU:0, one launch (start us, length us, event | category | flops | bytes accessed | tf_op | source)
XLA Modules:
  0.0 529.6 jit_solution(3232329252017656933)
XLA Ops:
  16.0 7.0 %collective-permute-done.3 = bf16[1,96,768]{2,1,0:T(8,128)(2,1)S(1)} collective-permute-done((bf16[1,96,768]{2,1,0:T(8,128)(2,1)S(1)}, bf16[1,96,768]{2,1,0:T(8,128)(2,1)S(1)}, u32[]{:S(2)}, u32[]{:S(2)}) %collective-permute-start.3) | collective-permute-done | bytes 147488 | tf_op jit(solution)/shard_map/ppermute | solution.py:25
  28.4 12.4 %collective-permute-done.4 = bf16[2,96,768]{2,1,0:T(8,128)(2,1)S(1)} collective-permute-done((bf16[2,96,768]{2,1,0:T(8,128)(2,1)S(1)}, bf16[2,96,768]{2,1,0:T(8,128)(2,1)S(1)}, u32[]{:S(2)}, u32[]{:S(2)}) %collective-permute-start.4) | collective-permute-done | bytes 294944 | tf_op jit(solution)/shard_map/ppermute | solution.py:25
  44.0 14.7 %collective-permute-done.9 = bf16[2,96,768]{2,1,0:T(8,128)(2,1)S(1)} collective-permute-done((bf16[2,96,768]{2,1,0:T(8,128)(2,1)S(1)}, bf16[2,96,768]{2,1,0:T(8,128)(2,1)S(1)}, u32[]{:S(2)}, u32[]{:S(2)}) %collective-permute-start.9) | collective-permute-done | bytes 294944 | tf_op jit(solution)/shard_map/ppermute | solution.py:25
  67.5 6.3 %reshape.188 = bf16[8,8,4,2,4,768]{5,4,3,2,1,0:T(4,128)(2,1)} reshape(bf16[2048,768]{1,0:T(8,128)(2,1)} %param.21) | data formatting | bytes 6291456 | tf_op jit(solution)/shard_map/reshape | solution.py:628
  76.3 6.6 %all-to-all-start.1 = ((bf16[8,2,8,4,768]{4,3,2,1,0:T(4,128)(2,1)}), bf16[8,2,8,4,768]{4,3,2,1,0:T(4,128)(2,1)}, u32[]{:S(2)}, u32[]{:S(2)}) async-start(bf16[8,2,8,4,768]{4,3,2,1,0:T(4,128)(2,1)} %copy_bitcast_fusion), calls=%async_computation.1 | async-start | bytes 1572864 | tf_op jit(solution)/shard_map/all_to_all | solution.py:630
  92.1 21.3 %collective-permute-done.6 = bf16[8,96,768]{2,1,0:T(8,128)(2,1)} collective-permute-done((bf16[8,96,768]{2,1,0:T(8,128)(2,1)}, bf16[8,96,768]{2,1,0:T(8,128)(2,1)}, u32[]{:S(2)}, u32[]{:S(2)}) %collective-permute-start.6) | collective-permute-done | bytes 1179680 | tf_op jit(solution)/shard_map/ppermute | solution.py:25
  127.8 17.0 %shard_map.186 = (bf16[2,256,768]{2,1,0:T(8,128)(2,1)S(1)}, bf16[2,256,768]{2,1,0:T(8,128)(2,1)S(1)}, bf16[2,4,256,576]{3,2,1,0:T(8,128)(2,1)}, bf16[2,12,256,25...) custom-call(s32[3]{0:T(128)S(1)} %add_add_fusion.1.meta, ...), custom_call_target="tpu_custom_call" | custom-call | flops 2818572288 | bytes 16777216 | tf_op jit(solution)/shard_map/pallas_call | solution.py:218
  148.2 5.6 %all-to-all-start = ((bf16[32,2,2,4,768]{4,3,2,1,0:T(4,128)(2,1)}), bf16[32,2,2,4,768]{4,3,2,1,0:T(4,128)(2,1)S(1)}, u32[]{:S(2)}, u32[]{:S(2)}) async-start(bf16[32,2,2,4,768]{4,3,2,1,0:T(4,128)(2,1)} %bitcast.84), calls=%async_computation | async-start | bytes 1572864 | tf_op jit(solution)/shard_map/all_to_all | solution.py:619
  159.7 14.7 %all-to-all-done = bf16[32,2,2,4,768]{4,3,2,1,0:T(4,128)(2,1)S(1)} async-done(((bf16[32,2,2,4,768]{4,3,2,1,0:T(4,128)(2,1)}), bf16[32,2,2,4,768]{4,3,2,1,0:T(4,128)(2,1)S(1)}, u32[]{:S(2)}, u32[]{:S(2)}) %all-to-all-start) | async-done | bytes 786464 | tf_op jit(solution)/shard_map/all_to_all | solution.py:619
  177.9 17.0 %shard_map.187 = (f32[2,256,768]{2,1,0:T(8,128)}, bf16[2,256,768]{2,1,0:T(8,128)(2,1)S(1)}, bf16[2,4,256,576]{3,2,1,0:T(8,128)(2,1)}, bf16[2,12,256,256]{3,2,1,0...) custom-call(s32[3]{0:T(128)S(1)} %add_add_fusion.meta, ...), custom_call_target="tpu_custom_call" | custom-call | flops 2818572288 | bytes 16777216 | tf_op jit(solution)/shard_map/pallas_call | solution.py:218
  196.9 23.6 %shard_map.188 = (bf16[512,768]{1,0:T(8,128)(2,1)S(1)}, f32[512,768]{1,0:T(8,128)}, f32[4,2304]{1,0:T(4,128)S(1)}, bf16[4,8,1,96,768]{4,3,2,1,0:T(8,128)(2,1)}, bf16[4,8,1,96,768]{4,3,2,1,0:T(8,128)(2,1)}) custom-call(s32[3]{0:T(128)S(1)} %add_add_fusion.meta, f32[512,768]{1,0:T(8,128)} %bitcast.112, bf16[512,768]{1,0:T(8,128)(2,1)S(1)} %copy-done.6, ...), custom_call_target="tpu_custom_call" | custom-call | flops 14495514624 | bytes 41943040 | tf_op jit(solution)/shard_map/pallas_call | solution.py:491
  225.2 24.0 %all_to_all.20 = bf16[8,2,8,4,768]{4,3,2,1,0:T(4,128)(2,1)S(1)} all-to-all(bf16[8,2,8,4,768]{4,3,2,1,0:T(4,128)(2,1)S(1)} %bitcast.90), channel_id=1, replica_groups=mesh['tp'=4,'sp'=8] {'sp'}, dimensions={0} | all-to-all | bytes 1572864 | tf_op jit(solution)/shard_map/all_to_all | solution.py:635
  250.2 20.2 %shard_map.189 = (bf16[2,256,768]{2,1,0:T(8,128)(2,1)S(1)}, bf16[2,4,256,576]{3,2,1,0:T(8,128)(2,1)}, bf16[2,256,768]{2,1,0:T(8,128)(2,1)S(1)}, f32[4,2304]{1,0:T(4,128)S(1)}) custom-call(s32[3]{0:T(128)S(1)} %add_add_fusion.meta, f32[2,256,768]{2,1,0:T(8,128)} %bitcast.99, bf16[2,256,768]{2,1,0:T(8,128)(2,1)} %reshape.185.x, ...), custom_call_target="tpu_custom_call" | custom-call | flops 3221225472 | bytes 16777216 | tf_op jit(solution)/shard_map/pallas_call | solution.py:319
  280.6 20.5 %all-to-all-done.3 = bf16[32,2,2,4,768]{4,3,1,2,0:T(4,128)(2,1)} async-done(((bf16[32,2,2,4,768]{4,3,1,2,0:T(4,128)(2,1)}), bf16[32,2,2,4,768]{4,3,1,2,0:T(4,128)(2,1)}, u32[]{:S(2)}, u32[]{:S(2)}) %all-to-all-start.3) | async-done | bytes 786464 | tf_op jit(solution)/shard_map/all_to_all | solution.py:624
  305.9 19.8 %shard_map.190 = (bf16[2,256,768]{2,1,0:T(8,128)(2,1)S(1)}, bf16[2,4,256,576]{3,2,1,0:T(8,128)(2,1)}, bf16[2,256,768]{2,1,0:T(8,128)(2,1)S(1)}, f32[4,2304]{1,0:T(4,128)S(1)}) custom-call(s32[3]{0:T(128)S(1)} %add_add_fusion.1.meta, bf16[2,256,768]{2,1,0:T(8,128)(2,1)} %reshape.195.dx, bf16[8,256,768]{2,1,0:T(8,128)(2,1)} %bitcast.92, ...), custom_call_target="tpu_custom_call" | custom-call | flops 3221225472 | bytes 16777216 | tf_op jit(solution)/shard_map/pallas_call | solution.py:319
  327.5 8.7 %pad_maximum_fusion = bf16[4,8,2,96,768]{4,3,2,1,0:T(8,128)(2,1)} fusion(bf16[4,8,1,96,768]{4,3,2,1,0:T(8,128)(2,1)} %get-tuple-element.59, bf16[4,8,1,96,768]{4,3,2,1,0:T(8,128)(2,1)} %get-tuple-element.58), kind=kLoop, calls=%fused_computation | loop fusion | flops 4718592 | bytes 18874368 | tf_op jit(solution)/shard_map/concatenate | solution.py:532
  346.9 8.4 %shard_map.192 = bf16[4,8,96,768]{3,2,1,0:T(8,128)(2,1)} custom-call(s32[3]{0:T(128)S(1)} %add_add_fusion.meta, bf16[2,256,768]{2,1,0:T(8,128)(2,1)S(1)} %get-tuple-element.54.h, bf16[2,4,256,576]{3,2,1,0:T(8,128)(2,1)} %get-tuple-element.55.dqkv, bf16[2,256,768]{2,1,0:T(8,128)(2,1)S(1)} %copy-done.4, bf16[2,4,256,192]{3,2,1,0:T(8,128)(2,1)} %get-tuple-element.57.o), custom_call_target="tpu_custom_call" | custom-call | flops 2415919104 | bytes 8388608 | tf_op jit(solution)/shard_map/pallas_call | solution.py:398
  362.1 8.1 %shard_map.191 = bf16[4,8,96,768]{3,2,1,0:T(8,128)(2,1)} custom-call(s32[3]{0:T(128)S(1)} %add_add_fusion.meta, bf16[2,256,768]{2,1,0:T(8,128)(2,1)S(1)} %get-tuple-element.50.h, bf16[2,4,256,576]{3,2,1,0:T(8,128)(2,1)} %get-tuple-element.51.dqkv, bf16[2,256,768]{2,1,0:T(8,128)(2,1)S(1)} %copy-done.2, bf16[2,4,256,192]{3,2,1,0:T(8,128)(2,1)} %get-tuple-element.53.o), custom_call_target="tpu_custom_call" | custom-call | flops 2415919104 | bytes 8388608 | tf_op jit(solution)/shard_map/pallas_call | solution.py:398
  388.1 21.7 %collective-permute-done.32 = bf16[8,96,768]{2,1,0:T(8,128)(2,1)S(1)} collective-permute-done((bf16[8,96,768]{2,1,0:T(8,128)(2,1)S(1)}, bf16[8,96,768]{2,1,0:T(8,128)(2,1)S(1)}, u32[]{:S(2)}, u32[]{:S(2)}) %collective-permute-start.32) | collective-permute-done | bytes 1179680 | tf_op jit(solution)/shard_map/ppermute | solution.py:25
  413.4 27.9 %collective-permute-done.27 = bf16[8,96,768]{2,1,0:T(8,128)(2,1)S(1)} collective-permute-done((bf16[8,96,768]{2,1,0:T(8,128)(2,1)S(1)}, bf16[8,96,768]{2,1,0:T(8,128)(2,1)S(1)}, u32[]{:S(2)}, u32[]{:S(2)}) %collective-permute-start.27) | collective-permute-done | bytes 1179680 | tf_op jit(solution)/shard_map/ppermute | solution.py:25
  445.7 10.6 %collective-permute-done.34 = bf16[2,96,768]{2,1,0:T(8,128)(2,1)S(1)} collective-permute-done((bf16[2,96,768]{2,1,0:T(8,128)(2,1)}, bf16[2,96,768]{2,1,0:T(8,128)(2,1)S(1)}, u32[]{:S(2)}, u32[]{:S(2)}) %collective-permute-start.34) | collective-permute-done | bytes 294944 | tf_op jit(solution)/shard_map/ppermute | solution.py:25
  477.9 9.7 %collective-permute-done.30 = bf16[1,96,768]{2,1,0:T(8,128)(2,1)S(1)} collective-permute-done((bf16[1,96,768]{2,1,0:T(8,128)(2,1)S(1)}, bf16[1,96,768]{2,1,0:T(8,128)(2,1)S(1)}, u32[]{:S(2)}, u32[]{:S(2)}) %collective-permute-start.30) | collective-permute-done | bytes 147488 | tf_op jit(solution)/shard_map/ppermute | solution.py:25
  494.1 5.9 %reshape.192 = bf16[2048,768]{1,0:T(8,128)(2,1)} reshape(bf16[8,8,4,2,4,768]{5,4,3,2,1,0:T(4,128)(2,1)} %copy.118) | data formatting | bytes 6291456 | tf_op jit(solution)/shard_map/reshape | solution.py:637
  500.7 16.3 %reduce-scatter.2.cloned.1.call-done = bf16[1,2,96,768]{3,2,1,0:T(8,128)(2,1)} async-done(((bf16[32,2,96,768]{3,2,1,0:T(8,128)(2,1)}), bf16[1,2,96,768]{3,2,1,0:T(8,128)(2,1)}) %reduce-scatter.2.cloned.1.call-update) | async-done | bytes 294928 | tf_op jit(solution)/shard_map/reduce_scatter | solution.py:653
  (230 shorter events, 166.8 us)
Async XLA Ops:
  7.2 188.5 %all-gather.8.cloned.1.call-start = ((), (), s32[]{:S(2)}) async-start(), calls=%async_computation.7 | async-start | bytes 9732096 | tf_op jit(solution)/shard_map/all_gather | solution.py:585
  23.1 17.7 %collective-permute-start.4 = (bf16[2,96,768]{2,1,0:T(8,128)(2,1)S(1)}, bf16[2,96,768]{2,1,0:T(8,128)(2,1)S(1)}, u32[]{:S(2)}, u32[]{:S(2)}) collective-permute-start(bf16[2,96,768]{2,1,0:T(8,128)(2,1)S(1)} %pad_maximum_fusion.5), channel_id=1, source_target_pairs={{0,2},{1,3},{2,0},{3,1},{4,6},{5,7},{6,4},{7,5},{8,10},{9,11},{10,... | collective-permute-start | bytes 884744 | tf_op jit(solution)/shard_map/ppermute | solution.py:25
  25.1 17.9 %collective-permute-start.8 = (bf16[1,96,768]{2,1,0:T(8,128)(2,1)S(1)}, bf16[1,96,768]{2,1,0:T(8,128)(2,1)S(1)}, u32[]{:S(2)}, u32[]{:S(2)}) collective-permute-start(bf16[1,96,768]{2,1,0:T(8,128)(2,1)S(1)} %get-tuple-element.111), channel_id=1, source_target_pairs={{0,4},{1,5},{2,6},{3,7},{4,0},{5,1},{6,2},{7,3},{8,12},{9,13},{10,... | collective-permute-start | bytes 442376 | tf_op jit(solution)/shard_map/ppermute | solution.py:25
  41.7 19.4 %collective-permute-start.5 = (bf16[4,96,768]{2,1,0:T(8,128)(2,1)}, bf16[4,96,768]{2,1,0:T(8,128)(2,1)S(1)}, u32[]{:S(2)}, u32[]{:S(2)}) collective-permute-start(bf16[4,96,768]{2,1,0:T(8,128)(2,1)} %pad_maximum_fusion.3), channel_id=1, source_target_pairs={{0,1},{1,0},{2,3},{3,2},{4,5},{5,4},{6,7},{7,6},{8,9},{9,8},{10,11... | collective-permute-start | bytes 1769480 | tf_op jit(solution)/shard_map/ppermute | solution.py:25
  59.6 23.4 %collective-permute-start.10 = (bf16[4,96,768]{2,1,0:T(8,128)(2,1)}, bf16[4,96,768]{2,1,0:T(8,128)(2,1)}, u32[]{:S(2)}, u32[]{:S(2)}) collective-permute-start(bf16[4,96,768]{2,1,0:T(8,128)(2,1)} %pad_maximum_fusion.4), channel_id=1, source_target_pairs={{0,16},{8,24},{16,0},{24,8},{1,17},{9,25},{17,1},{25,9},{2,18},{10... | collective-permute-start | bytes 1769480 | tf_op jit(solution)/shard_map/ppermute | solution.py:25
  62.3 51.2 %collective-permute-start.6 = (bf16[8,96,768]{2,1,0:T(8,128)(2,1)}, bf16[8,96,768]{2,1,0:T(8,128)(2,1)}, u32[]{:S(2)}, u32[]{:S(2)}) collective-permute-start(bf16[8,96,768]{2,1,0:T(8,128)(2,1)} %pad_maximum_fusion.1), channel_id=1, source_target_pairs={{0,16},{8,24},{16,0},{24,8},{1,17},{9,25},{17,1},{25,9},{2,18},{10... | collective-permute-start | bytes 3538952 | tf_op jit(solution)/shard_map/ppermute | solution.py:25
  63.2 26.6 %collective-permute-start = (f32[4,6912]{1,0:T(4,128)S(1)}, f32[4,6912]{1,0:T(4,128)S(1)}, u32[]{:S(2)}, u32[]{:S(2)}) collective-permute-start(f32[4,6912]{1,0:T(4,128)S(1)} %fusion.17), channel_id=1, source_target_pairs={{0,1},{1,0},{2,3},{3,2},{4,5},{5,4},{6,7},{7,6},{8,9},{9,8},{10,11... | collective-permute-start | bytes 331784 | tf_op jit(solution)/shard_map/ppermute | solution.py:25
  76.3 71.9 %all-to-all-start.1 = ((bf16[8,2,8,4,768]{4,3,2,1,0:T(4,128)(2,1)}), bf16[8,2,8,4,768]{4,3,2,1,0:T(4,128)(2,1)}, u32[]{:S(2)}, u32[]{:S(2)}) async-start(bf16[8,2,8,4,768]{4,3,2,1,0:T(4,128)(2,1)} %copy_bitcast_fusion), calls=%async_computation.1 | async-start | bytes 1572864 | tf_op jit(solution)/shard_map/all_to_all | solution.py:630
  85.2 38.4 %collective-permute-start.11 = (bf16[8,96,768]{2,1,0:T(8,128)(2,1)}, bf16[8,96,768]{2,1,0:T(8,128)(2,1)}, u32[]{:S(2)}, u32[]{:S(2)}) collective-permute-start(bf16[8,96,768]{2,1,0:T(8,128)(2,1)} %pad_maximum_fusion.2), channel_id=1, source_target_pairs={{0,1},{1,0},{2,3},{3,2},{4,5},{5,4},{6,7},{7,6},{8,9},{9,8},{10,11... | collective-permute-start | bytes 3538952 | tf_op jit(solution)/shard_map/ppermute | solution.py:25
  89.8 26.7 %collective-permute-start.1 = (f32[4,6912]{1,0:T(4,128)S(1)}, f32[4,6912]{1,0:T(4,128)S(1)}, u32[]{:S(2)}, u32[]{:S(2)}) collective-permute-start(f32[4,6912]{1,0:T(4,128)S(1)} %add.116), channel_id=1, source_target_pairs={{0,2},{1,3},{2,0},{3,1},{4,6},{5,7},{6,4},{7,5},{8,10},{9,11},{10,... | collective-permute-start | bytes 331784 | tf_op jit(solution)/shard_map/ppermute | solution.py:25
  126.0 51.9 %collective-permute-start.12 = (bf16[16,96,768]{2,1,0:T(8,128)(2,1)}, bf16[16,96,768]{2,1,0:T(8,128)(2,1)}, u32[]{:S(2)}, u32[]{:S(2)}) collective-permute-start(bf16[16,96,768]{2,1,0:T(8,128)(2,1)} %constant_dynamic-update-slice_fusion.5.refs_0_), channel_id=1, source_target_pairs={{0,8},{8,0},{16,24},{24,16},{1,9},{9,1},{17,25},{25,17},{2,10},{10... | collective-permute-start | bytes 7077896 | tf_op jit(solution)/shard_map/ppermute | solution.py:25
  148.2 26.3 %all-to-all-start = ((bf16[32,2,2,4,768]{4,3,2,1,0:T(4,128)(2,1)}), bf16[32,2,2,4,768]{4,3,2,1,0:T(4,128)(2,1)S(1)}, u32[]{:S(2)}, u32[]{:S(2)}) async-start(bf16[32,2,2,4,768]{4,3,2,1,0:T(4,128)(2,1)} %bitcast.84), calls=%async_computation | async-start | bytes 1572864 | tf_op jit(solution)/shard_map/all_to_all | solution.py:619
  153.8 334.9 %all-gather.10.cloned.1.call-start = ((), (), s32[]{:S(2)}) async-start(), calls=%async_computation.8 | async-start | bytes 3932160 | tf_op jit(solution)/shard_map/all_gather | solution.py:636
  276.8 24.3 %all-to-all-start.3 = ((bf16[32,2,2,4,768]{4,3,1,2,0:T(4,128)(2,1)}), bf16[32,2,2,4,768]{4,3,1,2,0:T(4,128)(2,1)}, u32[]{:S(2)}, u32[]{:S(2)}) async-start(bf16[32,2,2,4,768]{4,3,1,2,0:T(4,128)(2,1)} %bitcast.89), calls=%async_computation.3 | async-start | bytes 1572864 | tf_op jit(solution)/shard_map/all_to_all | solution.py:624
  280.5 220.2 %all-gather.6.cloned.1.call-start = ((), (), s32[]{:S(2)}) async-start(), calls=%async_computation.5 | async-start | bytes 3932160 | tf_op jit(solution)/shard_map/all_gather | solution.py:669
  327.5 189.5 %reduce-scatter.2.cloned.1.call-start = ((), (), s32[]{:S(2)}) async-start(), calls=%async_computation.6 | async-start | bytes 9732096 | tf_op jit(solution)/shard_map/reduce_scatter | solution.py:653
  359.6 20.4 %collective-permute-start.31 = (bf16[16,96,768]{2,1,0:T(8,128)(2,1)S(1)}, bf16[16,96,768]{2,1,0:T(8,128)(2,1)S(1)}, u32[]{:S(2)}, u32[]{:S(2)}) collective-permute-start(bf16[16,96,768]{2,1,0:T(8,128)(2,1)S(1)} %bitcast.93), channel_id=1, source_target_pairs={{0,8},{8,0},{16,24},{24,16},{1,9},{9,1},{17,25},{25,17},{2,10},{10... | collective-permute-start | bytes 7077896 | tf_op jit(solution)/shard_map/ppermute | solution.py:25
  360.1 16.5 %collective-permute-start.22 = (f32[4,4608]{1,0:T(4,128)S(1)}, f32[4,4608]{1,0:T(4,128)S(1)}, u32[]{:S(2)}, u32[]{:S(2)}) collective-permute-start(f32[4,4608]{1,0:T(4,128)S(1)} %add.131), channel_id=1, source_target_pairs={{0,4},{1,5},{2,6},{3,7},{4,0},{5,1},{6,2},{7,3},{8,12},{9,13},{10,... | collective-permute-start | bytes 221192 | tf_op jit(solution)/shard_map/ppermute | solution.py:25
  380.9 29.0 %collective-permute-start.32 = (bf16[8,96,768]{2,1,0:T(8,128)(2,1)S(1)}, bf16[8,96,768]{2,1,0:T(8,128)(2,1)S(1)}, u32[]{:S(2)}, u32[]{:S(2)}) collective-permute-start(bf16[8,96,768]{2,1,0:T(8,128)(2,1)S(1)} %slice.157), channel_id=1, source_target_pairs={{0,16},{8,24},{16,0},{24,8},{1,17},{9,25},{17,1},{25,9},{2,18},{10... | collective-permute-start | bytes 3538952 | tf_op jit(solution)/shard_map/ppermute | solution.py:25
  384.4 56.8 %collective-permute-start.27 = (bf16[8,96,768]{2,1,0:T(8,128)(2,1)S(1)}, bf16[8,96,768]{2,1,0:T(8,128)(2,1)S(1)}, u32[]{:S(2)}, u32[]{:S(2)}) collective-permute-start(bf16[8,96,768]{2,1,0:T(8,128)(2,1)S(1)} %slice.145), channel_id=1, source_target_pairs={{0,16},{8,24},{16,0},{24,8},{1,17},{9,25},{17,1},{25,9},{2,18},{10... | collective-permute-start | bytes 3538952 | tf_op jit(solution)/shard_map/ppermute | solution.py:25
  387.8 23.8 %collective-permute-start.24 = (f32[2,4,96]{2,1,0:T(4,128)S(1)}, f32[2,4,96]{2,1,0:T(4,128)S(1)}, u32[]{:S(2)}, u32[]{:S(2)}) collective-permute-start(f32[2,4,96]{2,1,0:T(4,128)S(1)} %pad_maximum_fusion.14), channel_id=1, source_target_pairs={{0,2},{1,3},{2,0},{3,1},{4,6},{5,7},{6,4},{7,5},{8,10},{9,11},{10,... | collective-permute-start | bytes 9224 | tf_op jit(solution)/shard_map/ppermute | solution.py:25
  410.3 33.2 %collective-permute-start.33 = (bf16[4,96,768]{2,1,0:T(8,128)(2,1)S(1)}, bf16[4,96,768]{2,1,0:T(8,128)(2,1)S(1)}, u32[]{:S(2)}, u32[]{:S(2)}) collective-permute-start(bf16[4,96,768]{2,1,0:T(8,128)(2,1)S(1)} %slice.159), channel_id=1, source_target_pairs={{0,1},{1,0},{2,3},{3,2},{4,5},{5,4},{6,7},{7,6},{8,9},{9,8},{10,11... | collective-permute-start | bytes 1769480 | tf_op jit(solution)/shard_map/ppermute | solution.py:25
  411.6 34.0 %collective-permute-start.25 = (f32[4,4,96]{2,1,0:T(4,128)S(1)}, f32[4,4,96]{2,1,0:T(4,128)S(1)}, u32[]{:S(2)}, u32[]{:S(2)}) collective-permute-start(f32[4,4,96]{2,1,0:T(4,128)S(1)} %pad_maximum_fusion.12), channel_id=1, source_target_pairs={{0,4},{1,5},{2,6},{3,7},{4,0},{5,1},{6,2},{7,3},{8,12},{9,13},{10,... | collective-permute-start | bytes 18440 | tf_op jit(solution)/shard_map/ppermute | solution.py:25
  442.4 21.7 %collective-permute-start.28 = (bf16[4,96,768]{2,1,0:T(8,128)(2,1)}, bf16[4,96,768]{2,1,0:T(8,128)(2,1)}, u32[]{:S(2)}, u32[]{:S(2)}) collective-permute-start(bf16[4,96,768]{2,1,0:T(8,128)(2,1)} %slice.147), channel_id=1, source_target_pairs={{0,1},{1,0},{2,3},{3,2},{4,5},{5,4},{6,7},{7,6},{8,9},{9,8},{10,11... | collective-permute-start | bytes 1769480 | tf_op jit(solution)/shard_map/ppermute | solution.py:25
  (34 other events, 313.2 us)
Sparse Core Ops, SparseCore 0:
  11.5 110.1 all-gather.7
  250.3 27.5 all-gather.9
  327.6 29.1 all-gather.5
  362.5 154.4 reduce-scatter.1

commit v3 on v2

v3 whole, which is shorter than its diff:
```python
import functools

import jax
import jax.numpy as jnp
from jax import lax
from jax.experimental import pallas as pl
from jax.experimental.pallas import tpu as pltpu
from jax.sharding import PartitionSpec as P

HD = 64
PATCHES = 256
BLOCK_ROWS = 256
FEED_STEP = 2
TOKENS_STEP = 3
COSTS = (20, 20, 20, 1)
EPSILON = 1e-06
HIGHEST = lax.Precision.HIGHEST
BF = jnp.bfloat16
F32 = jnp.float32


def bits_of(size):
    return size.bit_length() - 1


def swap(value, axis, bit):
    size = lax.axis_size(axis)
    return lax.ppermute(value, axis, [(i, i ^ (1 << bit)) for i in range(size)])


def my_bit(axis, bit):
    return (lax.axis_index(axis) >> bit) & 1


def cube_sum(value, dims):
    for axis, bit in dims:
        value = value + swap(value, axis, bit)
    return value


def cube_gather(block, dims):
    held = block[None]
    for axis, bit in dims:
        other = swap(held, axis, bit)
        high = my_bit(axis, bit) == 1
        held = jnp.concatenate([jnp.where(high, other, held), jnp.where(high, held, other)])
    return held


def cube_scatter(parts, dims):
    for axis, bit in reversed(dims):
        half = parts.shape[0] // 2
        mine = my_bit(axis, bit)
        send = lax.dynamic_slice_in_dim(parts, (1 - mine) * half, half)
        keep = lax.dynamic_slice_in_dim(parts, mine * half, half)
        got = swap(send, axis, bit)
        parts = keep.astype(F32) + got.astype(F32)
        if half > 1:
            parts = parts.astype(BF)
    return parts[0]


def in_device_order(gathered, dims, back=False):
    count = len(dims)
    want = [("tp", b) for b in reversed(range(bits_of(lax.axis_size("tp"))))]
    want += [("sp", b) for b in reversed(range(bits_of(lax.axis_size("sp"))))]
    have = list(reversed(dims))
    tail = gathered.shape[1:]
    if back:
        have, want = want, have
    split = gathered.reshape((2,) * count + tail)
    order = [have.index(w) for w in want]
    split = split.transpose(order + [count + i for i in range(len(tail))])
    return split.reshape((2**count,) + tail)


VMEM_BYTES = 52 * 1024 * 1024


def cost(micros):
    return pl.CostEstimate(flops=micros * 10**9, bytes_accessed=2**10, transcendentals=0)


def after(value, *others):
    return lax.optimization_barrier((value,) + others)[0]


class Chain:
    def __init__(self, state, steps):
        self.state, self.steps = tuple(state), list(steps)

    def go(self):
        if self.steps:
            self.state = tuple(self.steps.pop(0)(*self.state))

    def run(self):
        while self.steps:
            self.go()
        return self.state


def stage(chains, *values):
    states, values = lax.optimization_barrier(([c.state for c in chains], values))
    for chain, state in zip(chains, states):
        chain.state = tuple(state)
    return values if len(values) != 1 else values[0]


def gather_chain(block, far, last):
    def far_step(dim):
        return lambda held: (jnp.concatenate([held, swap(held, *dim)]),)

    def split(held):
        half = held.shape[1] // 2
        one, two = held[:, :half], held[:, half:]
        return (
            jnp.concatenate([one, swap(one, *last[0])]),
            jnp.concatenate([two, swap(two, *last[1])]),
        )

    def join(one, two):
        return (jnp.concatenate([one, swap(one, *last[1]), two, swap(two, *last[0])]),)

    def final(held):
        return (held, swap(held, *last[2]))

    return Chain((block[None],), [far_step(d) for d in far] + [split, join, final])


def scatter_chain(mine, other, far, last):
    def add(left, right):
        return left.astype(F32) + right.astype(F32)

    def first(mine, other):
        total = add(mine, swap(other, *last[2]))
        count, rows = total.shape[0], total.shape[1]
        total = total.reshape((2, 2, count // 4, 2, rows // 2) + total.shape[2:]).astype(BF)
        one, two = total[:, :, :, 0], total[:, :, :, 1]
        return one[0], one[1], two[:, 0], two[:, 1]

    def second(keep_one, send_one, keep_two, send_two):
        one = add(keep_one, swap(send_one, *last[1])).astype(BF)
        two = add(keep_two, swap(send_two, *last[0])).astype(BF)
        return one[0], one[1], two[0], two[1]

    def third(keep_one, send_one, keep_two, send_two):
        one = add(keep_one, swap(send_one, *last[0])).astype(BF)
        two = add(keep_two, swap(send_two, *last[1])).astype(BF)
        both = jnp.concatenate([one, two], axis=1)
        half = both.shape[0] // 2
        return both[:half], both[half:]

    def far_step(dim):
        def step(keep, send):
            total = add(keep, swap(send, *dim))
            half = total.shape[0] // 2
            if half == 0:
                return (total[0],)
            total = total.astype(BF)
            return total[:half], total[half:]

        return step

    return Chain((mine, other), [first, second, third] + [far_step(d) for d in reversed(far)])


def sum_chain(value, dims):
    def step(axis, bits):
        masks = [0]
        for bit in bits:
            masks += [m | 1 << bit for m in masks]
        size = lax.axis_size(axis)

        def run(value):
            others = [lax.ppermute(value, axis, [(i, i ^ m) for i in range(size)]) for m in masks[1:]]
            return (sum(others, value),)

        return run

    return Chain((value,), [step(*d) for d in dims])


def dims_masks(dims):
    masks = []
    for m in range(2 ** len(dims)):
        flip = {"tp": 0, "sp": 0}
        for place, (axis, bit) in enumerate(dims):
            flip[axis] |= ((m >> place) & 1) << bit
        masks.append((flip["tp"], flip["sp"]))
    return masks


def piece_masks(far, last):
    masks = []
    for core in range(2):
        for half in range(2):
            pair = last[:2] if half == 0 else last[1::-1]
            for tp_flip, sp_flip in dims_masks(far + pair):
                masks.append((tp_flip | core << last[2][1], sp_flip, half))
    return masks


def dot(left, right, left_dim, right_dim):
    return lax.dot_general(
        left, right, (((left_dim,), (right_dim,)), ((), ())), preferred_element_type=F32
    )


def norm_rows(operand):
    centred = operand - jnp.mean(operand, axis=-1, keepdims=True)
    inverse = lax.rsqrt(jnp.mean(centred * centred, axis=-1, keepdims=True) + EPSILON)
    return (centred * inverse, inverse)


def norm_back(incoming, normed, inverse):
    first_mean = jnp.mean(incoming, axis=-1, keepdims=True)
    second_mean = jnp.mean(incoming * normed, axis=-1, keepdims=True)
    return inverse * (incoming - first_mean - normed * second_mean)


def params(count=1):
    return pltpu.CompilerParams(
        dimension_semantics=("arbitrary",) * count, vmem_limit_bytes=VMEM_BYTES
    )


def whole(shape):
    zeros = (0,) * len(shape)
    return pl.BlockSpec(shape, lambda g, meta: zeros, pipeline_mode=pl.Buffered(1))


def place_weights(meta, pieces, masks, target):
    if masks is None:
        target[...] = pieces[0][...].reshape(target.shape)
        return
    rows = pieces[0].shape[1]
    count = pieces[0].shape[0]
    for m, (tp_flip, sp_flip, half) in enumerate(masks):
        at = pl.multiple_of((meta[2] ^ sp_flip) * (2 * rows) + half * rows, rows)
        target[meta[1] ^ tp_flip, pl.ds(at, rows), :] = pieces[m // count][m % count]


def split_places(pair):
    count, width = pair.shape[0], pair.shape[3]
    one, two = pair[:, 0], pair[:, 1]
    upper = lax.broadcasted_iota(jnp.int32, one.shape, 1) < 4
    left = jnp.where(upper, one, pltpu.roll(two, 4, 1))
    right = jnp.where(upper, pltpu.roll(one, 4, 1), two)
    return left.reshape(count * 8, width), right.reshape(count * 8, width)


def join_places(left, right):
    count, width = left.shape[0] // 8, left.shape[1]
    left, right = left.reshape(count, 8, width), right.reshape(count, 8, width)
    upper = lax.broadcasted_iota(jnp.int32, left.shape, 1) < 4
    one = jnp.where(upper, left, pltpu.roll(right, 4, 1))
    two = jnp.where(upper, pltpu.roll(left, 4, 1), right)
    return one, two


def forward_kernel(masks, heads, masked, meta, x, hot, mst, key_r, key_c, *refs):
    pieces = refs[: 1 if masks is None else 2]
    x_out, h_out, qkv_out, p_out, o_out, a_out, w, both = refs[len(pieces) :]
    width = x.shape[-1]
    head_tp = heads * HD
    step = pl.program_id(0)
    zipped = len(x.shape) == 4

    @pl.when(step == 0)
    def _():
        place_weights(meta, pieces, masks, w)
        if zipped:
            both[0], both[1] = split_places(x[...].astype(F32))

    def modulation(i):
        return dot(hot[0], mst[:, i * width : (i + 1) * width], 1, 0)

    xin = both[step] if zipped else x[0].astype(F32)
    normed = norm_rows(xin)[0]
    h = (normed * (1.0 + modulation(1)) + modulation(0)).astype(BF)
    h_out[0] = h
    bias = jnp.where(key_r[...] == key_c[...], 0.0, -1e30) if masked else None
    total = None
    for t in range(w.shape[0]):
        proj = dot(h, w[t, :, : 3 * head_tp], 1, 0).astype(BF)
        qkv_out[0, t] = proj
        outs = []
        for j in range(heads):
            q, k, v = (
                proj[:, i * head_tp + j * HD : i * head_tp + (j + 1) * HD] for i in range(3)
            )
            scores = dot(k, q * jnp.asarray(0.125, BF), 1, 1)
            if masked:
                scores = scores + bias
            e = jnp.exp(scores - jnp.max(scores, axis=0, keepdims=True))
            p = (e * (1.0 / jnp.sum(e, axis=0, keepdims=True))).astype(BF)
            p_out[0, t * heads + j] = p
            outs.append(dot(v, p, 0, 0))
        o = jnp.concatenate(outs, axis=0).T.astype(BF)
        o_out[0, t] = o
        part = dot(o, w[t, :, 3 * head_tp :], 1, 1)
        total = part if total is None else total + part
    a_out[0] = total.astype(BF)
    x_new = xin + modulation(2) * total
    if zipped:
        both[step] = x_new

        @pl.when(step == 1)
        def _():
            one, two = join_places(both[0], both[1])
            x_out[:, 0], x_out[:, 1] = one.astype(x_out.dtype), two.astype(x_out.dtype)
    else:
        x_out[...] = x_new.reshape(x_out.shape).astype(x_out.dtype)


def weight_specs(pieces):
    return [whole(p.shape) for p in pieces]


def forward(meta, x, groups, rows, hot, mst, keys, pieces, masks, n_tp, heads, x_shape, out_dtype):
    width = x.shape[-1]
    lanes = 4 * heads * HD
    same = hot.shape[0] == 1
    masked = keys is not None
    zipped = x.ndim == 4
    if keys is None:
        keys = jnp.zeros((rows, 1), jnp.int32), jnp.zeros((1, rows), jnp.int32)

    def out(*shape):
        zeros = (0,) * len(shape)
        return (
            jax.ShapeDtypeStruct((groups,) + shape, BF),
            pl.BlockSpec((1,) + shape, lambda g, meta: (g,) + zeros),
        )

    if zipped:
        x_spec = whole(x.shape)
        x_out = whole(x_shape)
    else:
        x_spec = pl.BlockSpec((1, rows, width), lambda g, meta: (g + meta[0], 0, 0))
        if len(x_shape) == 4:
            x_out = pl.BlockSpec(
                (x_shape[0], 1) + x_shape[2:], lambda g, meta: (0, g, 0, 0)
            )
        else:
            x_out = pl.BlockSpec((1, rows, width), lambda g, meta: (g, 0, 0))
    outs = [
        (jax.ShapeDtypeStruct(x_shape, out_dtype), x_out),
        out(rows, width),
        out(n_tp, rows, 3 * heads * HD),
        out(n_tp * heads, rows, rows),
        out(n_tp, rows, heads * HD),
        out(rows, width),
    ]
    return pl.pallas_call(
        functools.partial(forward_kernel, masks, heads, masked),
        out_shape=[o[0] for o in outs],
        grid_spec=pltpu.PrefetchScalarGridSpec(
            num_scalar_prefetch=1,
            grid=(groups,),
            in_specs=[
                x_spec,
                pl.BlockSpec(
                    (1, rows, hot.shape[2]), lambda g, meta: (0 if same else g, 0, 0)
                ),
                whole(mst.shape),
                whole(keys[0].shape),
                whole(keys[1].shape),
            ]
            + weight_specs(pieces),
            out_specs=[o[1] for o in outs],
            scratch_shapes=[
                pltpu.VMEM((n_tp, width, lanes), BF),
                pltpu.VMEM((groups, rows, width) if zipped else (1, 8, 128), F32),
            ],
        ),
        compiler_params=params(),
        cost_estimate=cost(COSTS[0]),
    )(meta, x, hot, mst, *keys, *pieces)


def backward_kernel(masks, heads, meta, dx, x, hot, hot_t, mst, a, qkv, p, *refs):
    pieces = refs[: 1 if masks is None else 2]
    dx_out, dqkv_out, da_out, dm_out, w, both, grads = refs[len(pieces) :]
    width = x.shape[-1]
    head_tp = heads * HD
    step = pl.program_id(0)
    zipped = len(x.shape) == 4

    @pl.when(step == 0)
    def _():
        place_weights(meta, pieces, masks, w)
        if zipped:
            both[0], both[1] = split_places(x[...].astype(F32))
            grads[0], grads[1] = split_places(dx[...].astype(F32))

    def modulation(i):
        return dot(hot[0], mst[:, i * width : (i + 1) * width], 1, 0)

    if zipped:
        grad = grads[step]
    else:
        grad = dx[...].astype(F32).reshape(x.shape[1:])
    da = (modulation(2) * grad).astype(BF)
    da_out[0] = da
    dh = None
    for t in range(w.shape[0]):
        do = dot(da, w[t, :, 3 * head_tp :], 1, 0).astype(BF)
        got = [[], [], []]
        for j in range(heads):
            q, k, v = (
                qkv[0, t, :, i * head_tp + j * HD : i * head_tp + (j + 1) * HD]
                for i in range(3)
            )
            dop = do[:, j * HD : (j + 1) * HD]
            prob = p[0, t * heads + j]
            dp = dot(v, dop, 1, 1)
            prob32 = prob.astype(F32)
            prod = prob32 * dp
            ds = (prod - prob32 * jnp.sum(prod, axis=0, keepdims=True)).astype(BF)
            got[0].append(dot(k, ds, 0, 0))
            got[1].append(dot(ds, q, 1, 0))
            got[2].append(dot(prob, dop, 1, 0))
        dq = jnp.concatenate(got[0], axis=0).T * 0.125
        dk = jnp.concatenate(got[1], axis=1) * 0.125
        dqkv = jnp.concatenate([dq, dk] + got[2], axis=1).astype(BF)
        dqkv_out[0, t] = dqkv
        part = dot(dqkv, w[t, :, : 3 * head_tp], 1, 1)
        dh = part if dh is None else dh + part
    normed, inverse = norm_rows(both[step] if zipped else x[0].astype(F32))
    dx_new = grad + norm_back(dh * (1.0 + modulation(1)), normed, inverse)
    if zipped:
        grads[step] = dx_new

        @pl.when(step == 1)
        def _():
            one, two = join_places(grads[0], grads[1])
            dx_out[:, 0], dx_out[:, 1] = one.astype(BF), two.astype(BF)
    else:
        dx_out[0] = dx_new.astype(BF)

    def clip_sum(value):
        return dot(hot_t[0], value.astype(BF), 1, 0)

    sums = [clip_sum(dh), clip_sum(dh * normed), clip_sum(grad * a[0].astype(F32))]

    @pl.when(step == 0)
    def _():
        for i in range(3):
            dm_out[:, i * width : (i + 1) * width] = sums[i]

    @pl.when(step > 0)
    def _():
        for i in range(3):
            dm_out[:, i * width : (i + 1) * width] += sums[i]


def backward(meta, dx, x, hot, hot_t, mst, a, qkv, p, pieces, masks, heads):
    groups, n_tp, rows = qkv.shape[:3]
    width = dx.shape[-1]
    zipped = x.ndim == 4
    lanes = 4 * heads * HD
    same = hot.shape[0] == 1
    clips = hot_t.shape[1]

    def blocked(shape, offset=False, fixed=False):
        zeros = (0,) * (len(shape) - 1)
        return pl.BlockSpec(
            (1,) + shape[1:],
            lambda g, meta: (0 if fixed else g + meta[0] if offset else g,) + zeros,
        )

    if zipped:
        dx_spec, x_spec, dx_out, dx_shape = whole(dx.shape), whole(x.shape), whole(x.shape), x.shape
    else:
        x_spec = blocked(x.shape, offset=True)
        dx_shape = (groups, rows, width)
        dx_out = blocked(dx_shape)
        if dx.ndim == 4:
            dx_spec = pl.BlockSpec((dx.shape[0], 1) + dx.shape[2:], lambda g, meta: (0, g, 0, 0))
        else:
            dx_spec = blocked(dx.shape)
    return pl.pallas_call(
        functools.partial(backward_kernel, masks, heads),
        out_shape=[
            jax.ShapeDtypeStruct(dx_shape, BF),
            jax.ShapeDtypeStruct(qkv.shape, BF),
            jax.ShapeDtypeStruct((groups, rows, width), BF),
            jax.ShapeDtypeStruct((clips, 3 * width), F32),
        ],
        grid_spec=pltpu.PrefetchScalarGridSpec(
            num_scalar_prefetch=1,
            grid=(groups,),
            in_specs=[
                dx_spec,
                x_spec,
                blocked(hot.shape, fixed=same),
                blocked(hot_t.shape, fixed=same),
                whole(mst.shape),
                blocked(a.shape),
                blocked(qkv.shape),
                blocked(p.shape),
            ]
            + weight_specs(pieces),
            out_specs=[
                dx_out,
                blocked(qkv.shape),
                blocked((groups, rows, width)),
                pl.BlockSpec((clips, 3 * width), lambda g, meta: (0, 0)),
            ],
            scratch_shapes=[
                pltpu.VMEM((n_tp, width, lanes), BF),
                pltpu.VMEM((groups, rows, width) if zipped else (1, 8, 128), F32),
                pltpu.VMEM((groups, rows, width) if zipped else (1, 8, 128), F32),
            ],
        ),
        compiler_params=params(),
        cost_estimate=cost(COSTS[1]),
    )(meta, dx, x, hot, hot_t, mst, a, qkv, p, *pieces)


def store_blocks(meta, masks, scratch, target):
    count, rows = target.shape[0], target.shape[1]
    for place in range(count):
        at = pl.multiple_of((meta[2] ^ masks[place][1]) * rows, rows)
        target[place] = scratch[pl.ds(at, rows), :]


def tp_of(masks, n_tp, g, meta):
    if masks is None:
        return g
    flips = [masks[i * (len(masks) // n_tp)][0] for i in range(n_tp)]
    flips = flips[n_tp // 2 :] + flips[: n_tp // 2]
    flip = 0
    for i, value in enumerate(flips):
        flip = jnp.where(g == i, value, flip)
    return meta[1] ^ flip


def grads_kernel(masks, meta, h, dqkv, da, o, *refs):
    outs, scratch = refs[:-1], refs[-1]
    groups = h.shape[0]
    wide = dqkv.shape[3]
    first, second = None, None
    for g in range(groups):
        one = dot(h[g], dqkv[g, 0], 0, 0)
        two = dot(da[g], o[g, 0], 0, 0)
        first = one if first is None else first + one
        second = two if second is None else second + two
    if masks is None:
        outs[0][0, :, :wide] = first.astype(BF)
        outs[0][0, :, wide:] = second.astype(BF)
        return
    scratch[:, :wide] = first.astype(BF)
    scratch[:, wide:] = second.astype(BF)
    step = pl.program_id(0)
    half = pl.num_programs(0) // 2

    @pl.when(step < half)
    def _():
        store_blocks(meta, masks, scratch, outs[0].at[0])

    @pl.when(step >= half)
    def _():
        store_blocks(meta, masks, scratch, outs[1].at[0])


def half_specs(n_tp, shape):
    zeros = (0,) * len(shape)
    half = n_tp // 2
    return [
        pl.BlockSpec((1,) + shape, lambda g, meta: (jnp.minimum(g, half - 1),) + zeros),
        pl.BlockSpec((1,) + shape, lambda g, meta: (jnp.maximum(g - half, 0),) + zeros),
    ]


def weight_grads(meta, h, dqkv, da, o, masks, row_sp):
    groups, rows, width = h.shape
    n_tp, wide, narrow = dqkv.shape[1], dqkv.shape[3], o.shape[3]
    lanes = wide + narrow
    if masks is None:
        out_shape = [jax.ShapeDtypeStruct((n_tp, width, lanes), BF)]
        out_specs = [pl.BlockSpec((1, width, lanes), lambda g, meta: (g, 0, 0))]
    else:
        shape = (len(masks) // n_tp, row_sp, lanes)
        out_shape = [jax.ShapeDtypeStruct((n_tp // 2,) + shape, BF)] * 2
        out_specs = half_specs(n_tp, shape)
    at = lambda g, meta: (0, tp_of(masks, n_tp, g, meta), 0, 0)
    return pl.pallas_call(
        functools.partial(grads_kernel, masks),
        out_shape=out_shape,
        grid_spec=pltpu.PrefetchScalarGridSpec(
            num_scalar_prefetch=1,
            grid=(n_tp,),
            in_specs=[
                whole(h.shape),
                pl.BlockSpec((groups, 1, rows, wide), at),
                whole(da.shape),
                pl.BlockSpec((groups, 1, rows, narrow), at),
            ],
            out_specs=out_specs,
            scratch_shapes=[pltpu.VMEM((width, lanes), BF)],
        ),
        compiler_params=params(),
        cost_estimate=cost(COSTS[2]),
    )(meta, h, dqkv, da, o)


GELU_A = 0.7978845608028654
GELU_B = 0.044715


def feed_kernel(masks, last_call, meta, x2, dy, hot, hot_t, mst, up, down, *refs):
    if last_call:
        acc_in, dh_in, out, dx_out, dm_out, *grads, h3, da3, acc, dh, blocks = refs
    else:
        acc, dh, *grads, h3, da3, blocks = refs
    width = x2.shape[1]
    step = pl.program_id(0)

    def modulation(i):
        return dot(hot[...], mst[:, i * width : (i + 1) * width], 1, 0)

    @pl.when(step == 0)
    def _():
        normed = norm_rows(x2[...])[0]
        h3[...] = (normed * (1.0 + modulation(1)) + modulation(0)).astype(BF)
        da3[...] = (modulation(2) * dy[...].astype(F32)).astype(BF)
        if last_call:
            acc[...], dh[...] = acc_in[...], dh_in[...]
        else:
            acc[...] = jnp.zeros_like(acc)
            dh[...] = jnp.zeros_like(dh)

    wu = up[...].reshape(width, -1)
    wd = down[...].reshape(width, -1)
    u = dot(h3[...], wu, 1, 0)
    square = u * u
    th = jnp.tanh(GELU_A * (u + GELU_B * (square * u)))
    g = (0.5 * u * (1.0 + th)).astype(BF)
    slope = 0.5 * (1.0 + th) + (0.5 * GELU_A) * u * (1.0 - th * th) * (
        1.0 + (3.0 * GELU_B) * square
    )
    dg = dot(da3[...], wd, 1, 0)
    du = (dg * slope).astype(BF)
    acc[...] += dot(g, wd, 1, 1)
    dh[...] += dot(du, wu, 1, 1)
    grad_up = dot(h3[...], du, 0, 0).astype(BF)
    grad_down = dot(da3[...], g, 0, 0).astype(BF)
    if masks is None:
        grads[0][0], grads[1][0] = grad_up, grad_down
    else:
        for i, value in enumerate((grad_up, grad_down)):
            blocks[...] = value
            store_blocks(meta, masks, blocks, grads[0].at[0, :, i])

    if last_call:

        @pl.when(step == pl.num_programs(0) - 1)
        def _():
            grad = dy[...].astype(F32)
            a3 = acc[...]
            xin = x2[...]
            normed, inverse = norm_rows(xin)
            out[...] = (xin + modulation(2) * a3).astype(BF)
            dh3 = dh[...]
            dx_out[...] = grad + norm_back(dh3 * (1.0 + modulation(1)), normed, inverse)
            for i, value in enumerate([dh3, dh3 * normed, grad * a3]):
                dm_out[:, i * width : (i + 1) * width] = dot(hot_t[...], value.astype(BF), 1, 0)


def feed_half(meta, x2, dy, hot, hot_t, mst, weights, masks, sums):
    rows, width = x2.shape
    n_tp, n_sp, unused, row_sp, units = weights.shape
    clips = hot_t.shape[0]
    half = n_tp // 2
    last_call = sums is not None
    start = half if last_call else 0
    at = lambda g, meta: tp_of(masks, n_tp, g + start, meta)
    if masks is None:
        blocked = weights.transpose(2, 0, 1, 3, 4).reshape(2, n_tp, width, units)
        up, down = blocked[0], blocked[1]
        specs = [pl.BlockSpec((1, width, units), lambda g, meta: (g + start, 0, 0))] * 2
        grad_shapes = [(half, width, units)] * 2
    else:
        up = down = weights
        specs = [
            pl.BlockSpec(
                (1, n_sp, 1, row_sp, units), lambda g, meta, i=i: (at(g, meta), 0, i, 0, 0)
            )
            for i in range(2)
        ]
        grad_shapes = [(half, n_sp, 2, row_sp, units)]
    zeros = (0,) * (len(grad_shapes[0]) - 1)
    grad_spec = pl.BlockSpec((1,) + grad_shapes[0][1:], lambda g, meta: (g,) + zeros)
    plain = lambda s: pl.BlockSpec(s, lambda g, meta: (0, 0))
    total = pltpu.VMEM((rows, width), F32)
    kept = [pltpu.VMEM((rows, width), BF), pltpu.VMEM((rows, width), BF)]
    if last_call:
        out_types = [((rows, width), BF), ((rows, width), F32), ((clips, 3 * width), F32)]
        scratch = kept + [total, total]
    else:
        out_types = [((rows, width), F32), ((rows, width), F32)]
        scratch = kept
    return pl.pallas_call(
        functools.partial(feed_kernel, masks, last_call),
        out_shape=[jax.ShapeDtypeStruct(*t) for t in out_types]
        + [jax.ShapeDtypeStruct(g, BF) for g in grad_shapes],
        grid_spec=pltpu.PrefetchScalarGridSpec(
            num_scalar_prefetch=1,
            grid=(half,),
            in_specs=[
                whole(x2.shape),
                whole(dy.shape),
                whole(hot.shape),
                whole(hot_t.shape),
                whole(mst.shape),
            ]
            + specs
            + ([whole(x2.shape)] * 2 if last_call else []),
            out_specs=[plain(t[0]) for t in out_types] + [grad_spec] * len(grad_shapes),
            scratch_shapes=scratch + [pltpu.VMEM((width, units), BF)],
        ),
        compiler_params=params(),
        cost_estimate=cost(COSTS[3]),
    )(meta, x2, dy, hot, hot_t, mst, up, down, *(sums or ()))


def shards(
    tokens, condition, clip_ids, w_mod, w_qkv_s, w_o_s, w_qkv_t, w_o_t, w_up, w_down, grad_out
):
    n_tp, n_sp = lax.axis_size("tp"), lax.axis_size("sp")
    devices = n_tp * n_sp
    my_tp, my_sp = lax.axis_index("tp"), lax.axis_index("sp")
    width = tokens.shape[1]
    sp_frames = tokens.shape[0] // PATCHES
    frames = sp_frames // n_tp
    all_frames = sp_frames * n_sp
    places = PATCHES // devices
    per_block = max(1, min(places, BLOCK_ROWS // all_frames))
    blocks = places // per_block
    rows = all_frames * per_block
    clips = condition.shape[0]
    head_tp = w_o_s.shape[0]
    heads = head_tp // HD
    row_sp = w_up.shape[0]
    zipped = (frames, per_block, blocks) == (2, 4, 2)

    sp_bits = bits_of(n_sp)
    tp_bits = bits_of(n_tp)
    far = [("sp", b) for b in reversed(range(1, sp_bits))]
    last = [("sp", 0), ("tp", 1), ("tp", 0)]
    every = [("tp", b) for b in range(tp_bits)] + [("sp", b) for b in range(sp_bits)]
    sp_dims = [("sp", b) for b in range(sp_bits)]
    near = row_sp % 32 == 0

    def pack(w_qkv, w_o):
        flat = w_qkv.transpose(1, 0, 2).reshape(row_sp, -1)
        return jnp.concatenate([flat, w_o.T], axis=1)

    masks = dims_masks(far + last) if near else None

    def scatter(terms):
        if near:
            other, mine = (v.reshape((devices // 2, -1) + v.shape[-1:]) for v in terms)
            return scatter_chain(mine, other, far, last)
        terms = terms[0].reshape((devices, -1) + terms[0].shape[-1:])
        terms = in_device_order(terms, far + last, back=True)
        return Chain((terms,), [lambda v: (cube_scatter(v, far + last),)])

    def attention_grads(mine):
        mine = mine.reshape(row_sp, 4, head_tp)
        return mine[:, :3].transpose(1, 0, 2), mine[:, 3].T

    def gather(block):
        if near:
            return gather_chain(block, far, last)
        dims = far + last

        def run(block):
            full = in_device_order(cube_gather(block, dims), dims)
            return (full.reshape(n_tp, width, -1),)

        return Chain((block,), [run])

    cond_act = jax.nn.silu(condition).astype(BF)
    cond_rows = lax.dynamic_slice_in_dim(cond_act, my_sp * row_sp, row_sp, axis=1)
    modulation = sum_chain(
        jnp.dot(cond_rows, w_mod, preferred_element_type=F32), [(a, [b]) for a, b in sp_dims]
    )
    place = piece_masks(far, last) if near else None
    chain_s = gather(pack(w_qkv_s, w_o_s))
    chain_t = gather(pack(w_qkv_t, w_o_t))

    def hot_of(ids):
        hot = (ids[..., None] == jnp.arange(clips, dtype=jnp.int32)).astype(BF)
        return jnp.concatenate([hot, hot], axis=-1), jnp.swapaxes(hot, -1, -2)

    first = my_sp * sp_frames + my_tp * frames
    ids_s = lax.dynamic_slice_in_dim(clip_ids, first, frames)
    hot_s, hot_s_t = hot_of(jnp.repeat(ids_s[:, None], PATCHES, axis=1))
    ids_t = jnp.repeat(clip_ids, per_block)
    hot_t, hot_t_t = hot_of(ids_t[None])
    hot_f, hot_f_t = hot_of(
        jnp.repeat(clip_ids, places) if zipped else jnp.tile(ids_t, blocks)
    )
    key = ids_t * per_block + jnp.tile(jnp.arange(per_block, dtype=jnp.int32), all_frames)
    keys = key[:, None], key[None, :]
    meta0 = jnp.stack([0 * my_tp, my_tp, my_sp]).astype(jnp.int32)
    meta_s = jnp.stack([my_tp * frames, my_tp, my_sp]).astype(jnp.int32)

    def exchange(value):
        return lax.all_to_all(value, ("sp", "tp"), 0, 0, tiled=True)

    def to_places(value):
        if zipped:
            return exchange(value)
        split = value.reshape(frames, devices, blocks, per_block, width).transpose(1, 2, 0, 3, 4)
        return exchange(split).transpose(1, 0, 2, 3, 4).reshape(blocks, rows, width)

    def to_frames(value):
        if zipped:
            return exchange(value)
        split = value.reshape(blocks, devices, frames, per_block, width).transpose(1, 0, 2, 3, 4)
        return exchange(split).transpose(2, 0, 1, 3, 4).reshape(frames, PATCHES, width)

    def input_to_places(value):
        split = value.reshape(sp_frames, n_sp, n_tp, places, width)
        split = lax.dynamic_slice_in_dim(split, my_tp, 1, axis=2)[:, :, 0].transpose(1, 0, 2, 3)
        got = lax.all_to_all(split, "sp", 0, 0, tiled=True)
        if not zipped:
            got = got.reshape(all_frames, blocks, per_block, width).transpose(1, 0, 2, 3)
        return got.reshape(blocks * rows, width)

    def split_output(value):
        if not zipped:
            value = value.reshape(blocks, all_frames, per_block, width).transpose(1, 0, 2, 3)
        return lax.all_to_all(
            value.reshape(n_sp, sp_frames, places, width), "sp", 0, 0, tiled=True
        )

    feed_in = w_up, w_down
    for step in range(max(5, len(modulation.steps))):
        chain_s.go()
        modulation.go()
        if step in (2, 3, 4):
            chain_t.go()
        if step == FEED_STEP:
            feed_in = stage([chain_s, chain_t, modulation], *feed_in)
        else:
            stage([chain_s, chain_t, modulation])
    feed = lax.all_gather(jnp.stack([feed_in[0], feed_in[1].T]), ("tp", "sp"), axis=0)
    feed = feed.reshape(n_tp, n_sp, 2, row_sp, -1)
    (modulation,) = modulation.state
    coarse = lax.reduce_precision(modulation, 8, 7)
    mst = jnp.concatenate([coarse, modulation - coarse]).astype(BF)
    mst_s, mst_t, mst_f = (mst[:, i * 3 * width : (i + 1) * 3 * width] for i in range(3))


    own = tokens.reshape(sp_frames, PATCHES, width)
    x1_shape = (devices, frames, places, width) if zipped else (frames, PATCHES, width)
    x1_frames, h1, qkv1, p1, o1, a1 = forward(
        meta_s, own, frames, PATCHES, hot_s, mst_s, None, chain_s.state, place, n_tp, heads,
        x1_shape, BF,
    )
    chain_t.go()
    x1 = to_places(x1_frames)
    x1 = stage([chain_t], x1)
    chain_t.go()
    x1, grad_in = stage([chain_t], x1, grad_out)
    grad_rows = input_to_places(grad_in)
    x2, h2, qkv2, p2, o2, a2 = forward(
        meta0, x1, blocks, rows, hot_t, mst_t, keys, chain_t.state, place, n_tp, heads,
        x1.shape, F32,
    )

    feed_args = x2.reshape(blocks * rows, width), grad_rows, hot_f, hot_f_t, mst_f, feed, masks
    if near:
        *sums, far_terms = feed_half(meta0, *feed_args, None)
        block_out, dx2, dm_f, near_terms = feed_half(meta0, *feed_args, sums)
        out_f = scatter([far_terms, near_terms])
        out_f.go()
        dx2, block_out = stage([out_f], dx2, block_out)
    else:
        *sums, up_one, down_one = feed_half(meta0, *feed_args, None)
        block_out, dx2, dm_f, up_two, down_two = feed_half(meta0, *feed_args, sums)
        pair = [jnp.concatenate(p) for p in ((up_one, up_two), (down_one, down_two))]
        pair = [scatter([terms]).run()[0] for terms in pair]
        out_f = Chain((jnp.concatenate(pair),), [])

    out_f.go()
    block_out = split_output(block_out)
    dx1, dqkv2, da2, dm_t = backward(
        meta0, dx2.reshape(x2.shape), x1, hot_t, hot_t_t, mst_t, a2, qkv2, p2,
        chain_t.state, place, heads,
    )
    dx1_frames = to_frames(dx1)
    dqkv2, block_out = stage([out_f], dqkv2, block_out)
    out_f.go()
    terms_t = weight_grads(meta0, h2, dqkv2, da2, o2, masks, row_sp)
    all_out = lax.all_gather(block_out, "tp", axis=0)
    dx1_frames, terms_t = stage([out_f], dx1_frames, terms_t)

    out_t = scatter(terms_t)
    out_t.go()
    out_f.go()
    dx0, dqkv1, da1, dm_s = backward(
        meta_s, dx1_frames, own, hot_s, hot_s_t, mst_s, a1, qkv1, p1, chain_s.state, place, heads
    )
    dx0, dqkv1, dm_s = stage([out_t, out_f], dx0, dqkv1, dm_s)
    wide = [("sp", list(range(1, sp_bits)))] if near else [("sp", [b]) for a, b in far]
    dm = sum_chain(
        jnp.concatenate([dm_s, dm_t, dm_f], axis=-1),
        [("tp", list(range(tp_bits)))] + [("sp", [b]) for b in range(sp_bits)],
    )
    grad_tokens = lax.all_gather(dx0.reshape(-1, width), "tp", axis=0, tiled=True)
    out_t.go()
    out_f.go()
    dm.go()
    terms_s = weight_grads(meta0, h1, dqkv1, da1, o1, masks, row_sp)
    terms_s, all_out = stage([out_t, out_f, dm], terms_s, all_out)
    out_s = scatter(terms_s)

    def condition_part(low):
        mine = jnp.dot(low, w_mod.T, preferred_element_type=F32)
        spot = jnp.arange(n_sp)[:, None, None] == my_sp
        return sum_chain(jnp.where(spot, mine[None], 0.0), [("sp", [0])] + wide)

    done = {}
    part, step = None, 0
    chains = [out_s, out_t, out_f, dm]
    while part is None or any(c.steps for c in chains + [part]):
        out_s.go()
        if out_t.steps:
            out_t.go()
        elif "t" not in done:
            done["t"] = attention_grads(out_t.state[0])
        if out_f.steps:
            out_f.go()
        elif "f" not in done:
            done["f"] = out_f.state[0][:row_sp], out_f.state[0][row_sp:].T
        if step == 2:
            done["out"] = all_out.transpose(2, 1, 0, 3, 4).reshape(-1, width)
        if dm.steps:
            dm.go()
        elif part is None:
            low = dm.state[0].astype(BF)
            part = condition_part(low)
            done["mod"] = jnp.dot(cond_rows.T, low, preferred_element_type=F32)
        if part is not None:
            part.go()
        if step == TOKENS_STEP:
            done["tokens"] = grad_tokens
        names = sorted(done)
        waits = chains + ([part] if part is not None else [])
        values = stage(waits, [done[n] for n in names])
        done = dict(zip(names, values))
        step += 1
    grad_act = part.state[0].transpose(1, 0, 2).reshape(clips, width)
    unused, silu_pull = jax.vjp(jax.nn.silu, condition)
    grad_condition = silu_pull(grad_act)[0]
    if "t" not in done:
        done["t"] = attention_grads(out_t.state[0])
    sum_qt, sum_ot = done["t"]
    sum_qs, sum_os = attention_grads(out_s.state[0])
    return (
        done["out"],
        done["tokens"],
        grad_condition,
        done["mod"],
        sum_qs,
        sum_os,
        sum_qt,
        sum_ot,
        *done["f"],
    )


def solution(mesh):
    placed = (
        P("sp", None),
        P(),
        P(),
        P("sp", None),
        P(None, "sp", "tp"),
        P("tp", "sp"),
        P(None, "sp", "tp"),
        P("tp", "sp"),
        P("sp", "tp"),
        P("tp", "sp"),
        P("sp", None),
    )
    return jax.shard_map(
        shards,
        mesh=mesh,
        in_specs=placed,
        out_specs=(
            P("sp", None),
            P("sp", None),
            P(),
            P("sp", None),
            P(None, "sp", "tp"),
            P("tp", "sp"),
            P(None, "sp", "tp"),
            P("tp", "sp"),
            P("sp", "tp"),
            P("tp", "sp"),
        ),
        check_vma=False,
    )
```

time: 538 us -> 453 us (0.84)
  local copies, waits for them, and re-layouts: 83.3 us -> 31.9 us
  waiting for transfers between devices: 196 us -> 160 us
  blocking collectives: 24 us -> 0 us
  other arithmetic: 23.6 us -> 38.3 us
  Pallas kernels: 114 us -> 124 us
    ppermute x0 -> x13, waiting for transfers between devices: none -> 42.9 us  [run(): lax.ppermute(value, axis, [(i, i ^ m) for i in range(size)])]
    all_to_all x3 -> x4, waiting for transfers between devices: 35.2 us -> 2.92 us  [the longest x2 1.95 us: exchange(): return lax.all_to_all(value, ('sp', 'tp'), 0, 0, tiled=True)]
    ppermute x36 -> x35, waiting for transfers between devices: 145 us -> 114 us  [swap(): return lax.ppermute(value, axis, [(i, i ^ 1 << bit) for i in range(size)])]
    reshape x14 -> x5, local copies, waits for them, and re-layouts: 31.5 us -> 1.6 us  [the longest x2 0.95 us: pack(): flat = w_qkv.transpose(1, 0, 2).reshape(row_sp, -1)]
    all_to_all x1 -> x0, blocking collectives: 24 us -> none  [places_to_output(): got = lax.all_to_all(split, 'sp', 0, 0, tiled=True)]
    ppermute x36 -> x35, starting transfers between devices: 54.4 us -> 31.8 us  [swap(): return lax.ppermute(value, axis, [(i, i ^ 1 << bit) for i in range(size)])]
    ppermute x0 -> x13, starting transfers between devices: none -> 17.9 us  [run(): lax.ppermute(value, axis, [(i, i ^ m) for i in range(size)])]
    reduce_scatter x1 -> x0, waiting for transfers between devices: 16.3 us -> none  [shards(): lax.psum_scatter(feed_grad.reshape(devices, 2, row_sp, -1), ('tp', 'sp'),...]
  transfers between devices with their start and end apart: 43 -> 55, of which waited for: 18 -> 27; matrix products, arithmetic and copies ran while one was open for 17% -> 11% of each run, Pallas kernels for 17% -> 25%
where the time goes in v3:
time: 453 us; the launch traced here: 444 us
  waiting for transfers between devices  160 us (35%)
  Pallas kernels  124 us (27%)
  starting transfers between devices  70.8 us (16%)
  other arithmetic  38.3 us (8%)
  local copies, waits for them, and re-layouts  31.9 us (7%)
  between operations  14.9 us (3%)
    ppermute x35, waiting for transfers between devices, swap(): return lax.ppermute(value, axis, [(i, i ^ 1 << bit) for i in range(size)])  114 us
    ppermute x13, waiting for transfers between devices, run(): lax.ppermute(value, axis, [(i, i ^ m) for i in range(size)])  42.9 us
    pallas_call x2, Pallas kernels, backward(): pl.pallas_call(functools.partial(backward_kernel, masks, heads), out_shap...  41 us
    pallas_call x2, Pallas kernels, forward(): pl.pallas_call(functools.partial(forward_kernel, masks, heads, masked), o...  35.6 us
    ppermute x35, starting transfers between devices, swap(): return lax.ppermute(value, axis, [(i, i ^ 1 << bit) for i in range(size)])  31.8 us
    pallas_call x2, Pallas kernels, feed_half(): pl.pallas_call(functools.partial(feed_kernel, masks, last_call), out_shap...  30.7 us
    ppermute x13, starting transfers between devices, run(): lax.ppermute(value, axis, [(i, i ^ m) for i in range(size)])  17.9 us
    pallas_call x2, Pallas kernels, weight_grads(): pl.pallas_call(functools.partial(grads_kernel, masks), out_shape=out_shap...  17 us
  transfers between devices with their start and end apart: 55, of which 27 were waited for; matrix products, arithmetic and copies ran while one was open for 11% of the time, Pallas kernels for 25%

profile of v3, /device:TPU:0, one launch (start us, length us, event | category | flops | bytes accessed | tf_op | source)
XLA Modules:
  0.0 444.1 jit_solution(2481155807786016065)
XLA Ops:
  26.1 8.5 %collective-permute-done.3 = f32[4,6912]{1,0:T(4,128)S(1)} collective-permute-done((f32[4,6912]{1,0:T(4,128)S(1)}, f32[4,6912]{1,0:T(4,128)S(1)}, u32[]{:S(2)}, u32[]{:S(2)}) %collective-permute-start.3) | collective-permute-done | bytes 110624 | tf_op jit(solution)/shard_map/ppermute | solution.py:175
  39.8 9.2 %collective-permute-done.7 = f32[4,6912]{1,0:T(4,128)S(1)} collective-permute-done((f32[4,6912]{1,0:T(4,128)S(1)}, f32[4,6912]{1,0:T(4,128)S(1)}, u32[]{:S(2)}, u32[]{:S(2)}) %collective-permute-start.7) | collective-permute-done | bytes 110624 | tf_op jit(solution)/shard_map/ppermute | solution.py:175
  54.3 6.6 %collective-permute-done.10 = bf16[2,96,768]{2,1,0:T(8,128)(2,1)S(1)} collective-permute-done((bf16[2,96,768]{2,1,0:T(8,128)(2,1)S(1)}, bf16[2,96,768]{2,1,0:T(8,128)(2,1)S(1)}, u32[]{:S(2)}, u32[]{:S(2)}) %collective-permute-start.10) | collective-permute-done | bytes 294944 | tf_op jit(solution)/shard_map/ppermute | solution.py:28
  61.8 7.0 %collective-permute-done.8 = bf16[8,48,768]{2,1,0:T(8,128)(2,1)S(1)} collective-permute-done((bf16[8,48,768]{2,1,0:T(8,128)(2,1)}, bf16[8,48,768]{2,1,0:T(8,128)(2,1)S(1)}, u32[]{:S(2)}, u32[]{:S(2)}) %collective-permute-start.8) | collective-permute-done | bytes 589856 | tf_op jit(solution)/shard_map/ppermute | solution.py:28
  76.6 8.6 %collective-permute-done.13 = bf16[4,48,768]{2,1,0:T(8,128)(2,1)} collective-permute-done((bf16[4,48,768]{2,1,0:T(8,128)(2,1)}, bf16[4,48,768]{2,1,0:T(8,128)(2,1)}, u32[]{:S(2)}, u32[]{:S(2)}) %collective-permute-start.13) | collective-permute-done | bytes 294944 | tf_op jit(solution)/shard_map/ppermute | solution.py:28
  91.0 17.3 %shard_map.186 = (bf16[32,2,8,768]{3,2,1,0:T(8,128)(2,1)S(1)}, bf16[2,256,768]{2,1,0:T(8,128)(2,1)S(1)}, bf16[2,4,256,576]{3,2,1,0:T(8,128)(2,1)}, bf16[2,12,256...) custom-call(s32[3]{0:T(128)S(1)} %add_add_fusion.3.meta, ...), custom_call_target="tpu_custom_call" | custom-call | flops 20000000000 | bytes 1024 | tf_op jit(solution)/shard_map/pallas_call | solution.py:355
  110.2 7.2 %all-to-all-start = ((bf16[32,2,8,768]{3,2,1,0:T(8,128)(2,1)}), bf16[32,2,8,768]{3,2,1,0:T(8,128)(2,1)}, u32[]{:S(2)}, u32[]{:S(2)}) async-start(bf16[32,2,8,768]{3,2,1,0:T(8,128)(2,1)} %copy-done.2), calls=%async_computation | async-start | bytes 1572864 | tf_op jit(solution)/shard_map/all_to_all | solution.py:813
  120.6 24.5 %collective-permute-done.14 = bf16[8,48,768]{2,1,0:T(8,128)(2,1)S(1)} collective-permute-done((bf16[8,48,768]{2,1,0:T(8,128)(2,1)}, bf16[8,48,768]{2,1,0:T(8,128)(2,1)S(1)}, u32[]{:S(2)}, u32[]{:S(2)}) %collective-permute-start.14) | collective-permute-done | bytes 589856 | tf_op jit(solution)/shard_map/ppermute | solution.py:28
  162.0 18.2 %shard_map.187 = (f32[32,2,8,768]{3,2,1,0:T(8,128)}, bf16[2,256,768]{2,1,0:T(8,128)(2,1)S(1)}, bf16[2,4,256,576]{3,2,1,0:T(8,128)(2,1)}, bf16[2,12,256,256]{3,2,...) custom-call(s32[3]{0:T(128)S(1)} %add_add_fusion.2.meta, ...), custom_call_target="tpu_custom_call" | custom-call | flops 20000000000 | bytes 1024 | tf_op jit(solution)/shard_map/pallas_call | solution.py:355
  181.2 13.8 %shard_map.188 = (f32[512,768]{1,0:T(8,128)}, f32[512,768]{1,0:T(8,128)}, bf16[2,8,2,96,768]{4,3,2,1,0:T(8,128)(2,1)}) custom-call(s32[3]{0:T(128)S(1)} %add_add_fusion.2.meta, f32[512,768]{1,0:T(8,128)} %bitcast.154, bf16[512,768]{1,0:T(8,128)(2,1)S(1)} %bitcast.142, bf16[512,8]{1,0:T(8,128)(2,1)S(1)} %concatenate.82.hot, bf16[4,512]{1,0:T(4,128)(2,1)S(1)} %fusion.15.hot_t, ...), custom_call_target="tpu_custom_call" | custom-call | flops 1000000000 | bytes 1024 | tf_op jit(solution)/shard_map/pallas_call | solution.py:705
  195.2 16.9 %shard_map.189 = (bf16[512,768]{1,0:T(8,128)(2,1)}, f32[512,768]{1,0:T(8,128)}, f32[4,2304]{1,0:T(4,128)S(1)}, bf16[2,8,2,96,768]{4,3,2,1,0:T(8,128)(2,1)}) custom-call(s32[3]{0:T(128)S(1)} %add_add_fusion.2.meta, f32[512,768]{1,0:T(8,128)} %bitcast.155, bf16[512,768]{1,0:T(8,128)(2,1)S(1)} %bitcast.143, bf16[512,8]{1,0:T(8,128)(2,1)S(1)} %concatenate.82.hot, ...), custom_call_target="tpu_custom_call" | custom-call | flops 1000000000 | bytes 1024 | tf_op jit(solution)/shard_map/pallas_call | solution.py:705
  227.0 21.0 %shard_map.190 = (bf16[32,2,8,768]{3,2,1,0:T(8,128)(2,1)}, bf16[2,4,256,576]{3,2,1,0:T(8,128)(2,1)}, bf16[2,256,768]{2,1,0:T(8,128)(2,1)S(1)}, f32[4,2304]{1,0:T(4,128)S(1)}) custom-call(s32[3]{0:T(128)S(1)} %add_add_fusion.2.meta, f32[32,2,8,768]{3,2,1,0:T(8,128)} %bitcast.179, bf16[32,2,8,768]{3,2,1,0:T(8,128)(2,1)} %all-to-all-done.x, ...), custom_call_target="tpu_custom_call" | custom-call | flops 20000000000 | bytes 1024 | tf_op jit(solution)/shard_map/pallas_call | solution.py:483
  247.9 6.6 %collective-permute-done.19 = bf16[2,4,96,768]{3,2,1,0:T(8,128)(2,1)} collective-permute-done((bf16[2,4,96,768]{3,2,1,0:T(8,128)(2,1)}, bf16[2,4,96,768]{3,2,1,0:T(8,128)(2,1)}, u32[]{:S(2)}, u32[]{:S(2)}) %collective-permute-start.19) | collective-permute-done | bytes 1179680 | tf_op jit(solution)/shard_map/ppermute | solution.py:28
  260.0 5.4 %all-to-all-start.3 = ((bf16[32,2,8,768]{3,2,1,0:T(8,128)(2,1)}), bf16[32,2,8,768]{3,2,1,0:T(8,128)(2,1)}, u32[]{:S(2)}, u32[]{:S(2)}) async-start(bf16[32,2,8,768]{3,2,1,0:T(8,128)(2,1)} %get-tuple-element.194), calls=%async_computation.3 | async-start | bytes 1572864 | tf_op jit(solution)/shard_map/all_to_all | solution.py:813
  268.8 8.5 %shard_map.191 = (bf16[2,8,96,768]{3,2,1,0:T(8,128)(2,1)}, bf16[2,8,96,768]{3,2,1,0:T(8,128)(2,1)}) custom-call(s32[3]{0:T(128)S(1)} %add_add_fusion.2.meta, bf16[2,256,768]{2,1,0:T(8,128)(2,1)S(1)} %copy-done.16, bf16[2,4,256,576]{3,2,1,0:T(8,128)(2,1)} %get-tuple-element.196.dqkv, bf16[2,256,768]{2,1,0:T(8,128)(2,1)S(1)} %copy-done.12, ...), custom_call_target="tpu_custom_call" | custom-call | flops 20000000000 | bytes 1024 | tf_op jit(solution)/shard_map/pallas_call | solution.py:589
  277.2 12.1 %collective-permute-done.20 = bf16[4,96,768]{2,1,0:T(8,128)(2,1)} collective-permute-done((bf16[4,96,768]{2,1,0:T(8,128)(2,1)}, bf16[4,96,768]{2,1,0:T(8,128)(2,1)}, u32[]{:S(2)}, u32[]{:S(2)}) %collective-permute-start.20) | collective-permute-done | bytes 589856 | tf_op jit(solution)/shard_map/ppermute | solution.py:28
  290.5 7.6 %collective-permute-done.21 = bf16[4,96,768]{2,1,0:T(8,128)(2,1)} collective-permute-done((bf16[4,96,768]{2,1,0:T(8,128)(2,1)}, bf16[4,96,768]{2,1,0:T(8,128)(2,1)}, u32[]{:S(2)}, u32[]{:S(2)}) %collective-permute-start.21) | collective-permute-done | bytes 589856 | tf_op jit(solution)/shard_map/ppermute | solution.py:28
  301.5 20.0 %shard_map.192 = (bf16[2,256,768]{2,1,0:T(8,128)(2,1)}, bf16[2,4,256,576]{3,2,1,0:T(8,128)(2,1)}, bf16[2,256,768]{2,1,0:T(8,128)(2,1)S(1)}, f32[4,2304]{1,0:T(4,128)S(1)}) custom-call(s32[3]{0:T(128)S(1)} %copy-done.9, bf16[32,2,8,768]{3,2,1,0:T(8,128)(2,1)} %all-to-all-done.3.dx, bf16[8,256,768]{2,1,0:T(8,128)(2,1)} %bitcast.176, ...), custom_call_target="tpu_custom_call" | custom-call | flops 20000000000 | bytes 1024 | tf_op jit(solution)/shard_map/pallas_call | solution.py:483
  330.7 8.5 %shard_map.193 = (bf16[2,8,96,768]{3,2,1,0:T(8,128)(2,1)}, bf16[2,8,96,768]{3,2,1,0:T(8,128)(2,1)}) custom-call(s32[3]{0:T(128)S(1)} %add_add_fusion.2.meta, bf16[2,256,768]{2,1,0:T(8,128)(2,1)S(1)} %copy-done.14, bf16[2,4,256,576]{3,2,1,0:T(8,128)(2,1)} %get-tuple-element.222.dqkv, bf16[2,256,768]{2,1,0:T(8,128)(2,1)S(1)} %get-tuple-element.223.da, ...), custom_call_target="tpu_custom_call" | custom-call | flops 20000000000 | bytes 1024 | tf_op jit(solution)/shard_map/pallas_call | solution.py:589
  344.8 9.9 %collective-permute-done.24 = bf16[2,4,48,768]{3,2,1,0:T(8,128)(2,1)S(1)} collective-permute-done((bf16[2,4,48,768]{3,2,1,0:T(8,128)(2,1)S(1)}, bf16[2,4,48,768]{3,2,1,0:T(8,128)(2,1)S(1)}, u32[]{:S(2)}, u32[]{:S(2)}) %collective-permute-start.24) | collective-permute-done | bytes 589856 | tf_op jit(solution)/shard_map/ppermute | solution.py:28
  358.3 8.5 %collective-permute-done.33 = f32[4,6912]{1,0:T(4,128)S(1)} collective-permute-done((f32[4,6912]{1,0:T(4,128)S(1)}, f32[4,6912]{1,0:T(4,128)S(1)}, u32[]{:S(2)}, u32[]{:S(2)}) %collective-permute-start.33) | collective-permute-done | bytes 110624 | tf_op jit(solution)/shard_map/ppermute | solution.py:175
  374.9 5.9 %collective-permute-done.37 = f32[4,6912]{1,0:T(4,128)S(1)} collective-permute-done((f32[4,6912]{1,0:T(4,128)S(1)}, f32[4,6912]{1,0:T(4,128)S(1)}, u32[]{:S(2)}, u32[]{:S(2)}) %collective-permute-start.37) | collective-permute-done | bytes 110624 | tf_op jit(solution)/shard_map/ppermute | solution.py:175
  386.4 9.0 %collective-permute-done.34 = bf16[2,4,48,768]{3,2,1,0:T(8,128)(2,1)S(1)} collective-permute-done((bf16[2,4,48,768]{3,2,1,0:T(8,128)(2,1)S(1)}, bf16[2,4,48,768]{3,2,1,0:T(8,128)(2,1)S(1)}, u32[]{:S(2)}, u32[]{:S(2)}) %collective-permute-start.34) | collective-permute-done | bytes 589856 | tf_op jit(solution)/shard_map/ppermute | solution.py:28
  401.5 6.9 %collective-permute-done.41 = f32[4,6912]{1,0:T(4,128)S(1)} collective-permute-done((f32[4,6912]{1,0:T(4,128)S(1)}, f32[4,6912]{1,0:T(4,128)S(1)}, u32[]{:S(2)}, u32[]{:S(2)}) %collective-permute-start.41) | collective-permute-done | bytes 110624 | tf_op jit(solution)/shard_map/ppermute | solution.py:175
  (289 shorter events, 161.6 us)
Async XLA Ops:
  7.2 174.0 %all-gather.8.cloned.1.call-start = ((), (), s32[]{:S(2)}) async-start(), calls=%async_computation.5 | async-start | bytes 9732096 | tf_op jit(solution)/shard_map/all_gather | solution.py:852
  52.2 16.6 %collective-permute-start.8 = (bf16[8,48,768]{2,1,0:T(8,128)(2,1)}, bf16[8,48,768]{2,1,0:T(8,128)(2,1)S(1)}, u32[]{:S(2)}, u32[]{:S(2)}) collective-permute-start(bf16[8,48,768]{2,1,0:T(8,128)(2,1)} %pad_maximum_fusion.4), channel_id=1, source_target_pairs={{0,16},{8,24},{16,0},{24,8},{1,17},{9,25},{17,1},{25,9},{2,18},{10... | collective-permute-start | bytes 1769480 | tf_op jit(solution)/shard_map/ppermute | solution.py:28
  52.8 16.2 %collective-permute-start.9 = (bf16[8,48,768]{2,1,0:T(8,128)(2,1)}, bf16[8,48,768]{2,1,0:T(8,128)(2,1)S(1)}, u32[]{:S(2)}, u32[]{:S(2)}) collective-permute-start(bf16[8,48,768]{2,1,0:T(8,128)(2,1)} %pad_maximum_fusion.5), channel_id=1, source_target_pairs={{0,1},{1,0},{2,3},{3,2},{4,5},{5,4},{6,7},{7,6},{8,9},{9,8},{10,11... | collective-permute-start | bytes 1769480 | tf_op jit(solution)/shard_map/ppermute | solution.py:28
  72.1 17.3 %collective-permute-start.11 = (bf16[32,48,768]{2,1,0:T(8,128)(2,1)}, bf16[32,48,768]{2,1,0:T(8,128)(2,1)}, u32[]{:S(2)}, u32[]{:S(2)}) collective-permute-start(bf16[32,48,768]{2,1,0:T(8,128)(2,1)} %pad_maximum_fusion.refs_0_), channel_id=1, source_target_pairs={{0,8},{8,0},{16,24},{24,16},{1,9},{9,1},{17,25},{25,17},{2,10},{10... | collective-permute-start | bytes 7077896 | tf_op jit(solution)/shard_map/ppermute | solution.py:28
  110.2 40.2 %all-to-all-start = ((bf16[32,2,8,768]{3,2,1,0:T(8,128)(2,1)}), bf16[32,2,8,768]{3,2,1,0:T(8,128)(2,1)}, u32[]{:S(2)}, u32[]{:S(2)}) async-start(bf16[32,2,8,768]{3,2,1,0:T(8,128)(2,1)} %copy-done.2), calls=%async_computation | async-start | bytes 1572864 | tf_op jit(solution)/shard_map/all_to_all | solution.py:813
  117.4 27.7 %collective-permute-start.14 = (bf16[8,48,768]{2,1,0:T(8,128)(2,1)}, bf16[8,48,768]{2,1,0:T(8,128)(2,1)S(1)}, u32[]{:S(2)}, u32[]{:S(2)}) collective-permute-start(bf16[8,48,768]{2,1,0:T(8,128)(2,1)} %pad_maximum_fusion.7), channel_id=1, source_target_pairs={{0,16},{8,24},{16,0},{24,8},{1,17},{9,25},{17,1},{25,9},{2,18},{10... | collective-permute-start | bytes 1769480 | tf_op jit(solution)/shard_map/ppermute | solution.py:28
  119.1 26.2 %collective-permute-start.15 = (bf16[8,48,768]{2,1,0:T(8,128)(2,1)}, bf16[8,48,768]{2,1,0:T(8,128)(2,1)S(1)}, u32[]{:S(2)}, u32[]{:S(2)}) collective-permute-start(bf16[8,48,768]{2,1,0:T(8,128)(2,1)} %pad_maximum_fusion.8), channel_id=1, source_target_pairs={{0,1},{1,0},{2,3},{3,2},{4,5},{5,4},{6,7},{7,6},{8,9},{9,8},{10,11... | collective-permute-start | bytes 1769480 | tf_op jit(solution)/shard_map/ppermute | solution.py:28
  156.8 24.4 %all-to-all-start.1 = ((bf16[8,8,8,768]{3,2,1,0:T(8,128)(2,1)}), bf16[8,8,8,768]{3,2,1,0:T(8,128)(2,1)S(1)}, u32[]{:S(2)}, u32[]{:S(2)}) async-start(bf16[8,8,8,768]{3,2,1,0:T(8,128)(2,1)} %copy_bitcast_fusion), calls=%async_computation.1 | async-start | bytes 1572864 | tf_op jit(solution)/shard_map/all_to_all | solution.py:830
  195.0 17.0 %collective-permute-start.17 = (bf16[16,192,768]{2,1,0:T(8,128)(2,1)}, bf16[16,192,768]{2,1,0:T(8,128)(2,1)S(1)}, u32[]{:S(2)}, u32[]{:S(2)}) collective-permute-start(bf16[16,192,768]{2,1,0:T(8,128)(2,1)} %bitcast.174), channel_id=1, source_target_pairs={{0,8},{8,0},{16,24},{24,16},{1,9},{9,1},{17,25},{25,17},{2,10},{10... | collective-permute-start | bytes 14155784 | tf_op jit(solution)/shard_map/ppermute | solution.py:28
  219.1 35.4 %collective-permute-start.19 = (bf16[2,4,96,768]{3,2,1,0:T(8,128)(2,1)}, bf16[2,4,96,768]{3,2,1,0:T(8,128)(2,1)}, u32[]{:S(2)}, u32[]{:S(2)}) collective-permute-start(bf16[2,4,96,768]{3,2,1,0:T(8,128)(2,1)} %get-tuple-element.183), channel_id=1, source_target_pairs={{0,1},{1,0},{2,3},{3,2},{4,5},{5,4},{6,7},{7,6},{8,9},{9,8},{10,11... | collective-permute-start | bytes 3538952 | tf_op jit(solution)/shard_map/ppermute | solution.py:28
  220.6 36.7 %collective-permute-start.18 = (bf16[2,4,96,768]{3,2,1,0:T(8,128)(2,1)}, bf16[2,4,96,768]{3,2,1,0:T(8,128)(2,1)}, u32[]{:S(2)}, u32[]{:S(2)}) collective-permute-start(bf16[2,4,96,768]{3,2,1,0:T(8,128)(2,1)} %get-tuple-element.181), channel_id=1, source_target_pairs={{0,16},{8,24},{16,0},{24,8},{1,17},{9,25},{17,1},{25,9},{2,18},{10... | collective-permute-start | bytes 3538952 | tf_op jit(solution)/shard_map/ppermute | solution.py:28
  222.2 37.7 %all-to-all-start.2 = ((bf16[8,8,8,768]{3,2,1,0:T(8,128)(2,1)}), bf16[8,8,8,768]{3,2,1,0:T(8,128)(2,1)}, u32[]{:S(2)}, u32[]{:S(2)}) async-start(bf16[8,8,8,768]{3,2,1,0:T(8,128)(2,1)} %bitcast.35), calls=%async_computation.2 | async-start | bytes 1572864 | tf_op jit(solution)/shard_map/all_to_all | solution.py:838
  260.0 40.3 %all-to-all-start.3 = ((bf16[32,2,8,768]{3,2,1,0:T(8,128)(2,1)}), bf16[32,2,8,768]{3,2,1,0:T(8,128)(2,1)}, u32[]{:S(2)}, u32[]{:S(2)}) async-start(bf16[32,2,8,768]{3,2,1,0:T(8,128)(2,1)} %get-tuple-element.194), calls=%async_computation.3 | async-start | bytes 1572864 | tf_op jit(solution)/shard_map/all_to_all | solution.py:813
  265.4 89.5 %all-gather.10.cloned.1.call-start = ((), (), s32[]{:S(2)}) async-start(), calls=%async_computation.6 | async-start | bytes 3932160 | tf_op jit(solution)/shard_map/all_gather | solution.py:901
  265.4 23.9 %collective-permute-start.20 = (bf16[4,96,768]{2,1,0:T(8,128)(2,1)}, bf16[4,96,768]{2,1,0:T(8,128)(2,1)}, u32[]{:S(2)}, u32[]{:S(2)}) collective-permute-start(bf16[4,96,768]{2,1,0:T(8,128)(2,1)} %get-tuple-element.191), channel_id=1, source_target_pairs={{0,1},{1,0},{2,3},{3,2},{4,5},{5,4},{6,7},{7,6},{8,9},{9,8},{10,11... | collective-permute-start | bytes 1769480 | tf_op jit(solution)/shard_map/ppermute | solution.py:28
  267.2 31.0 %collective-permute-start.21 = (bf16[4,96,768]{2,1,0:T(8,128)(2,1)}, bf16[4,96,768]{2,1,0:T(8,128)(2,1)}, u32[]{:S(2)}, u32[]{:S(2)}) collective-permute-start(bf16[4,96,768]{2,1,0:T(8,128)(2,1)} %get-tuple-element.193), channel_id=1, source_target_pairs={{0,16},{8,24},{16,0},{24,8},{1,17},{9,25},{17,1},{25,9},{2,18},{10... | collective-permute-start | bytes 1769480 | tf_op jit(solution)/shard_map/ppermute | solution.py:28
  268.7 149.7 %all-gather.6.cloned.1.call-start = ((), (), s32[]{:S(2)}) async-start(), calls=%async_computation.4 | async-start | bytes 3932160 | tf_op jit(solution)/shard_map/all_gather | solution.py:916
  300.3 21.3 %collective-permute-start.23 = (bf16[2,192,768]{2,1,0:T(8,128)(2,1)}, bf16[2,192,768]{2,1,0:T(8,128)(2,1)S(1)}, u32[]{:S(2)}, u32[]{:S(2)}) collective-permute-start(bf16[2,192,768]{2,1,0:T(8,128)(2,1)} %get-tuple-element.204), channel_id=1, source_target_pairs={{0,2},{1,3},{2,0},{3,1},{4,6},{5,7},{6,4},{7,5},{8,10},{9,11},{10,... | collective-permute-start | bytes 1769480 | tf_op jit(solution)/shard_map/ppermute | solution.py:28
  301.5 20.2 %collective-permute-start.22 = (bf16[16,96,768]{2,1,0:T(8,128)(2,1)}, bf16[16,96,768]{2,1,0:T(8,128)(2,1)S(1)}, u32[]{:S(2)}, u32[]{:S(2)}) collective-permute-start(bf16[16,96,768]{2,1,0:T(8,128)(2,1)} %bitcast.178), channel_id=1, source_target_pairs={{0,8},{8,0},{16,24},{24,16},{1,9},{9,1},{17,25},{25,17},{2,10},{10... | collective-permute-start | bytes 7077896 | tf_op jit(solution)/shard_map/ppermute | solution.py:28
  326.3 16.8 %collective-permute-start.26 = (bf16[1,192,768]{2,1,0:T(8,128)(2,1)S(1)}, bf16[1,192,768]{2,1,0:T(8,128)(2,1)S(1)}, u32[]{:S(2)}, u32[]{:S(2)}) collective-permute-start(bf16[1,192,768]{2,1,0:T(8,128)(2,1)S(1)} %get-tuple-element.217), channel_id=1, source_target_pairs={{0,4},{1,5},{2,6},{3,7},{4,0},{5,1},{6,2},{7,3},{8,12},{9,13},{10,... | collective-permute-start | bytes 884744 | tf_op jit(solution)/shard_map/ppermute | solution.py:28
  328.9 15.7 %collective-permute-start.25 = (bf16[2,4,48,768]{3,2,1,0:T(8,128)(2,1)S(1)}, bf16[2,4,48,768]{3,2,1,0:T(8,128)(2,1)S(1)}, u32[]{:S(2)}, u32[]{:S(2)}) collective-permute-start(bf16[2,4,48,768]{3,2,1,0:T(8,128)(2,1)S(1)} %get-tuple-element.215), channel_id=1, source_target_pairs={{0,1},{1,0},{2,3},{3,2},{4,5},{5,4},{6,7},{7,6},{8,9},{9,8},{10,11... | collective-permute-start | bytes 1769480 | tf_op jit(solution)/shard_map/ppermute | solution.py:28
  339.2 15.5 %collective-permute-start.24 = (bf16[2,4,48,768]{3,2,1,0:T(8,128)(2,1)S(1)}, bf16[2,4,48,768]{3,2,1,0:T(8,128)(2,1)S(1)}, u32[]{:S(2)}, u32[]{:S(2)}) collective-permute-start(bf16[2,4,48,768]{3,2,1,0:T(8,128)(2,1)S(1)} %get-tuple-element.213), channel_id=1, source_target_pairs={{0,16},{8,24},{16,0},{24,8},{1,17},{9,25},{17,1},{25,9},{2,18},{10... | collective-permute-start | bytes 1769480 | tf_op jit(solution)/shard_map/ppermute | solution.py:28
  354.9 15.0 %collective-permute-start.30 = (bf16[16,96,768]{2,1,0:T(8,128)(2,1)}, bf16[16,96,768]{2,1,0:T(8,128)(2,1)}, u32[]{:S(2)}, u32[]{:S(2)}) collective-permute-start(bf16[16,96,768]{2,1,0:T(8,128)(2,1)} %bitcast.177), channel_id=1, source_target_pairs={{0,8},{8,0},{16,24},{24,16},{1,9},{9,1},{17,25},{25,17},{2,10},{10... | collective-permute-start | bytes 7077896 | tf_op jit(solution)/shard_map/ppermute | solution.py:28
  374.6 20.8 %collective-permute-start.34 = (bf16[2,4,48,768]{3,2,1,0:T(8,128)(2,1)S(1)}, bf16[2,4,48,768]{3,2,1,0:T(8,128)(2,1)S(1)}, u32[]{:S(2)}, u32[]{:S(2)}) collective-permute-start(bf16[2,4,48,768]{3,2,1,0:T(8,128)(2,1)S(1)} %get-tuple-element.237), channel_id=1, source_target_pairs={{0,16},{8,24},{16,0},{24,8},{1,17},{9,25},{17,1},{25,9},{2,18},{10... | collective-permute-start | bytes 1769480 | tf_op jit(solution)/shard_map/ppermute | solution.py:28
  (65 other events, 855.6 us)
Sparse Core Ops, SparseCore 0:
  52.4 103.3 all-gather.7
  268.8 38.7 all-gather.9
  355.4 36.5 all-gather.5

commit v4 on v3

v4 whole, which is shorter than its diff:
```python
import functools

import jax
import jax.numpy as jnp
from jax import lax
from jax.experimental import pallas as pl
from jax.experimental.pallas import tpu as pltpu
from jax.sharding import PartitionSpec as P

HD = 64
PATCHES = 256
BLOCK_ROWS = 256
COSTS = (20, 20, 2, 1, 20)
LATE_STEP = -1
DM_EARLY = 0
EPSILON = 1e-06
HIGHEST = lax.Precision.HIGHEST
BF = jnp.bfloat16
F32 = jnp.float32


def bits_of(size):
    return size.bit_length() - 1


def swap(value, axis, bit):
    size = lax.axis_size(axis)
    return lax.ppermute(value, axis, [(i, i ^ (1 << bit)) for i in range(size)])


def swap_far(value, far, mask):
    axis = far[0][0]
    flip = sum(1 << bit for i, (a, bit) in enumerate(far) if mask >> i & 1)
    size = lax.axis_size(axis)
    return lax.ppermute(value, axis, [(i, i ^ flip) for i in range(size)])


def swap_both(value, one, two):
    sizes = lax.axis_size("tp"), lax.axis_size("sp")
    bits = dict([one, two])
    flip = (sizes[1] << bits["tp"]) ^ (1 << bits["sp"])
    return lax.ppermute(value, ("tp", "sp"), [(i, i ^ flip) for i in range(sizes[0] * sizes[1])])


def my_bit(axis, bit):
    return (lax.axis_index(axis) >> bit) & 1


def cube_sum(value, dims):
    for axis, bit in dims:
        value = value + swap(value, axis, bit)
    return value


def cube_gather(block, dims):
    held = block[None]
    for axis, bit in dims:
        other = swap(held, axis, bit)
        high = my_bit(axis, bit) == 1
        held = jnp.concatenate([jnp.where(high, other, held), jnp.where(high, held, other)])
    return held


def cube_scatter(parts, dims):
    for axis, bit in reversed(dims):
        half = parts.shape[0] // 2
        mine = my_bit(axis, bit)
        send = lax.dynamic_slice_in_dim(parts, (1 - mine) * half, half)
        keep = lax.dynamic_slice_in_dim(parts, mine * half, half)
        got = swap(send, axis, bit)
        parts = keep.astype(F32) + got.astype(F32)
        if half > 1:
            parts = parts.astype(BF)
    return parts[0]


def in_device_order(gathered, dims, back=False):
    count = len(dims)
    want = [("tp", b) for b in reversed(range(bits_of(lax.axis_size("tp"))))]
    want += [("sp", b) for b in reversed(range(bits_of(lax.axis_size("sp"))))]
    have = list(reversed(dims))
    tail = gathered.shape[1:]
    if back:
        have, want = want, have
    split = gathered.reshape((2,) * count + tail)
    order = [have.index(w) for w in want]
    split = split.transpose(order + [count + i for i in range(len(tail))])
    return split.reshape((2**count,) + tail)


VMEM_BYTES = 52 * 1024 * 1024


def cost(micros):
    return pl.CostEstimate(flops=micros * 10**9, bytes_accessed=2**10, transcendentals=0)


def after(value, *others):
    return lax.optimization_barrier((value,) + others)[0]


class Chain:
    def __init__(self, state, steps):
        self.state, self.steps = tuple(state), list(steps)

    def go(self):
        if self.steps:
            self.state = tuple(self.steps.pop(0)(*self.state))

    def run(self):
        while self.steps:
            self.go()
        return self.state


def stage(chains, *values):
    states, values = lax.optimization_barrier(([c.state for c in chains], values))
    for chain, state in zip(chains, states):
        chain.state = tuple(state)
    return values if len(values) != 1 else values[0]


def gather_chain(block, far, last):
    def far_step(held):
        return (jnp.concatenate([held] + [swap_far(held, far, m) for m in range(1, 1 << len(far))]),)

    def split(held):
        half = held.shape[1] // 2
        one, two = held[:, :half], held[:, half:]
        return (
            jnp.concatenate([one, swap(one, *last[0])]),
            jnp.concatenate([two, swap(two, *last[1])]),
        )

    def join(one, two):
        return (jnp.concatenate([one, swap(one, *last[1]), two, swap(two, *last[0])]),)

    def final(held):
        return (held, swap(held, *last[2]))

    return Chain((block[None],), [far_step, split, join, final])


def scatter_chain(other, mine, far, last, direct=False, early=False, by_bits=False):
    def add(left, *rights):
        return sum((r.astype(F32) for r in rights), left.astype(F32))

    def first(other, mine):
        total = add(mine, swap(other, *last[2])).astype(BF)
        count, rows = total.shape[0], total.shape[1]
        if direct:
            parts = total.reshape((2, 2, count // 4, rows) + total.shape[2:])
            return parts[0, 0], parts[0, 1], parts[1, 0], parts[1, 1]
        total = total.reshape((2, 2, count // 4, 2, rows // 2) + total.shape[2:])
        one, two = total[:, :, :, 0], total[:, :, :, 1]
        return one[0], one[1], two[:, 0], two[:, 1]

    def second(keep_one, send_one, keep_two, send_two):
        return keep_one, swap(send_one, *last[1]), keep_two, swap(send_two, *last[0])

    def second_sum(keep_one, got_one, keep_two, got_two):
        one = add(keep_one, got_one).astype(BF)
        two = add(keep_two, got_two).astype(BF)
        return one[0], one[1], two[0], two[1]

    def third(keep_one, send_one, keep_two, send_two):
        one = add(keep_one, swap(send_one, *last[0])).astype(BF)
        two = add(keep_two, swap(send_two, *last[1])).astype(BF)
        both = jnp.concatenate([one, two], axis=1)
        return tuple(both[m] for m in range(both.shape[0]))

    def at_once(keep, send_near, send_far, send_both):
        got = (
            swap(send_near, *last[0]),
            swap(send_far, *last[1]),
            swap_both(send_both, last[0], last[1]),
        )
        total = add(keep, *got).astype(BF)
        return tuple(total[m] for m in range(total.shape[0]))

    def far_step(*parts):
        return (add(parts[0], *[swap_far(p, far, m + 1) for m, p in enumerate(parts[1:])]),)

    def bit_step(bit):
        def run(*parts):
            half = len(parts) // 2
            sent = swap(jnp.stack(parts[half:]), *far[bit])
            sums = [add(p, g) for p, g in zip(parts[:half], sent)]
            return (sums[0],) if half == 1 else tuple(v.astype(BF) for v in sums)

        return run

    far_steps = [bit_step(b) for b in reversed(range(len(far)))] if by_bits else [far_step]

    def both_seconds(*state):
        return second_sum(*second(*state))

    if direct:
        steps = [first, at_once]
    elif early:
        steps = [first, second, second_sum, third]
    else:
        steps = [first, both_seconds, third]
    return Chain((other, mine), steps + far_steps)


def sum_chain(value, dims):
    def step(axis, bits):
        masks = [0]
        for bit in bits:
            masks += [m | 1 << bit for m in masks]
        size = lax.axis_size(axis)

        def run(value):
            others = [lax.ppermute(value, axis, [(i, i ^ m) for i in range(size)]) for m in masks[1:]]
            return (sum(others, value),)

        return run

    return Chain((value,), [step(*d) for d in dims])


def dims_masks(dims):
    masks = []
    for m in range(2 ** len(dims)):
        flip = {"tp": 0, "sp": 0}
        for place, (axis, bit) in enumerate(dims):
            flip[axis] |= ((m >> place) & 1) << bit
        masks.append((flip["tp"], flip["sp"]))
    return masks


def tp_flip(last, step):
    return (step % 2) << last[1][1] | (1 - step // 2) << last[2][1]


def tp_at(place, step, meta):
    if place is None:
        return step
    return meta[1] ^ tp_flip(place[1], step)


def dot(left, right, left_dim, right_dim):
    return lax.dot_general(
        left, right, (((left_dim,), (right_dim,)), ((), ())), preferred_element_type=F32
    )


def norm_rows(operand):
    centred = operand - jnp.mean(operand, axis=-1, keepdims=True)
    inverse = lax.rsqrt(jnp.mean(centred * centred, axis=-1, keepdims=True) + EPSILON)
    return (centred * inverse, inverse)


def norm_back(incoming, normed, inverse):
    first_mean = jnp.mean(incoming, axis=-1, keepdims=True)
    second_mean = jnp.mean(incoming * normed, axis=-1, keepdims=True)
    return inverse * (incoming - first_mean - normed * second_mean)


def params(count=1):
    return pltpu.CompilerParams(
        dimension_semantics=("arbitrary",) * count, vmem_limit_bytes=VMEM_BYTES
    )


def whole(shape):
    zeros = (0,) * len(shape)
    return pl.BlockSpec(shape, lambda g, meta: zeros, pipeline_mode=pl.Buffered(1))


def step_weights(meta, pieces, place, step, target):
    if place is None:
        return pieces[0]
    far, last = place
    near_count = 1 << len(far)
    half = pieces[0].shape[1]
    index = step % 2

    def fill(piece):
        for m in range(2 * near_count):
            z, y = m % near_count, m // near_count
            flip = sum(1 << bit for i, (a, bit) in enumerate(far) if z >> i & 1)
            flip |= y << last[0][1]
            at = pl.multiple_of((meta[2] ^ flip) * (2 * half), 2 * half)
            target[pl.ds(at, half), :] = piece[index * 2 * near_count + m]
            target[pl.ds(at + half, half), :] = piece[
                4 * near_count + y * 2 * near_count + index * near_count + z
            ]

    @pl.when(step // 2 == 1)
    def _():
        fill(pieces[0])

    @pl.when(step // 2 == 0)
    def _():
        fill(pieces[1])

    return target


def columns(weights, start, stop):
    if len(weights.shape) == 2:
        return weights[:, start:stop]
    if len(weights.shape) == 3:
        return weights[0, :, start:stop]
    return weights[0, :, 0, :, start:stop].reshape(-1, stop - start)


def split_places(pair):
    count, width = pair.shape[0], pair.shape[3]
    one, two = pair[:, 0], pair[:, 1]
    upper = lax.broadcasted_iota(jnp.int32, one.shape, 1) < 4
    left = jnp.where(upper, one, pltpu.roll(two, 4, 1))
    right = jnp.where(upper, pltpu.roll(one, 4, 1), two)
    return left.reshape(count * 8, width), right.reshape(count * 8, width)


def join_places(left, right):
    count, width = left.shape[0] // 8, left.shape[1]
    left, right = left.reshape(count, 8, width), right.reshape(count, 8, width)
    upper = lax.broadcasted_iota(jnp.int32, left.shape, 1) < 4
    one = jnp.where(upper, left, pltpu.roll(right, 4, 1))
    two = jnp.where(upper, pltpu.roll(left, 4, 1), right)
    return one, two


def blocks_of(x, groups):
    if len(x.shape) == 4 and groups == 2 and x.shape[1:3] == (2, 8):
        return list(split_places(x[...].astype(F32)))
    return [x[g].astype(F32) for g in range(groups)]


def forward_kernel(place, heads, masked, zipped, meta, x, hot, mst, key_r, key_c, *refs):
    pieces = refs[: 1 if place is None else 2]
    x_out, h_out, qkv_out, p_out, o_out, a_out, w, acc = refs[len(pieces) :]
    groups, rows, width = h_out.shape
    head_tp = heads * HD
    step = pl.program_id(0)

    def modulation(g, i):
        return dot(hot[g % hot.shape[0]], mst[:, i * width : (i + 1) * width], 1, 0)

    @pl.when(step == 0)
    def _():
        for g, xin in enumerate(blocks_of(x, groups)):
            normed = norm_rows(xin)[0]
            h_out[g] = (normed * (1.0 + modulation(g, 1)) + modulation(g, 0)).astype(BF)

    wt = step_weights(meta, pieces, place, step, w)
    bias = jnp.where(key_r[...] == key_c[...], 0.0, -1e30) if masked else None
    h = h_out[...].reshape(groups * rows, width)
    proj = dot(h, columns(wt, 0, 3 * head_tp), 1, 0).astype(BF)
    qkv_out[:, 0] = proj.reshape(groups, rows, 3 * head_tp)
    mixed = []
    for g in range(groups):
        outs = []
        for j in range(heads):
            q, k, v = (
                proj[g * rows : (g + 1) * rows, i * head_tp + j * HD : i * head_tp + (j + 1) * HD]
                for i in range(3)
            )
            scores = dot(k, q * jnp.asarray(0.125, BF), 1, 1)
            if masked:
                scores = scores + bias
            e = jnp.exp(scores - jnp.max(scores, axis=0, keepdims=True))
            p = (e * (1.0 / jnp.sum(e, axis=0, keepdims=True))).astype(BF)
            p_out[g, j] = p
            outs.append(dot(v, p, 0, 0))
        mixed.append(jnp.concatenate(outs, axis=0).T.astype(BF))
        o_out[g, 0] = mixed[-1]
    o = jnp.concatenate(mixed, axis=0)
    part = dot(o, columns(wt, 3 * head_tp, 4 * head_tp), 1, 1)

    @pl.when(step == 0)
    def _():
        acc[...] = part

    @pl.when(step > 0)
    def _():
        acc[...] += part

    @pl.when(step == pl.num_programs(0) - 1)
    def _():
        new = []
        for g, xin in enumerate(blocks_of(x, groups)):
            total = acc[g * rows : (g + 1) * rows, :]
            a_out[g] = total.astype(BF)
            new.append(xin + modulation(g, 2) * total)
        if zipped:
            one, two = join_places(*new)
            x_out[:, 0], x_out[:, 1] = one.astype(x_out.dtype), two.astype(x_out.dtype)
        else:
            for g in range(groups):
                if len(x_out.shape) == 4:
                    shape = (x_out.shape[0],) + x_out.shape[2:]
                    x_out[:, g] = new[g].reshape(shape).astype(x_out.dtype)
                else:
                    x_out[g] = new[g].astype(x_out.dtype)


def weight_specs(pieces, place):
    if place is not None:
        return [whole(p.shape) for p in pieces]
    (full,) = pieces
    if full.ndim == 5:
        block = (1, full.shape[1], 1) + full.shape[3:]
        return [pl.BlockSpec(block, lambda g, meta: (g, 0, 0, 0, 0))]
    return [pl.BlockSpec((1,) + full.shape[1:], lambda g, meta: (g, 0, 0))]


def head_spec(place, groups, *shape):
    zeros = (0,) * (len(shape) - 1)
    return pl.BlockSpec((groups,) + shape, lambda g, meta: (0, tp_at(place, g, meta)) + zeros)


def fixed(shape):
    zeros = (0,) * len(shape)
    return pl.BlockSpec(shape, lambda g, meta: zeros)


def rows_spec(x, groups, zipped):
    if zipped or x.ndim == 4:
        return whole(x.shape)
    return pl.BlockSpec(
        (groups,) + x.shape[1:], lambda g, meta: (meta[0] // groups, 0, 0),
        pipeline_mode=pl.Buffered(1),
    )


def forward(meta, x, groups, rows, hot, mst, keys, pieces, place, n_tp, heads, x_shape, out_dtype):
    width = x.shape[-1]
    lanes = 4 * heads * HD
    masked = keys is not None
    zipped = x.ndim == 4
    if keys is None:
        keys = jnp.zeros((8, 1), jnp.int32), jnp.zeros((1, 128), jnp.int32)
    return pl.pallas_call(
        functools.partial(forward_kernel, place, heads, masked, zipped),
        out_shape=[
            jax.ShapeDtypeStruct(x_shape, out_dtype),
            jax.ShapeDtypeStruct((groups, rows, width), BF),
            jax.ShapeDtypeStruct((groups, n_tp, rows, 3 * heads * HD), BF),
            jax.ShapeDtypeStruct((groups, n_tp * heads, rows, rows), BF),
            jax.ShapeDtypeStruct((groups, n_tp, rows, heads * HD), BF),
            jax.ShapeDtypeStruct((groups, rows, width), BF),
        ],
        grid_spec=pltpu.PrefetchScalarGridSpec(
            num_scalar_prefetch=1,
            grid=(n_tp,),
            in_specs=[
                rows_spec(x, groups, zipped),
                whole(hot.shape),
                whole(mst.shape),
                whole(keys[0].shape),
                whole(keys[1].shape),
            ]
            + weight_specs(pieces, place),
            out_specs=[
                fixed(x_shape),
                fixed((groups, rows, width)),
                head_spec(place, groups, 1, rows, 3 * heads * HD),
                head_spec(place, groups, heads, rows, rows),
                head_spec(place, groups, 1, rows, heads * HD),
                fixed((groups, rows, width)),
            ],
            scratch_shapes=[
                pltpu.VMEM((width, lanes), BF),
                pltpu.VMEM((groups * rows, width), F32),
            ],
        ),
        compiler_params=params(),
        cost_estimate=cost(COSTS[0]),
    )(meta, x, hot, mst, *keys, *pieces)


def grads_in(dx, groups, rows):
    if len(dx.shape) == 4 and dx.shape[1] == groups and dx.shape[0] * dx.shape[2] == rows:
        return [dx[:, g].astype(F32).reshape(rows, dx.shape[3]) for g in range(groups)]
    return [dx[g].astype(F32) for g in range(groups)]


def heads_back(heads, w, da, qkv, p, groups, rows):
    head_tp = heads * HD
    do = dot(da, columns(w, 3 * head_tp, 4 * head_tp), 1, 0).astype(BF)
    out = []
    for g in range(groups):
        got = [[], [], []]
        for j in range(heads):
            q, k, v = (
                qkv[g, 0, :, i * head_tp + j * HD : i * head_tp + (j + 1) * HD] for i in range(3)
            )
            dop = do[g * rows : (g + 1) * rows, j * HD : (j + 1) * HD]
            prob = p[g, j]
            dp = dot(v, dop, 1, 1)
            prob32 = prob.astype(F32)
            prod = prob32 * dp
            ds = (prod - prob32 * jnp.sum(prod, axis=0, keepdims=True)).astype(BF)
            got[0].append(dot(k, ds, 0, 0))
            got[1].append(dot(ds, q, 1, 0))
            got[2].append(dot(prob, dop, 1, 0))
        dq = jnp.concatenate(got[0], axis=0).T * 0.125
        dk = jnp.concatenate(got[1], axis=1) * 0.125
        out.append(jnp.concatenate([dq, dk] + got[2], axis=1).astype(BF))
    return out[0] if groups == 1 else jnp.concatenate(out, axis=0)


def finish_rows(hot, hot_t, mst, x, a, grads, dh, dm_out, groups):
    rows, width = a.shape[1], a.shape[2]
    sums = None
    out = []
    for g, xin in enumerate(blocks_of(x, groups)):
        at = slice(g * rows, (g + 1) * rows)
        gain = 1.0 + dot(hot[g % hot.shape[0]], mst[:, width : 2 * width], 1, 0)
        normed, inverse = norm_rows(xin)
        part = dh[at, :]
        grad = grads[g]
        out.append(grad + norm_back(part * gain, normed, inverse))
        new = [
            dot(hot_t[g % hot.shape[0]], value.astype(BF), 1, 0)
            for value in (part, part * normed, grad * a[g].astype(F32))
        ]
        sums = new if sums is None else [s + n for s, n in zip(sums, new)]
    for i in range(3):
        dm_out[:, i * width : (i + 1) * width] = sums[i]
    return out


def half_specs(half, shape):
    zeros = (0,) * len(shape)
    return [
        pl.BlockSpec((1,) + shape, lambda g, meta: (jnp.minimum(g, half - 1),) + zeros),
        pl.BlockSpec((1,) + shape, lambda g, meta: (jnp.maximum(g - half, 0),) + zeros),
    ]


def store_grads(masks, meta, step, first, second, blocks, outs):
    wide = first.shape[1]
    if masks is None:
        outs[0][0, :, :wide] = first
        outs[0][0, :, wide:] = second
        return
    blocks[:, :wide] = first
    blocks[:, wide:] = second
    half = pl.num_programs(0) // 2

    @pl.when(step < half)
    def _():
        store_blocks(meta, masks, blocks, outs[0].at[0])

    @pl.when(step >= half)
    def _():
        store_blocks(meta, masks, blocks, outs[1].at[0])


def grads_out(masks, n_tp, width, row_sp, lanes):
    if masks is None:
        out_shape = [jax.ShapeDtypeStruct((n_tp, width, lanes), BF)]
        return out_shape, [pl.BlockSpec((1, width, lanes), lambda g, meta: (g, 0, 0))]
    half = n_tp // 2
    shape = (len(masks) // n_tp, row_sp, lanes)
    return [jax.ShapeDtypeStruct((half,) + shape, BF)] * 2, half_specs(half, shape)


def back_kernel(masks, heads, meta, dx, x, hot, hot_t, mst, a, h, o, qkv, p, w, *refs):
    dx_out, dm_out, *outs, dh, h_t, da, da_t, blocks = refs
    groups, rows, width = a.shape
    head_tp = heads * HD
    step = pl.program_id(0)
    zipped = len(x.shape) == 4

    @pl.when(step == 0)
    def _():
        for g, grad in enumerate(blocks_of(dx, groups)):
            at = slice(g * rows, (g + 1) * rows)
            gate = dot(hot[g % hot.shape[0]], mst[:, 2 * width :], 1, 0)
            low = (gate * grad).astype(BF)
            da[at, :] = low
            da_t[:, at] = low.T
            h_t[:, at] = h[g].T

    dqkv = heads_back(heads, w, da[...], qkv, p, groups, rows)
    part = dot(dqkv, columns(w, 0, 3 * head_tp), 1, 1)
    first = dot(h_t[...], dqkv, 1, 0).astype(BF)
    second = dot(da_t[...], o[...].reshape(groups * rows, head_tp), 1, 0).astype(BF)
    store_grads(masks, meta, step, first, second, blocks, outs)

    @pl.when(step == 0)
    def _():
        dh[...] = part

    @pl.when(step > 0)
    def _():
        dh[...] += part

    @pl.when(step == pl.num_programs(0) - 1)
    def _():
        grads = blocks_of(dx, groups)
        new = finish_rows(hot, hot_t, mst, x, a, grads, dh, dm_out, groups)
        if zipped:
            one, two = join_places(*new)
            dx_out[:, 0], dx_out[:, 1] = one.astype(BF), two.astype(BF)
        else:
            for g in range(groups):
                dx_out[g] = new[g].astype(BF)


def backward(meta, dx, x, hot, hot_t, mst, a, h, o, qkv, p, pieces, place, masks, row_sp, heads):
    groups, n_tp, rows = qkv.shape[:3]
    width = a.shape[2]
    clips = hot_t.shape[1]
    lanes = 4 * heads * HD
    out_shape, out_specs = grads_out(masks, n_tp, width, row_sp, lanes)
    (full,) = pieces
    ahead = (1, full.shape[1], 1) if full.ndim == 5 else (1,)
    block = ahead + full.shape[-2:]
    zeros = (0,) * (len(block) - 1)
    return pl.pallas_call(
        functools.partial(back_kernel, masks, heads),
        out_shape=[
            jax.ShapeDtypeStruct(x.shape, BF),
            jax.ShapeDtypeStruct((clips, 3 * width), F32),
        ]
        + out_shape,
        grid_spec=pltpu.PrefetchScalarGridSpec(
            num_scalar_prefetch=1,
            grid=(n_tp,),
            in_specs=[
                whole(dx.shape),
                whole(x.shape),
                whole(hot.shape),
                whole(hot_t.shape),
                whole(mst.shape),
                whole(a.shape),
                whole(h.shape),
                head_spec(place, groups, 1, rows, heads * HD),
                head_spec(place, groups, 1, rows, 3 * heads * HD),
                head_spec(place, groups, heads, rows, rows),
                pl.BlockSpec(block, lambda g, meta: (tp_at(place, g, meta),) + zeros),
            ],
            out_specs=[fixed(x.shape), fixed((clips, 3 * width))] + out_specs,
            scratch_shapes=[
                pltpu.VMEM((groups * rows, width), F32),
                pltpu.VMEM((width, groups * rows), BF),
                pltpu.VMEM((groups * rows, width), BF),
                pltpu.VMEM((width, groups * rows), BF),
                pltpu.VMEM((width, lanes), BF),
            ],
        ),
        compiler_params=params(),
        cost_estimate=cost(COSTS[1]),
    )(meta, dx, x, hot, hot_t, mst, a, h, o, qkv, p, full)


def back_grads_kernel(place, masks, heads, meta, dx, hot, mst, h, o, qkv, p, *refs):
    pieces = refs[: 1 if place is None else 2]
    dqkv_out, *outs, w, h_t, da, da_t, blocks = refs[len(pieces) :]
    groups, rows, width = h.shape
    head_tp = heads * HD
    step = pl.program_id(0)

    @pl.when(step == 0)
    def _():
        for g, grad in enumerate(grads_in(dx, groups, rows)):
            at = slice(g * rows, (g + 1) * rows)
            gate = dot(hot[g % hot.shape[0]], mst[:, 2 * width :], 1, 0)
            low = (gate * grad).astype(BF)
            da[at, :] = low
            da_t[:, at] = low.T
            h_t[:, at] = h[g].T

    wt = step_weights(meta, pieces, place, step, w)
    dqkv = heads_back(heads, wt, da[...], qkv, p, groups, rows)
    dqkv_out[:, 0] = dqkv.reshape(groups, rows, 3 * head_tp)
    first = dot(h_t[...], dqkv, 1, 0).astype(BF)
    second = dot(da_t[...], o[...].reshape(groups * rows, head_tp), 1, 0).astype(BF)
    store_grads(masks, meta, step, first, second, blocks, outs)


def backward_grads(meta, dx, hot, mst, h, o, qkv, p, pieces, place, masks, row_sp, heads):
    groups, n_tp, rows = qkv.shape[:3]
    width = h.shape[2]
    lanes = 4 * heads * HD
    out_shape, out_specs = grads_out(masks, n_tp, width, row_sp, lanes)
    return pl.pallas_call(
        functools.partial(back_grads_kernel, place, masks, heads),
        out_shape=[jax.ShapeDtypeStruct(qkv.shape, BF)] + out_shape,
        grid_spec=pltpu.PrefetchScalarGridSpec(
            num_scalar_prefetch=1,
            grid=(n_tp,),
            in_specs=[
                whole(dx.shape),
                whole(hot.shape),
                whole(mst.shape),
                whole(h.shape),
                head_spec(place, groups, 1, rows, heads * HD),
                head_spec(place, groups, 1, rows, 3 * heads * HD),
                head_spec(place, groups, heads, rows, rows),
            ]
            + weight_specs(pieces, place),
            out_specs=[head_spec(place, groups, 1, rows, 3 * heads * HD)] + out_specs,
            scratch_shapes=[
                pltpu.VMEM((width, lanes), BF),
                pltpu.VMEM((width, groups * rows), BF),
                pltpu.VMEM((groups * rows, width), BF),
                pltpu.VMEM((width, groups * rows), BF),
                pltpu.VMEM((width, lanes), BF),
            ],
        ),
        compiler_params=params(),
        cost_estimate=cost(COSTS[1]),
    )(meta, dx, hot, mst, h, o, qkv, p, *pieces)


def input_back_kernel(place, heads, meta, dx, x, hot, hot_t, mst, a, dqkv, *refs):
    pieces = refs[: 1 if place is None else 2]
    dx_out, dm_out, w, dh = refs[len(pieces) :]
    groups, rows, width = a.shape
    head_tp = heads * HD
    step = pl.program_id(0)
    wt = step_weights(meta, pieces, place, step, w)
    all_rows = dqkv[...].reshape(groups * rows, 3 * head_tp)
    part = dot(all_rows, columns(wt, 0, 3 * head_tp), 1, 1)

    @pl.when(step == 0)
    def _():
        dh[...] = part

    @pl.when(step > 0)
    def _():
        dh[...] += part

    @pl.when(step == pl.num_programs(0) - 1)
    def _():
        grads = grads_in(dx, groups, rows)
        new = finish_rows(hot, hot_t, mst, x, a, grads, dh, dm_out, groups)
        for g in range(groups):
            dx_out[g] = new[g].astype(BF)


def input_back(meta, dx, x, hot, hot_t, mst, a, dqkv, pieces, place, heads):
    groups, n_tp, rows = dqkv.shape[:3]
    width = a.shape[2]
    clips = hot_t.shape[1]
    return pl.pallas_call(
        functools.partial(input_back_kernel, place, heads),
        out_shape=[
            jax.ShapeDtypeStruct(a.shape, BF),
            jax.ShapeDtypeStruct((clips, 3 * width), F32),
        ],
        grid_spec=pltpu.PrefetchScalarGridSpec(
            num_scalar_prefetch=1,
            grid=(n_tp,),
            in_specs=[
                whole(dx.shape),
                rows_spec(x, groups, False),
                whole(hot.shape),
                whole(hot_t.shape),
                whole(mst.shape),
                whole(a.shape),
                head_spec(place, groups, 1, rows, 3 * heads * HD),
            ]
            + weight_specs(pieces, place),
            out_specs=[fixed(a.shape), fixed((clips, 3 * width))],
            scratch_shapes=[
                pltpu.VMEM((width, 4 * heads * HD), BF),
                pltpu.VMEM((groups * rows, width), F32),
            ],
        ),
        compiler_params=params(),
        cost_estimate=cost(COSTS[4]),
    )(meta, dx, x, hot, hot_t, mst, a, dqkv, *pieces)


def store_blocks(meta, masks, scratch, target):
    count, rows = target.shape[0], target.shape[1]
    for place in range(count):
        at = pl.multiple_of((meta[2] ^ masks[place][1]) * rows, rows)
        target[place] = scratch[pl.ds(at, rows), :]


def tp_of(masks, n_tp, g, meta):
    if masks is None:
        return g
    flips = [masks[i * (len(masks) // n_tp)][0] for i in range(n_tp)]
    flips = flips[n_tp // 2 :] + flips[: n_tp // 2]
    flip = 0
    for i, value in enumerate(flips):
        flip = jnp.where(g == i, value, flip)
    return meta[1] ^ flip


GELU_A = 0.7978845608028654
GELU_B = 0.044715


def feed_kernel(masks, last_call, meta, x2, dy, hot, hot_t, mst, up, down, *refs):
    if last_call:
        acc_in, dh_in, out, dx_out, dm_out, *grads, h3, da3, h3_t, da3_t, acc, dh, blocks = refs
    else:
        acc, dh, *grads, h3, da3, h3_t, da3_t, blocks = refs
    width = x2.shape[1]
    step = pl.program_id(0)

    def modulation(i):
        return dot(hot[...], mst[:, i * width : (i + 1) * width], 1, 0)

    @pl.when(step == 0)
    def _():
        normed = norm_rows(x2[...])[0]
        h3[...] = (normed * (1.0 + modulation(1)) + modulation(0)).astype(BF)
        da3[...] = (modulation(2) * dy[...].astype(F32)).astype(BF)
        h3_t[...] = h3[...].T
        da3_t[...] = da3[...].T
        if last_call:
            acc[...], dh[...] = acc_in[...], dh_in[...]
        else:
            acc[...] = jnp.zeros_like(acc)
            dh[...] = jnp.zeros_like(dh)

    wu = up[...].reshape(width, -1)
    wd = down[...].reshape(width, -1)
    u = dot(h3[...], wu, 1, 0)
    square = u * u
    th = jnp.tanh(GELU_A * (u + GELU_B * (square * u)))
    g = (0.5 * u * (1.0 + th)).astype(BF)
    slope = 0.5 * (1.0 + th) + (0.5 * GELU_A) * u * (1.0 - th * th) * (
        1.0 + (3.0 * GELU_B) * square
    )
    dg = dot(da3[...], wd, 1, 0)
    du = (dg * slope).astype(BF)
    acc[...] += dot(g, wd, 1, 1)
    dh[...] += dot(du, wu, 1, 1)
    grad_up = dot(h3_t[...], du, 1, 0).astype(BF)
    grad_down = dot(da3_t[...], g, 1, 0).astype(BF)
    if masks is None:
        grads[0][0], grads[1][0] = grad_up, grad_down
    else:
        for i, value in enumerate((grad_up, grad_down)):
            blocks[...] = value
            store_blocks(meta, masks, blocks, grads[0].at[0, :, i])

    if last_call:

        @pl.when(step == pl.num_programs(0) - 1)
        def _():
            grad = dy[...].astype(F32)
            a3 = acc[...]
            xin = x2[...]
            normed, inverse = norm_rows(xin)
            out[...] = (xin + modulation(2) * a3).astype(BF)
            dh3 = dh[...]
            dx_out[...] = grad + norm_back(dh3 * (1.0 + modulation(1)), normed, inverse)
            for i, value in enumerate([dh3, dh3 * normed, grad * a3]):
                dm_out[:, i * width : (i + 1) * width] = dot(hot_t[...], value.astype(BF), 1, 0)


def feed_half(meta, x2, dy, hot, hot_t, mst, weights, masks, sums):
    rows, width = x2.shape
    n_tp, n_sp, unused, row_sp, units = weights.shape
    clips = hot_t.shape[0]
    half = n_tp // 2
    last_call = sums is not None
    start = half if last_call else 0
    at = lambda g, meta: tp_of(masks, n_tp, g + start, meta)
    if masks is None:
        blocked = weights.transpose(2, 0, 1, 3, 4).reshape(3, n_tp, width, units)
        up, down = blocked[1], blocked[2]
        specs = [pl.BlockSpec((1, width, units), lambda g, meta: (g + start, 0, 0))] * 2
        grad_shapes = [(half, width, units)] * 2
    else:
        up = down = weights
        specs = [
            pl.BlockSpec(
                (1, n_sp, 1, row_sp, units), lambda g, meta, i=i: (at(g, meta), 0, i, 0, 0)
            )
            for i in (1, 2)
        ]
        grad_shapes = [(half, n_sp, 2, row_sp, units)]
    zeros = (0,) * (len(grad_shapes[0]) - 1)
    grad_spec = pl.BlockSpec((1,) + grad_shapes[0][1:], lambda g, meta: (g,) + zeros)
    plain = lambda s: pl.BlockSpec(s, lambda g, meta: (0, 0))
    total = pltpu.VMEM((rows, width), F32)
    kept = [pltpu.VMEM((rows, width), BF)] * 2 + [pltpu.VMEM((width, rows), BF)] * 2
    if last_call:
        out_types = [((rows, width), BF), ((rows, width), F32), ((clips, 3 * width), F32)]
        scratch = kept + [total, total]
    else:
        out_types = [((rows, width), F32), ((rows, width), F32)]
        scratch = kept
    return pl.pallas_call(
        functools.partial(feed_kernel, masks, last_call),
        out_shape=[jax.ShapeDtypeStruct(*t) for t in out_types]
        + [jax.ShapeDtypeStruct(g, BF) for g in grad_shapes],
        grid_spec=pltpu.PrefetchScalarGridSpec(
            num_scalar_prefetch=1,
            grid=(half,),
            in_specs=[
                whole(x2.shape),
                whole(dy.shape),
                whole(hot.shape),
                whole(hot_t.shape),
                whole(mst.shape),
            ]
            + specs
            + ([whole(x2.shape)] * 2 if last_call else []),
            out_specs=[plain(t[0]) for t in out_types] + [grad_spec] * len(grad_shapes),
            scratch_shapes=scratch + [pltpu.VMEM((width, units), BF)],
        ),
        compiler_params=params(),
        cost_estimate=cost(COSTS[3]),
    )(meta, x2, dy, hot, hot_t, mst, up, down, *(sums or ()))


def shards(
    tokens, condition, clip_ids, w_mod, w_qkv_s, w_o_s, w_qkv_t, w_o_t, w_up, w_down, grad_out
):
    n_tp, n_sp = lax.axis_size("tp"), lax.axis_size("sp")
    devices = n_tp * n_sp
    my_tp, my_sp = lax.axis_index("tp"), lax.axis_index("sp")
    width = tokens.shape[1]
    sp_frames = tokens.shape[0] // PATCHES
    frames = sp_frames // n_tp
    all_frames = sp_frames * n_sp
    places = PATCHES // devices
    per_block = max(1, min(places, BLOCK_ROWS // all_frames))
    blocks = places // per_block
    rows = all_frames * per_block
    clips = condition.shape[0]
    head_tp = w_o_s.shape[0]
    heads = head_tp // HD
    row_sp = w_up.shape[0]
    zipped = (frames, per_block, blocks) == (2, 4, 2)

    sp_bits = bits_of(n_sp)
    tp_bits = bits_of(n_tp)
    far = [("sp", b) for b in reversed(range(1, sp_bits))]
    last = [("sp", 0), ("tp", 1), ("tp", 0)]
    every = [("tp", b) for b in range(tp_bits)] + [("sp", b) for b in range(sp_bits)]
    sp_dims = [("sp", b) for b in range(sp_bits)]
    near = row_sp % 32 == 0

    def pack(w_qkv, w_o):
        flat = w_qkv.transpose(1, 0, 2).reshape(row_sp, -1)
        return jnp.concatenate([flat, w_o.T], axis=1)

    masks = dims_masks(far + last) if near else None

    def scatter(terms, **how):
        if near:
            other, mine = (v.reshape((devices // 2, -1) + v.shape[-1:]) for v in terms)
            return scatter_chain(other, mine, far, last, **how)
        terms = jnp.concatenate(terms)
        terms = terms.reshape((devices, -1) + terms.shape[-1:])
        terms = in_device_order(terms, far + last, back=True)
        return Chain((terms,), [lambda v: (cube_scatter(v, far + last),)])

    def attention_grads(mine):
        mine = mine.reshape(row_sp, 4, head_tp)
        return mine[:, :3].transpose(1, 0, 2), mine[:, 3].T

    def gather(block):
        if near:
            return gather_chain(block, far, last)
        dims = far + last

        def run(block):
            full = in_device_order(cube_gather(block, dims), dims)
            return (full.reshape(n_tp, width, -1),)

        return Chain((block,), [run])

    cond_act = jax.nn.silu(condition).astype(BF)
    cond_rows = lax.dynamic_slice_in_dim(cond_act, my_sp * row_sp, row_sp, axis=1)
    wide = [("sp", [0]), ("sp", list(range(1, sp_bits)))] if near else [("sp", [b]) for a, b in sp_dims]
    modulation = sum_chain(jnp.dot(cond_rows, w_mod, preferred_element_type=F32), wide)
    place = (far, last) if near else None
    chain_s = gather(pack(w_qkv_s, w_o_s))
    late = jnp.stack([pack(w_qkv_t, w_o_t), w_up, w_down.T])

    def hot_of(ids):
        hot = (ids[..., None] == jnp.arange(clips, dtype=jnp.int32)).astype(BF)
        return jnp.concatenate([hot, hot], axis=-1), jnp.swapaxes(hot, -1, -2)

    first = my_sp * sp_frames + my_tp * frames
    ids_s = lax.dynamic_slice_in_dim(clip_ids, first, frames)
    hot_s, hot_s_t = hot_of(jnp.repeat(ids_s[:, None], PATCHES, axis=1))
    ids_t = jnp.repeat(clip_ids, per_block)
    hot_t, hot_t_t = hot_of(ids_t[None])
    hot_f, hot_f_t = hot_of(
        jnp.repeat(clip_ids, places) if zipped else jnp.tile(ids_t, blocks)
    )
    key = ids_t * per_block + jnp.tile(jnp.arange(per_block, dtype=jnp.int32), all_frames)
    keys = key[:, None], key[None, :]
    meta0 = jnp.stack([0 * my_tp, my_tp, my_sp]).astype(jnp.int32)
    meta_s = jnp.stack([my_tp * frames, my_tp, my_sp]).astype(jnp.int32)

    def exchange(value):
        return lax.all_to_all(value, ("sp", "tp"), 0, 0, tiled=True)

    def to_places(value):
        if zipped:
            return exchange(value)
        split = value.reshape(frames, devices, blocks, per_block, width).transpose(1, 2, 0, 3, 4)
        return exchange(split).transpose(1, 0, 2, 3, 4).reshape(blocks, rows, width)

    def to_frames(value):
        if zipped:
            return exchange(value)
        split = value.reshape(blocks, devices, frames, per_block, width).transpose(1, 0, 2, 3, 4)
        return exchange(split).transpose(2, 0, 1, 3, 4).reshape(frames, PATCHES, width)

    def input_to_places(value):
        split = value.reshape(sp_frames, n_sp, n_tp, places, width)
        split = lax.dynamic_slice_in_dim(split, my_tp, 1, axis=2)[:, :, 0].transpose(1, 0, 2, 3)
        got = lax.all_to_all(split, "sp", 0, 0, tiled=True)
        if not zipped:
            got = got.reshape(all_frames, blocks, per_block, width).transpose(1, 0, 2, 3)
        return got.reshape(blocks * rows, width)

    def split_output(value):
        if not zipped:
            value = value.reshape(blocks, all_frames, per_block, width).transpose(1, 0, 2, 3)
        return lax.all_to_all(
            value.reshape(n_sp, sp_frames, places, width), "sp", 0, 0, tiled=True
        )

    step = 0
    while chain_s.steps or modulation.steps:
        chain_s.go()
        modulation.go()
        if step == LATE_STEP:
            late = stage([chain_s, modulation], late)
        else:
            stage([chain_s, modulation])
        step += 1
    late = lax.all_gather(late, ("tp", "sp"), axis=0).reshape(n_tp, n_sp, 3, row_sp, -1)
    if row_sp % 16:
        late_t = [late[:, :, 0].reshape(n_tp, width, -1)]
    else:
        late_t = [late]
    (modulation,) = modulation.state
    coarse = lax.reduce_precision(modulation, 8, 7)
    mst = jnp.concatenate([coarse, modulation - coarse]).astype(BF)
    mst_s, mst_t, mst_f = (mst[:, i * 3 * width : (i + 1) * 3 * width] for i in range(3))


    own = tokens.reshape(sp_frames, PATCHES, width)
    x1_shape = (devices, frames, places, width) if zipped else (frames, PATCHES, width)
    x1_frames, h1, qkv1, p1, o1, a1 = forward(
        meta_s, own, frames, PATCHES, hot_s, mst_s, None, chain_s.state, place, n_tp, heads,
        x1_shape, BF,
    )
    x1 = to_places(x1_frames)
    x1, grad_in = stage([], x1, grad_out)
    grad_rows = input_to_places(grad_in)
    x2, h2, qkv2, p2, o2, a2 = forward(
        meta0, x1, blocks, rows, hot_t, mst_t, keys, late_t, None, n_tp, heads, x1.shape, F32
    )

    feed_args = x2.reshape(blocks * rows, width), grad_rows, hot_f, hot_f_t, mst_f, late, masks
    if near:
        *sums, far_terms = feed_half(meta0, *feed_args, None)
        block_out, dx2, dm_f, near_terms = feed_half(meta0, *feed_args, sums)
        out_f = scatter([far_terms, near_terms], early=True)
        out_f.go()
        dx2, block_out = stage([out_f], dx2, block_out)
    else:
        *sums, up_one, down_one = feed_half(meta0, *feed_args, None)
        block_out, dx2, dm_f, up_two, down_two = feed_half(meta0, *feed_args, sums)
        pair = [scatter(p).run()[0] for p in ((up_one, up_two), (down_one, down_two))]
        out_f = Chain((jnp.concatenate(pair),), [])

    out_f.go()
    block_out = split_output(block_out)
    dx1, dm_t, *terms_t = backward(
        meta0, dx2.reshape(x2.shape), x1, hot_t, hot_t_t, mst_t, a2, h2, o2, qkv2, p2, late_t,
        place, masks, row_sp, heads,
    )
    dx1_frames = to_frames(dx1)
    block_out, terms_t = stage([out_f], block_out, terms_t)
    all_out = lax.all_gather(block_out, "tp", axis=0)
    out_t = scatter(terms_t, by_bits=True)
    out_f.go()
    out_f.go()
    out_t.go()
    dx1_frames = stage([out_t, out_f], dx1_frames)

    out_f.go()
    out_t.go()
    dqkv1, *terms_s = backward_grads(
        meta0, dx1_frames, hot_s, mst_s, h1, o1, qkv1, p1, chain_s.state, place, masks, row_sp, heads
    )
    dqkv1, terms_s, all_out = stage([out_t, out_f], dqkv1, terms_s, all_out)
    out_s = scatter(terms_s, direct=True)
    out_s.go()
    out_t.go()
    dqkv1 = stage([out_s, out_t], dqkv1)
    out_s.go()
    out_t.go()
    dx0, dm_s = input_back(
        meta_s, dx1_frames, own, hot_s, hot_s_t, mst_s, a1, dqkv1, chain_s.state, place, heads
    )
    dm = sum_chain(
        jnp.concatenate([dm_s, dm_t, dm_f], axis=-1), [(a, [b]) for a, b in reversed(far + last)]
    )
    for _ in range(DM_EARLY):
        dm.go()
    dx0, dm.state = stage([out_s, out_t], dx0, dm.state)

    grad_tokens = lax.all_gather(dx0, "tp", axis=0).reshape(-1, width)
    out_s.run()
    (dm,) = dm.run()
    sum_f, sum_t = out_f.run()[0], attention_grads(out_t.run()[0])
    sum_f = sum_f[:row_sp], sum_f[row_sp:].T
    all_out = all_out.transpose(2, 1, 0, 3, 4).reshape(-1, width)
    sum_t, sum_f, dm, all_out = stage([out_s], sum_t, sum_f, dm, all_out)
    low = dm.astype(BF)
    mine = jnp.dot(low, w_mod.T, preferred_element_type=F32)
    spot = jnp.arange(n_sp)[:, None, None] == my_sp
    part = sum_chain(jnp.where(spot, mine[None], 0.0), wide)
    part.run()
    grad_mod = jnp.dot(cond_rows.T, low, preferred_element_type=F32)
    grad_act = part.state[0].transpose(1, 0, 2).reshape(clips, width)
    unused, silu_pull = jax.vjp(jax.nn.silu, condition)
    grad_condition = silu_pull(grad_act)[0]
    sum_qs, sum_os = attention_grads(out_s.state[0])
    return (
        all_out,
        grad_tokens,
        grad_condition,
        grad_mod,
        sum_qs,
        sum_os,
        *sum_t,
        *sum_f,
    )


def solution(mesh):
    placed = (
        P("sp", None),
        P(),
        P(),
        P("sp", None),
        P(None, "sp", "tp"),
        P("tp", "sp"),
        P(None, "sp", "tp"),
        P("tp", "sp"),
        P("sp", "tp"),
        P("tp", "sp"),
        P("sp", None),
    )
    return jax.shard_map(
        shards,
        mesh=mesh,
        in_specs=placed,
        out_specs=(
            P("sp", None),
            P("sp", None),
            P(),
            P("sp", None),
            P(None, "sp", "tp"),
            P("tp", "sp"),
            P(None, "sp", "tp"),
            P("tp", "sp"),
            P("sp", "tp"),
            P("tp", "sp"),
        ),
        check_vma=False,
    )
```

time: 453 us -> 424 us (0.936)
  waiting for transfers between devices: 160 us -> 134 us
  other arithmetic: 38.3 us -> 28.1 us
  starting transfers between devices: 70.8 us -> 78.3 us
    ppermute x35 -> x20, waiting for transfers between devices: 114 us -> 66.5 us  [swap(): return lax.ppermute(value, axis, [(i, i ^ 1 << bit) for i in range(size)])]
    ppermute x13, waiting for transfers between devices: 42.9 us -> 14.2 us  [run(): lax.ppermute(value, axis, [(i, i ^ m) for i in range(size)])]
    all_to_all x2, waiting for transfers between devices: 1.95 us -> 28.4 us  [exchange(): return lax.all_to_all(value, ('sp', 'tp'), 0, 0, tiled=True)]
    ppermute x0 -> x10, waiting for transfers between devices: none -> 20.3 us  [the longest x1 11.8 us: swap_both(): lax.ppermute(value, ('tp', 'sp'), [(i, i ^ flip) for i in range(sizes[0]...]
    ppermute x0 -> x10, starting transfers between devices: none -> 16.1 us  [the longest x9 14.5 us: swap_far(): return lax.ppermute(value, axis, [(i, i ^ flip) for i in range(size)])]
    ppermute x35 -> x20, starting transfers between devices: 31.8 us -> 17.5 us  [swap(): return lax.ppermute(value, axis, [(i, i ^ 1 << bit) for i in range(size)])]
    ppermute x13, starting transfers between devices: 17.9 us -> 27.1 us  [run(): lax.ppermute(value, axis, [(i, i ^ m) for i in range(size)])]
    convert_element_type x12 -> x9, other arithmetic: 10.9 us -> 13.6 us  [the longest x3 8.46 us: first(): total = add(mine, swap(other, *last[2])).astype(BF)]
  transfers between devices with their start and end apart: 55 -> 50, of which waited for: 27 -> 26; matrix products, arithmetic and copies ran while one was open for 11% -> 10% of each run, Pallas kernels for 25% -> 26%
where the time goes in v4:
time: 424 us; the launch traced here: 417 us
  waiting for transfers between devices  134 us (32%)
  Pallas kernels  122 us (29%)
  starting transfers between devices  78.3 us (18%)
  local copies, waits for them, and re-layouts  36 us (8%)
  other arithmetic  28.1 us (7%)
  between operations  14.6 us (3%)
    ppermute x20, waiting for transfers between devices, swap(): return lax.ppermute(value, axis, [(i, i ^ 1 << bit) for i in range(size)])  66.5 us
    pallas_call x2, Pallas kernels, forward(): pl.pallas_call(functools.partial(forward_kernel, place, heads, masked, zi...  34.6 us
    pallas_call x2, Pallas kernels, feed_half(): pl.pallas_call(functools.partial(feed_kernel, masks, last_call), out_shap...  31.1 us
    all_to_all x2, waiting for transfers between devices, exchange(): return lax.all_to_all(value, ('sp', 'tp'), 0, 0, tiled=True)  28.4 us
    ppermute x13, starting transfers between devices, run(): lax.ppermute(value, axis, [(i, i ^ m) for i in range(size)])  27.1 us
    pallas_call x1, Pallas kernels, backward(): pl.pallas_call(functools.partial(back_kernel, masks, heads), out_shape=[j...  25.3 us
    pallas_call x1, Pallas kernels, backward_grads(): pl.pallas_call(functools.partial(back_grads_kernel, place, masks, heads),...  20.9 us
    ppermute x20, starting transfers between devices, swap(): return lax.ppermute(value, axis, [(i, i ^ 1 << bit) for i in range(size)])  17.5 us
  transfers between devices with their start and end apart: 50, of which 26 were waited for; matrix products, arithmetic and copies ran while one was open for 10% of the time, Pallas kernels for 26%

profile of v4, /device:TPU:0, one launch (start us, length us, event | category | flops | bytes accessed | tf_op | source)
XLA Modules:
  0.0 417.0 jit_solution(11806601863169481348)
XLA Ops:
  26.7 4.3 %collective-permute-done.3 = f32[4,6912]{1,0:T(4,128)S(1)} collective-permute-done((f32[4,6912]{1,0:T(4,128)S(1)}, f32[4,6912]{1,0:T(4,128)S(1)}, u32[]{:S(2)}, u32[]{:S(2)}) %collective-permute-start.3) | collective-permute-done | bytes 110624 | tf_op jit(solution)/shard_map/ppermute | solution.py:215
  31.1 4.2 %collective-permute-done.2 = bf16[1,96,768]{2,1,0:T(8,128)(2,1)} collective-permute-done((bf16[1,96,768]{2,1,0:T(8,128)(2,1)S(1)}, bf16[1,96,768]{2,1,0:T(8,128)(2,1)}, u32[]{:S(2)}, u32[]{:S(2)}) %collective-permute-start.2) | collective-permute-done | bytes 147488 | tf_op jit(solution)/shard_map/ppermute | solution.py:35
  36.4 8.0 %collective-permute-start.6 = (f32[4,6912]{1,0:T(4,128)S(1)}, f32[4,6912]{1,0:T(4,128)S(1)}, u32[]{:S(2)}, u32[]{:S(2)}) collective-permute-start(f32[4,6912]{1,0:T(4,128)S(1)} %add.153), channel_id=1, source_target_pairs={{0,2},{1,3},{2,0},{3,1},{4,6},{5,7},{6,4},{7,5},{8,10},{9,11},{10,... | collective-permute-start | bytes 331784 | tf_op jit(solution)/shard_map/ppermute | solution.py:215
  51.7 4.1 collective-permute-done.8
  55.9 5.7 %collective-permute-done.5 = bf16[4,48,768]{2,1,0:T(8,128)(2,1)S(1)} collective-permute-done((bf16[4,48,768]{2,1,0:T(8,128)(2,1)S(1)}, bf16[4,48,768]{2,1,0:T(8,128)(2,1)S(1)}, u32[]{:S(2)}, u32[]{:S(2)}) %collective-permute-start.5) | collective-permute-done | bytes 294944 | tf_op jit(solution)/shard_map/ppermute | solution.py:28
  67.3 10.2 %collective-permute-done.10 = bf16[8,48,768]{2,1,0:T(8,128)(2,1)S(1)} collective-permute-done((bf16[8,48,768]{2,1,0:T(8,128)(2,1)S(1)}, bf16[8,48,768]{2,1,0:T(8,128)(2,1)S(1)}, u32[]{:S(2)}, u32[]{:S(2)}) %collective-permute-start.10) | collective-permute-done | bytes 589856 | tf_op jit(solution)/shard_map/ppermute | solution.py:28
  77.5 4.2 collective-permute-done.9
  84.0 4.4 %collective-permute-done.11.refs_1_ = bf16[32,48,768]{2,1,0:T(8,128)(2,1)} collective-permute-done((bf16[32,48,768]{2,1,0:T(8,128)(2,1)}, bf16[32,48,768]{2,1,0:T(8,128)(2,1)}, u32[]{:S(2)}, u32[]{:S(2)}) %collective-permute-start.11) | collective-permute-done | bytes 2359328 | tf_op jit(solution)/shard_map/ppermute | solution.py:28
  89.1 17.7 %shard_map.186 = (bf16[32,2,8,768]{3,2,1,0:T(8,128)(2,1)S(1)}, bf16[2,256,768]{2,1,0:T(8,128)(2,1)S(1)}, bf16[2,4,256,576]{3,2,1,0:T(8,128)(2,1)}, bf16[2,12,256...) custom-call(s32[3]{0:T(128)S(1)} %add_add_fusion.2.meta, ...), custom_call_target="tpu_custom_call" | custom-call | flops 20000000000 | bytes 1024 | tf_op jit(solution)/shard_map/pallas_call | solution.py:438
  108.6 6.7 %all-to-all-start = ((bf16[32,2,8,768]{3,2,1,0:T(8,128)(2,1)}), bf16[32,2,8,768]{3,2,1,0:T(8,128)(2,1)}, u32[]{:S(2)}, u32[]{:S(2)}) async-start(bf16[32,2,8,768]{3,2,1,0:T(8,128)(2,1)} %copy-done.2), calls=%async_computation | async-start | bytes 1572864 | tf_op jit(solution)/shard_map/all_to_all | solution.py:999
  119.8 28.4 %all-to-all-done.x = bf16[32,2,8,768]{3,2,1,0:T(8,128)(2,1)} async-done(((bf16[32,2,8,768]{3,2,1,0:T(8,128)(2,1)}), bf16[32,2,8,768]{3,2,1,0:T(8,128)(2,1)}, u32[]{:S(2)}, u32[]{:S(2)}) %all-to-all-start) | async-done | bytes 786464 | tf_op jit(solution)/shard_map/all_to_all | solution.py:999
  154.4 16.8 %shard_map.187 = (f32[32,2,8,768]{3,2,1,0:T(8,128)}, bf16[2,256,768]{2,1,0:T(8,128)(2,1)S(1)}, bf16[2,4,256,576]{3,2,1,0:T(8,128)(2,1)}, bf16[2,12,256,256]{3,2,...) custom-call(s32[3]{0:T(128)S(1)} %add_add_fusion.1.meta, ...), custom_call_target="tpu_custom_call" | custom-call | flops 20000000000 | bytes 1024 | tf_op jit(solution)/shard_map/pallas_call | solution.py:438
  173.4 14.0 %shard_map.188 = (f32[512,768]{1,0:T(8,128)}, f32[512,768]{1,0:T(8,128)}, bf16[2,8,2,96,768]{4,3,2,1,0:T(8,128)(2,1)}) custom-call(s32[3]{0:T(128)S(1)} %add_add_fusion.1.meta, f32[512,768]{1,0:T(8,128)} %bitcast.184, bf16[512,768]{1,0:T(8,128)(2,1)S(1)} %bitcast.171, bf16[512,8]{1,0:T(8,128)(2,1)S(1)} %concatenate.55.hot, bf16[4,512]{1,0:T(4,128)(2,1)S(1)} %fusion.30.hot_t, ...), custom_call_target="tpu_custom_call" | custom-call | flops 1000000000 | bytes 1024 | tf_op jit(solution)/shard_map/pallas_call | solution.py:891
  187.5 17.1 %shard_map.189 = (bf16[512,768]{1,0:T(8,128)(2,1)}, f32[512,768]{1,0:T(8,128)}, f32[4,2304]{1,0:T(4,128)S(1)}, bf16[2,8,2,96,768]{4,3,2,1,0:T(8,128)(2,1)}) custom-call(s32[3]{0:T(128)S(1)} %add_add_fusion.1.meta, f32[512,768]{1,0:T(8,128)} %bitcast.185, bf16[512,768]{1,0:T(8,128)(2,1)S(1)} %bitcast.172, bf16[512,8]{1,0:T(8,128)(2,1)S(1)} %concatenate.55.hot, ...), custom_call_target="tpu_custom_call" | custom-call | flops 1000000000 | bytes 1024 | tf_op jit(solution)/shard_map/pallas_call | solution.py:891
  218.6 25.3 %shard_map.190 = (bf16[32,2,8,768]{3,2,1,0:T(8,128)(2,1)}, f32[4,2304]{1,0:T(4,128)S(1)}, bf16[2,8,96,768]{3,2,1,0:T(8,128)(2,1)}, bf16[2,8,96,768]{3,2,1,0:T(8,128)(2,1)}) custom-call(s32[3]{0:T(128)S(1)} %add_add_fusion.1.meta, f32[32,2,8,768]{3,2,1,0:T(8,128)} %bitcast.212, bf16[32,2,8,768]{3,2,1,0:T(8,128)(2,1)} %all-to-all-done.x, ...), custom_call_target="tpu_custom_call" | custom-call | flops 20000000000 | bytes 1024 | tf_op jit(solution)/shard_map/pallas_call | solution.py:618
  243.9 4.7 %collective-permute-done.14 = bf16[2,4,96,768]{3,2,1,0:T(8,128)(2,1)} collective-permute-done((bf16[2,4,96,768]{3,2,1,0:T(8,128)(2,1)}, bf16[2,4,96,768]{3,2,1,0:T(8,128)(2,1)}, u32[]{:S(2)}, u32[]{:S(2)}) %collective-permute-start.14) | collective-permute-done | bytes 1179680 | tf_op jit(solution)/shard_map/ppermute | solution.py:28
  262.1 10.7 %collective-permute-done.16 = bf16[4,96,768]{2,1,0:T(8,128)(2,1)} collective-permute-done((bf16[4,96,768]{2,1,0:T(8,128)(2,1)}, bf16[4,96,768]{2,1,0:T(8,128)(2,1)}, u32[]{:S(2)}, u32[]{:S(2)}) %collective-permute-start.16) | collective-permute-done | bytes 589856 | tf_op jit(solution)/shard_map/ppermute | solution.py:28
  274.3 10.3 %collective-permute-done.17 = bf16[4,96,768]{2,1,0:T(8,128)(2,1)} collective-permute-done((bf16[4,96,768]{2,1,0:T(8,128)(2,1)}, bf16[4,96,768]{2,1,0:T(8,128)(2,1)}, u32[]{:S(2)}, u32[]{:S(2)}) %collective-permute-start.17) | collective-permute-done | bytes 589856 | tf_op jit(solution)/shard_map/ppermute | solution.py:28
  296.5 20.9 %shard_map.191 = (bf16[2,4,256,576]{3,2,1,0:T(8,128)(2,1)}, bf16[2,8,96,768]{3,2,1,0:T(8,128)(2,1)}, bf16[2,8,96,768]{3,2,1,0:T(8,128)(2,1)}) custom-call(s32[3]{0:T(128)S(1)} %add_add_fusion.1.meta, bf16[32,2,8,768]{3,2,1,0:T(8,128)(2,1)S(1)} %all-to-all-done.3.dx, bf16[2,256,8]{2,1,0:T(8,128)(2,1)S(1)} %copy-done.4, ...), custom_call_target="tpu_custom_call" | custom-call | flops 20000000000 | bytes 1024 | tf_op jit(solution)/shard_map/pallas_call | solution.py:685
  322.6 6.1 %collective-permute-done.24 = bf16[4,48,768]{2,1,0:T(8,128)(2,1)S(1)} collective-permute-done((bf16[4,48,768]{2,1,0:T(8,128)(2,1)S(1)}, bf16[4,48,768]{2,1,0:T(8,128)(2,1)S(1)}, u32[]{:S(2)}, u32[]{:S(2)}) %collective-permute-start.24) | collective-permute-done | bytes 294944 | tf_op jit(solution)/shard_map/ppermute | solution.py:28
  336.5 10.5 %shard_map.192 = (bf16[2,256,768]{2,1,0:T(8,128)(2,1)}, f32[4,2304]{1,0:T(4,128)S(1)}) custom-call(s32[3]{0:T(128)S(1)} %copy-done.9, bf16[32,2,8,768]{3,2,1,0:T(8,128)(2,1)S(1)} %all-to-all-done.3.dx, bf16[8,256,768]{2,1,0:T(8,128)(2,1)} %bitcast.209, bf16[2,256,8]{2,1,0:T(8,128)(2,1)S(1)} %copy-done.4, bf16[2,4,256]{2,1,0:T(4,128)(2,1)S(1)} %fusion.31.hot_t, ...), custom_call_target="tpu_custom_call" | custom-call | flops 20000000000 | bytes 1024 | tf_op jit(solution)/shard_map/pallas_call | solution.py:745
  349.6 11.8 %collective-permute-done.28 = bf16[4,96,768]{2,1,0:T(8,128)(2,1)S(1)} collective-permute-done((bf16[4,96,768]{2,1,0:T(8,128)(2,1)S(1)}, bf16[4,96,768]{2,1,0:T(8,128)(2,1)S(1)}, u32[]{:S(2)}, u32[]{:S(2)}) %collective-permute-start.28) | collective-permute-done | bytes 589856 | tf_op jit(solution)/shard_map/ppermute | solution.py:42
  381.7 4.2 collective-permute-start.38
  385.9 4.4 %collective-permute-done.33 = bf16[1,96,768]{2,1,0:T(8,128)(2,1)S(1)} collective-permute-done((bf16[1,96,768]{2,1,0:T(8,128)(2,1)S(1)}, bf16[1,96,768]{2,1,0:T(8,128)(2,1)S(1)}, u32[]{:S(2)}, u32[]{:S(2)}) %collective-permute-start.33) | collective-permute-done | bytes 147488 | tf_op jit(solution)/shard_map/ppermute | solution.py:28
  (253 shorter events, 147.6 us)
Async XLA Ops:
  7.2 145.8 %all-gather.7.cloned.1.call-start = ((), (), s32[]{:S(2)}) async-start(), calls=%async_computation.4 | async-start | bytes 14598144 | tf_op jit(solution)/shard_map/all_gather | solution.py:1037
  36.4 15.3 %collective-permute-start.6 = (f32[4,6912]{1,0:T(4,128)S(1)}, f32[4,6912]{1,0:T(4,128)S(1)}, u32[]{:S(2)}, u32[]{:S(2)}) collective-permute-start(f32[4,6912]{1,0:T(4,128)S(1)} %add.153), channel_id=1, source_target_pairs={{0,2},{1,3},{2,0},{3,1},{4,6},{5,7},{6,4},{7,5},{8,10},{9,11},{10,... | collective-permute-start | bytes 331784 | tf_op jit(solution)/shard_map/ppermute | solution.py:215
  66.0 15.7 %collective-permute-start.9 = (bf16[8,48,768]{2,1,0:T(8,128)(2,1)S(1)}, bf16[8,48,768]{2,1,0:T(8,128)(2,1)S(1)}, u32[]{:S(2)}, u32[]{:S(2)}) collective-permute-start(bf16[8,48,768]{2,1,0:T(8,128)(2,1)S(1)} %pad_maximum_fusion.2), channel_id=1, source_target_pairs={{0,16},{8,24},{16,0},{24,8},{1,17},{9,25},{17,1},{25,9},{2,18},{10... | collective-permute-start | bytes 1769480 | tf_op jit(solution)/shard_map/ppermute | solution.py:28
  108.6 39.5 %all-to-all-start = ((bf16[32,2,8,768]{3,2,1,0:T(8,128)(2,1)}), bf16[32,2,8,768]{3,2,1,0:T(8,128)(2,1)}, u32[]{:S(2)}, u32[]{:S(2)}) async-start(bf16[32,2,8,768]{3,2,1,0:T(8,128)(2,1)} %copy-done.2), calls=%async_computation | async-start | bytes 1572864 | tf_op jit(solution)/shard_map/all_to_all | solution.py:999
  149.1 24.3 %all-to-all-start.1 = ((bf16[8,8,8,768]{3,2,1,0:T(8,128)(2,1)}), bf16[8,8,8,768]{3,2,1,0:T(8,128)(2,1)S(1)}, u32[]{:S(2)}, u32[]{:S(2)}) async-start(bf16[8,8,8,768]{3,2,1,0:T(8,128)(2,1)} %copy_bitcast_fusion), calls=%async_computation.1 | async-start | bytes 1572864 | tf_op jit(solution)/shard_map/all_to_all | solution.py:1016
  187.4 17.2 %collective-permute-start.12 = (bf16[16,192,768]{2,1,0:T(8,128)(2,1)}, bf16[16,192,768]{2,1,0:T(8,128)(2,1)S(1)}, u32[]{:S(2)}, u32[]{:S(2)}) collective-permute-start(bf16[16,192,768]{2,1,0:T(8,128)(2,1)} %bitcast.207), channel_id=1, source_target_pairs={{0,8},{8,0},{16,24},{24,16},{1,9},{9,1},{17,25},{25,17},{2,10},{10... | collective-permute-start | bytes 14155784 | tf_op jit(solution)/shard_map/ppermute | solution.py:28
  211.7 32.2 %collective-permute-start.13 = (bf16[2,4,96,768]{3,2,1,0:T(8,128)(2,1)}, bf16[2,4,96,768]{3,2,1,0:T(8,128)(2,1)}, u32[]{:S(2)}, u32[]{:S(2)}) collective-permute-start(bf16[2,4,96,768]{3,2,1,0:T(8,128)(2,1)} %get-tuple-element.126), channel_id=1, source_target_pairs={{0,16},{8,24},{16,0},{24,8},{1,17},{9,25},{17,1},{25,9},{2,18},{10... | collective-permute-start | bytes 3538952 | tf_op jit(solution)/shard_map/ppermute | solution.py:28
  213.2 35.4 %collective-permute-start.14 = (bf16[2,4,96,768]{3,2,1,0:T(8,128)(2,1)}, bf16[2,4,96,768]{3,2,1,0:T(8,128)(2,1)}, u32[]{:S(2)}, u32[]{:S(2)}) collective-permute-start(bf16[2,4,96,768]{3,2,1,0:T(8,128)(2,1)} %get-tuple-element.128), channel_id=1, source_target_pairs={{0,1},{1,0},{2,3},{3,2},{4,5},{5,4},{6,7},{7,6},{8,9},{9,8},{10,11... | collective-permute-start | bytes 3538952 | tf_op jit(solution)/shard_map/ppermute | solution.py:28
  214.6 35.3 %all-to-all-start.2 = ((bf16[8,8,8,768]{3,2,1,0:T(8,128)(2,1)}), bf16[8,8,8,768]{3,2,1,0:T(8,128)(2,1)S(1)}, u32[]{:S(2)}, u32[]{:S(2)}) async-start(bf16[8,8,8,768]{3,2,1,0:T(8,128)(2,1)} %bitcast.29), calls=%async_computation.2 | async-start | bytes 1572864 | tf_op jit(solution)/shard_map/all_to_all | solution.py:1024
  249.9 37.0 %collective-permute-start.15 = (bf16[16,96,768]{2,1,0:T(8,128)(2,1)}, bf16[16,96,768]{2,1,0:T(8,128)(2,1)}, u32[]{:S(2)}, u32[]{:S(2)}) collective-permute-start(bf16[16,96,768]{2,1,0:T(8,128)(2,1)} %bitcast.211), channel_id=1, source_target_pairs={{0,8},{8,0},{16,24},{24,16},{1,9},{9,1},{17,25},{25,17},{2,10},{10... | collective-permute-start | bytes 7077896 | tf_op jit(solution)/shard_map/ppermute | solution.py:28
  253.0 19.8 %collective-permute-start.16 = (bf16[4,96,768]{2,1,0:T(8,128)(2,1)}, bf16[4,96,768]{2,1,0:T(8,128)(2,1)}, u32[]{:S(2)}, u32[]{:S(2)}) collective-permute-start(bf16[4,96,768]{2,1,0:T(8,128)(2,1)} %slice_bitcast_fusion.12), channel_id=1, source_target_pairs={{0,1},{1,0},{2,3},{3,2},{4,5},{5,4},{6,7},{7,6},{8,9},{9,8},{10,11... | collective-permute-start | bytes 1769480 | tf_op jit(solution)/shard_map/ppermute | solution.py:28
  257.9 26.7 %collective-permute-start.17 = (bf16[4,96,768]{2,1,0:T(8,128)(2,1)}, bf16[4,96,768]{2,1,0:T(8,128)(2,1)}, u32[]{:S(2)}, u32[]{:S(2)}) collective-permute-start(bf16[4,96,768]{2,1,0:T(8,128)(2,1)} %slice_bitcast_fusion.10), channel_id=1, source_target_pairs={{0,16},{8,24},{16,0},{24,8},{1,17},{9,25},{17,1},{25,9},{2,18},{10... | collective-permute-start | bytes 1769480 | tf_op jit(solution)/shard_map/ppermute | solution.py:28
  258.5 33.0 %all-to-all-start.3 = ((bf16[32,2,8,768]{3,2,1,0:T(8,128)(2,1)}), bf16[32,2,8,768]{3,2,1,0:T(8,128)(2,1)S(1)}, u32[]{:S(2)}, u32[]{:S(2)}) async-start(bf16[32,2,8,768]{3,2,1,0:T(8,128)(2,1)} %get-tuple-element.144), calls=%async_computation.3 | async-start | bytes 1572864 | tf_op jit(solution)/shard_map/all_to_all | solution.py:999
  261.3 57.6 %all-gather.9.cloned.1.call-start = ((), (), s32[]{:S(2)}) async-start(), calls=%async_computation.5 | async-start | bytes 3932160 | tf_op jit(solution)/shard_map/all_gather | solution.py:1082
  262.1 144.2 %all-gather.11.cloned.1.call-start = ((), (), s32[]{:S(2)}) async-start(), calls=%async_computation.6 | async-start | bytes 3932160 | tf_op jit(solution)/shard_map/all_gather | solution.py:1111
  291.5 25.9 %collective-permute-start.20 = (bf16[192,768]{1,0:T(8,128)(2,1)}, bf16[192,768]{1,0:T(8,128)(2,1)S(1)}, u32[]{:S(2)}, u32[]{:S(2)}) collective-permute-start(bf16[192,768]{1,0:T(8,128)(2,1)} %get-tuple-element.150), channel_id=1, source_target_pairs={{0,4},{1,5},{2,6},{3,7},{4,0},{5,1},{6,2},{7,3},{8,12},{9,13},{10,... | collective-permute-start | bytes 884744 | tf_op jit(solution)/shard_map/ppermute | solution.py:35
  291.5 25.9 %collective-permute-start.21 = (bf16[192,768]{1,0:T(8,128)(2,1)}, bf16[192,768]{1,0:T(8,128)(2,1)S(1)}, u32[]{:S(2)}, u32[]{:S(2)}) collective-permute-start(bf16[192,768]{1,0:T(8,128)(2,1)} %get-tuple-element.151), channel_id=1, source_target_pairs={{0,2},{1,3},{2,0},{3,1},{4,6},{5,7},{6,4},{7,5},{8,10},{9,11},{10,... | collective-permute-start | bytes 884744 | tf_op jit(solution)/shard_map/ppermute | solution.py:35
  292.0 25.5 %collective-permute-start.22 = (bf16[192,768]{1,0:T(8,128)(2,1)}, bf16[192,768]{1,0:T(8,128)(2,1)S(1)}, u32[]{:S(2)}, u32[]{:S(2)}) collective-permute-start(bf16[192,768]{1,0:T(8,128)(2,1)} %get-tuple-element.152), channel_id=1, source_target_pairs={{0,6},{1,7},{2,4},{3,5},{4,2},{5,3},{6,0},{7,1},{8,14},{9,15},{10,... | collective-permute-start | bytes 884744 | tf_op jit(solution)/shard_map/ppermute | solution.py:35
  295.9 22.5 %collective-permute-start.19 = (bf16[2,4,48,768]{3,2,1,0:T(8,128)(2,1)}, bf16[2,4,48,768]{3,2,1,0:T(8,128)(2,1)S(1)}, u32[]{:S(2)}, u32[]{:S(2)}) collective-permute-start(bf16[2,4,48,768]{3,2,1,0:T(8,128)(2,1)} %get-tuple-element.148), channel_id=1, source_target_pairs={{0,1},{1,0},{2,3},{3,2},{4,5},{5,4},{6,7},{7,6},{8,9},{9,8},{10,11... | collective-permute-start | bytes 1769480 | tf_op jit(solution)/shard_map/ppermute | solution.py:28
  295.9 22.7 %collective-permute-start.18 = (bf16[2,4,48,768]{3,2,1,0:T(8,128)(2,1)}, bf16[2,4,48,768]{3,2,1,0:T(8,128)(2,1)S(1)}, u32[]{:S(2)}, u32[]{:S(2)}) collective-permute-start(bf16[2,4,48,768]{3,2,1,0:T(8,128)(2,1)} %get-tuple-element.146), channel_id=1, source_target_pairs={{0,16},{8,24},{16,0},{24,8},{1,17},{9,25},{17,1},{25,9},{2,18},{10... | collective-permute-start | bytes 1769480 | tf_op jit(solution)/shard_map/ppermute | solution.py:28
  332.9 15.4 %collective-permute-start.26 = (bf16[4,96,768]{2,1,0:T(8,128)(2,1)S(1)}, bf16[4,96,768]{2,1,0:T(8,128)(2,1)S(1)}, u32[]{:S(2)}, u32[]{:S(2)}) collective-permute-start(bf16[4,96,768]{2,1,0:T(8,128)(2,1)S(1)} %get-tuple-element.170), channel_id=1, source_target_pairs={{0,1},{1,0},{2,3},{3,2},{4,5},{5,4},{6,7},{7,6},{8,9},{9,8},{10,11... | collective-permute-start | bytes 1769480 | tf_op jit(solution)/shard_map/ppermute | solution.py:28
  333.4 16.3 %collective-permute-start.27 = (bf16[4,96,768]{2,1,0:T(8,128)(2,1)S(1)}, bf16[4,96,768]{2,1,0:T(8,128)(2,1)S(1)}, u32[]{:S(2)}, u32[]{:S(2)}) collective-permute-start(bf16[4,96,768]{2,1,0:T(8,128)(2,1)S(1)} %get-tuple-element.171), channel_id=1, source_target_pairs={{0,16},{8,24},{16,0},{24,8},{1,17},{9,25},{17,1},{25,9},{2,18},{10... | collective-permute-start | bytes 1769480 | tf_op jit(solution)/shard_map/ppermute | solution.py:28
  334.8 26.6 %collective-permute-start.28 = (bf16[4,96,768]{2,1,0:T(8,128)(2,1)S(1)}, bf16[4,96,768]{2,1,0:T(8,128)(2,1)S(1)}, u32[]{:S(2)}, u32[]{:S(2)}) collective-permute-start(bf16[4,96,768]{2,1,0:T(8,128)(2,1)S(1)} %get-tuple-element.172), channel_id=1, source_target_pairs={{0,17},{1,16},{2,19},{3,18},{4,21},{5,20},{6,23},{7,22},{8,25},{9,... | collective-permute-start | bytes 1769480 | tf_op jit(solution)/shard_map/ppermute | solution.py:42
  374.6 15.6 %collective-permute-start.33 = (bf16[1,96,768]{2,1,0:T(8,128)(2,1)S(1)}, bf16[1,96,768]{2,1,0:T(8,128)(2,1)S(1)}, u32[]{:S(2)}, u32[]{:S(2)}) collective-permute-start(bf16[1,96,768]{2,1,0:T(8,128)(2,1)S(1)} %bitcast.201), channel_id=1, source_target_pairs={{0,4},{1,5},{2,6},{3,7},{4,0},{5,1},{6,2},{7,3},{8,12},{9,13},{10,... | collective-permute-start | bytes 442376 | tf_op jit(solution)/shard_map/ppermute | solution.py:28
  (57 other events, 683.2 us)
Sparse Core Ops, SparseCore 0:
  15.5 132.9 all-gather.6
  263.7 38.3 all-gather.8
  362.6 26.9 all-gather.10

commit v5 on v4

--- a/solution.py
+++ b/solution.py
@@ -1051,9 +1051,9 @@
         meta_s, own, frames, PATCHES, hot_s, mst_s, None, chain_s.state, place, n_tp, heads,
         x1_shape, BF,
     )
+    grad_rows = input_to_places(after(grad_out, *chain_s.state))
     x1 = to_places(x1_frames)
-    x1, grad_in = stage([], x1, grad_out)
-    grad_rows = input_to_places(grad_in)
+    x1, grad_rows = stage([], x1, grad_rows)
     x2, h2, qkv2, p2, o2, a2 = forward(
         meta0, x1, blocks, rows, hot_t, mst_t, keys, late_t, None, n_tp, heads, x1.shape, F32
     )

time: 424 us -> 431 us (1.017)
  waiting for transfers between devices: 134 us -> 147 us
    all_to_all x1, waiting for transfers between devices: 2.17 us -> 23.2 us  [input_to_places(): got = lax.all_to_all(split, 'sp', 0, 0, tiled=True)]
    all_to_all x2, waiting for transfers between devices: 28.4 us -> 19.6 us  [exchange(): return lax.all_to_all(value, ('sp', 'tp'), 0, 0, tiled=True)]
    unnamed x70 -> x54, local copies, waits for them, and re-layouts: 14.3 us -> 12.9 us
  transfers between devices with their start and end apart: 50 -> 50, of which waited for: 26 -> 26; matrix products, arithmetic and copies ran while one was open for 10% -> 9% of each run, Pallas kernels for 26% -> 22%
where the time goes in v5:
time: 431 us; the launch traced here: 425 us
  waiting for transfers between devices  147 us (34%)
  Pallas kernels  122 us (28%)
  starting transfers between devices  77.1 us (18%)
  local copies, waits for them, and re-layouts  34.1 us (8%)
  other arithmetic  25.3 us (6%)
  between operations  14.6 us (3%)
    ppermute x20, waiting for transfers between devices, swap(): return lax.ppermute(value, axis, [(i, i ^ 1 << bit) for i in range(size)])  67.4 us
    pallas_call x2, Pallas kernels, forward(): pl.pallas_call(functools.partial(forward_kernel, place, heads, masked, zi...  34.9 us
    pallas_call x2, Pallas kernels, feed_half(): pl.pallas_call(functools.partial(feed_kernel, masks, last_call), out_shap...  31.2 us
    ppermute x13, starting transfers between devices, run(): lax.ppermute(value, axis, [(i, i ^ m) for i in range(size)])  26.7 us
    pallas_call x1, Pallas kernels, backward(): pl.pallas_call(functools.partial(back_kernel, masks, heads), out_shape=[j...  25 us
    all_to_all x1, waiting for transfers between devices, input_to_places(): got = lax.all_to_all(split, 'sp', 0, 0, tiled=True)  23.2 us
    pallas_call x1, Pallas kernels, backward_grads(): pl.pallas_call(functools.partial(back_grads_kernel, place, masks, heads),...  20.9 us
    all_to_all x2, waiting for transfers between devices, exchange(): return lax.all_to_all(value, ('sp', 'tp'), 0, 0, tiled=True)  19.6 us
  transfers between devices with their start and end apart: 50, of which 26 were waited for; matrix products, arithmetic and copies ran while one was open for 9% of the time, Pallas kernels for 22%

profile of v5, /device:TPU:0, one launch (start us, length us, event | category | flops | bytes accessed | tf_op | source)
XLA Modules:
  0.0 424.8 jit_solution(2505137680537656949)
XLA Ops:
  26.7 4.3 %collective-permute-done.3 = f32[4,6912]{1,0:T(4,128)S(1)} collective-permute-done((f32[4,6912]{1,0:T(4,128)S(1)}, f32[4,6912]{1,0:T(4,128)S(1)}, u32[]{:S(2)}, u32[]{:S(2)}) %collective-permute-start.3) | collective-permute-done | bytes 110624 | tf_op jit(solution)/shard_map/ppermute | solution.py:215
  31.1 4.2 collective-permute-done.2
  36.4 8.0 %collective-permute-start.6 = (f32[4,6912]{1,0:T(4,128)S(1)}, f32[4,6912]{1,0:T(4,128)S(1)}, u32[]{:S(2)}, u32[]{:S(2)}) collective-permute-start(f32[4,6912]{1,0:T(4,128)S(1)} %add.153), channel_id=1, source_target_pairs={{0,2},{1,3},{2,0},{3,1},{4,6},{5,7},{6,4},{7,5},{8,10},{9,11},{10,... | collective-permute-start | bytes 331784 | tf_op jit(solution)/shard_map/ppermute | solution.py:215
  55.8 5.7 %collective-permute-done.5 = bf16[4,48,768]{2,1,0:T(8,128)(2,1)S(1)} collective-permute-done((bf16[4,48,768]{2,1,0:T(8,128)(2,1)S(1)}, bf16[4,48,768]{2,1,0:T(8,128)(2,1)S(1)}, u32[]{:S(2)}, u32[]{:S(2)}) %collective-permute-start.5) | collective-permute-done | bytes 294944 | tf_op jit(solution)/shard_map/ppermute | solution.py:28
  67.3 10.2 %collective-permute-done.10 = bf16[8,48,768]{2,1,0:T(8,128)(2,1)S(1)} collective-permute-done((bf16[8,48,768]{2,1,0:T(8,128)(2,1)S(1)}, bf16[8,48,768]{2,1,0:T(8,128)(2,1)S(1)}, u32[]{:S(2)}, u32[]{:S(2)}) %collective-permute-start.10) | collective-permute-done | bytes 589856 | tf_op jit(solution)/shard_map/ppermute | solution.py:28
  83.9 4.4 %collective-permute-done.11.refs_1_ = bf16[32,48,768]{2,1,0:T(8,128)(2,1)} collective-permute-done((bf16[32,48,768]{2,1,0:T(8,128)(2,1)}, bf16[32,48,768]{2,1,0:T(8,128)(2,1)}, u32[]{:S(2)}, u32[]{:S(2)}) %collective-permute-start.11) | collective-permute-done | bytes 2359328 | tf_op jit(solution)/shard_map/ppermute | solution.py:28
  89.3 6.3 %all-to-all-start.1 = ((bf16[8,8,8,768]{3,2,1,0:T(8,128)(2,1)}), bf16[8,8,8,768]{3,2,1,0:T(8,128)(2,1)S(1)}, u32[]{:S(2)}, u32[]{:S(2)}) async-start(bf16[8,8,8,768]{3,2,1,0:T(8,128)(2,1)} %copy_bitcast_fusion), calls=%async_computation.1 | async-start | bytes 1572864 | tf_op jit(solution)/shard_map/all_to_all | solution.py:1016
  95.8 18.1 %shard_map.186 = (bf16[32,2,8,768]{3,2,1,0:T(8,128)(2,1)}, bf16[2,256,768]{2,1,0:T(8,128)(2,1)S(1)}, bf16[2,4,256,576]{3,2,1,0:T(8,128)(2,1)}, bf16[2,12,256,256...) custom-call(s32[3]{0:T(128)S(1)} %add_add_fusion.2.meta, ...), custom_call_target="tpu_custom_call" | custom-call | flops 20000000000 | bytes 1024 | tf_op jit(solution)/shard_map/pallas_call | solution.py:438
  114.8 23.2 %all-to-all-done.1 = bf16[8,8,8,768]{3,2,1,0:T(8,128)(2,1)S(1)} async-done(((bf16[8,8,8,768]{3,2,1,0:T(8,128)(2,1)}), bf16[8,8,8,768]{3,2,1,0:T(8,128)(2,1)S(1)}, u32[]{:S(2)}, u32[]{:S(2)}) %all-to-all-start.1) | async-done | bytes 786464 | tf_op jit(solution)/shard_map/all_to_all | solution.py:1016
  142.7 19.6 %all-to-all-done.x = bf16[32,2,8,768]{3,2,1,0:T(8,128)(2,1)S(1)} async-done(((bf16[32,2,8,768]{3,2,1,0:T(8,128)(2,1)}), bf16[32,2,8,768]{3,2,1,0:T(8,128)(2,1)S(1)}, u32[]{:S(2)}, u32[]{:S(2)}) %all-to-all-start) | async-done | bytes 786464 | tf_op jit(solution)/shard_map/all_to_all | solution.py:999
  163.2 16.8 %shard_map.187 = (f32[32,2,8,768]{3,2,1,0:T(8,128)}, bf16[2,256,768]{2,1,0:T(8,128)(2,1)S(1)}, bf16[2,4,256,576]{3,2,1,0:T(8,128)(2,1)}, bf16[2,12,256,256]{3,2,...) custom-call(s32[3]{0:T(128)S(1)} %add_add_fusion.1.meta, ...), custom_call_target="tpu_custom_call" | custom-call | flops 20000000000 | bytes 1024 | tf_op jit(solution)/shard_map/pallas_call | solution.py:438
  180.0 14.0 %shard_map.188 = (f32[512,768]{1,0:T(8,128)}, f32[512,768]{1,0:T(8,128)}, bf16[2,8,2,96,768]{4,3,2,1,0:T(8,128)(2,1)}) custom-call(s32[3]{0:T(128)S(1)} %add_add_fusion.1.meta, f32[512,768]{1,0:T(8,128)} %bitcast.184, bf16[512,768]{1,0:T(8,128)(2,1)S(1)} %bitcast.171, bf16[512,8]{1,0:T(8,128)(2,1)S(1)} %concatenate.55.hot, bf16[4,512]{1,0:T(4,128)(2,1)S(1)} %fusion.30.hot_t, ...), custom_call_target="tpu_custom_call" | custom-call | flops 1000000000 | bytes 1024 | tf_op jit(solution)/shard_map/pallas_call | solution.py:891
  194.1 17.1 %shard_map.189 = (bf16[512,768]{1,0:T(8,128)(2,1)}, f32[512,768]{1,0:T(8,128)}, f32[4,2304]{1,0:T(4,128)S(1)}, bf16[2,8,2,96,768]{4,3,2,1,0:T(8,128)(2,1)}) custom-call(s32[3]{0:T(128)S(1)} %add_add_fusion.1.meta, f32[512,768]{1,0:T(8,128)} %bitcast.185, bf16[512,768]{1,0:T(8,128)(2,1)S(1)} %bitcast.172, bf16[512,8]{1,0:T(8,128)(2,1)S(1)} %concatenate.55.hot, ...), custom_call_target="tpu_custom_call" | custom-call | flops 1000000000 | bytes 1024 | tf_op jit(solution)/shard_map/pallas_call | solution.py:891
  225.3 25.0 %shard_map.190 = (bf16[32,2,8,768]{3,2,1,0:T(8,128)(2,1)}, f32[4,2304]{1,0:T(4,128)S(1)}, bf16[2,8,96,768]{3,2,1,0:T(8,128)(2,1)}, bf16[2,8,96,768]{3,2,1,0:T(8,128)(2,1)}) custom-call(s32[3]{0:T(128)S(1)} %add_add_fusion.1.meta, f32[32,2,8,768]{3,2,1,0:T(8,128)} %bitcast.212, bf16[32,2,8,768]{3,2,1,0:T(8,128)(2,1)S(1)} %copy-done.3, ...), custom_call_target="tpu_custom_call" | custom-call | flops 20000000000 | bytes 1024 | tf_op jit(solution)/shard_map/pallas_call | solution.py:618
  250.3 5.0 %collective-permute-done.14 = bf16[2,4,96,768]{3,2,1,0:T(8,128)(2,1)} collective-permute-done((bf16[2,4,96,768]{3,2,1,0:T(8,128)(2,1)}, bf16[2,4,96,768]{3,2,1,0:T(8,128)(2,1)}, u32[]{:S(2)}, u32[]{:S(2)}) %collective-permute-start.14) | collective-permute-done | bytes 1179680 | tf_op jit(solution)/shard_map/ppermute | solution.py:28
  268.6 11.1 %collective-permute-done.16 = bf16[4,96,768]{2,1,0:T(8,128)(2,1)} collective-permute-done((bf16[4,96,768]{2,1,0:T(8,128)(2,1)}, bf16[4,96,768]{2,1,0:T(8,128)(2,1)}, u32[]{:S(2)}, u32[]{:S(2)}) %collective-permute-start.16) | collective-permute-done | bytes 589856 | tf_op jit(solution)/shard_map/ppermute | solution.py:28
  281.0 10.4 %collective-permute-done.17 = bf16[4,96,768]{2,1,0:T(8,128)(2,1)} collective-permute-done((bf16[4,96,768]{2,1,0:T(8,128)(2,1)}, bf16[4,96,768]{2,1,0:T(8,128)(2,1)}, u32[]{:S(2)}, u32[]{:S(2)}) %collective-permute-start.17) | collective-permute-done | bytes 589856 | tf_op jit(solution)/shard_map/ppermute | solution.py:28
  298.5 4.4 %collective-permute-start.22 = (bf16[192,768]{1,0:T(8,128)(2,1)}, bf16[192,768]{1,0:T(8,128)(2,1)S(1)}, u32[]{:S(2)}, u32[]{:S(2)}) collective-permute-start(bf16[192,768]{1,0:T(8,128)(2,1)} %get-tuple-element.154), channel_id=1, source_target_pairs={{0,6},{1,7},{2,4},{3,5},{4,2},{5,3},{6,0},{7,1},{8,14},{9,15},{10,... | collective-permute-start | bytes 884744 | tf_op jit(solution)/shard_map/ppermute | solution.py:35
  303.4 20.9 %shard_map.191 = (bf16[2,4,256,576]{3,2,1,0:T(8,128)(2,1)}, bf16[2,8,96,768]{3,2,1,0:T(8,128)(2,1)}, bf16[2,8,96,768]{3,2,1,0:T(8,128)(2,1)}) custom-call(s32[3]{0:T(128)S(1)} %add_add_fusion.1.meta, bf16[32,2,8,768]{3,2,1,0:T(8,128)(2,1)S(1)} %all-to-all-done.3.dx, bf16[2,256,8]{2,1,0:T(8,128)(2,1)S(1)} %concatenate.45.hot, ...), custom_call_target="tpu_custom_call" | custom-call | flops 20000000000 | bytes 1024 | tf_op jit(solution)/shard_map/pallas_call | solution.py:685
  330.2 6.1 %collective-permute-done.24 = bf16[4,48,768]{2,1,0:T(8,128)(2,1)S(1)} collective-permute-done((bf16[4,48,768]{2,1,0:T(8,128)(2,1)S(1)}, bf16[4,48,768]{2,1,0:T(8,128)(2,1)S(1)}, u32[]{:S(2)}, u32[]{:S(2)}) %collective-permute-start.24) | collective-permute-done | bytes 294944 | tf_op jit(solution)/shard_map/ppermute | solution.py:28
  344.3 10.4 %shard_map.192 = (bf16[2,256,768]{2,1,0:T(8,128)(2,1)}, f32[4,2304]{1,0:T(4,128)S(1)}) custom-call(s32[3]{0:T(128)S(1)} %add_add_fusion.2.meta, bf16[32,2,8,768]{3,2,1,0:T(8,128)(2,1)S(1)} %all-to-all-done.3.dx, bf16[8,256,768]{2,1,0:T(8,128)(2,1)} %bitcast.209, bf16[2,256,8]{2,1,0:T(8,128)(2,1)S(1)} %concatenate.45.hot, ...), custom_call_target="tpu_custom_call" | custom-call | flops 20000000000 | bytes 1024 | tf_op jit(solution)/shard_map/pallas_call | solution.py:745
  357.3 11.9 %collective-permute-done.28 = bf16[4,96,768]{2,1,0:T(8,128)(2,1)S(1)} collective-permute-done((bf16[4,96,768]{2,1,0:T(8,128)(2,1)S(1)}, bf16[4,96,768]{2,1,0:T(8,128)(2,1)S(1)}, u32[]{:S(2)}, u32[]{:S(2)}) %collective-permute-start.28) | collective-permute-done | bytes 589856 | tf_op jit(solution)/shard_map/ppermute | solution.py:42
  389.4 4.2 collective-permute-start.38
  393.7 4.4 %collective-permute-done.33 = bf16[1,96,768]{2,1,0:T(8,128)(2,1)S(1)} collective-permute-done((bf16[1,96,768]{2,1,0:T(8,128)(2,1)S(1)}, bf16[1,96,768]{2,1,0:T(8,128)(2,1)S(1)}, u32[]{:S(2)}, u32[]{:S(2)}) %collective-permute-start.33) | collective-permute-done | bytes 147488 | tf_op jit(solution)/shard_map/ppermute | solution.py:28
  (237 shorter events, 144.4 us)
Async XLA Ops:
  7.2 155.1 %all-gather.7.cloned.1.call-start = ((), (), s32[]{:S(2)}) async-start(), calls=%async_computation.4 | async-start | bytes 14598144 | tf_op jit(solution)/shard_map/all_gather | solution.py:1037
  36.4 15.3 %collective-permute-start.6 = (f32[4,6912]{1,0:T(4,128)S(1)}, f32[4,6912]{1,0:T(4,128)S(1)}, u32[]{:S(2)}, u32[]{:S(2)}) collective-permute-start(f32[4,6912]{1,0:T(4,128)S(1)} %add.153), channel_id=1, source_target_pairs={{0,2},{1,3},{2,0},{3,1},{4,6},{5,7},{6,4},{7,5},{8,10},{9,11},{10,... | collective-permute-start | bytes 331784 | tf_op jit(solution)/shard_map/ppermute | solution.py:215
  66.0 15.7 %collective-permute-start.9 = (bf16[8,48,768]{2,1,0:T(8,128)(2,1)S(1)}, bf16[8,48,768]{2,1,0:T(8,128)(2,1)S(1)}, u32[]{:S(2)}, u32[]{:S(2)}) collective-permute-start(bf16[8,48,768]{2,1,0:T(8,128)(2,1)S(1)} %pad_maximum_fusion.2), channel_id=1, source_target_pairs={{0,16},{8,24},{16,0},{24,8},{1,17},{9,25},{17,1},{25,9},{2,18},{10... | collective-permute-start | bytes 1769480 | tf_op jit(solution)/shard_map/ppermute | solution.py:28
  89.3 48.7 %all-to-all-start.1 = ((bf16[8,8,8,768]{3,2,1,0:T(8,128)(2,1)}), bf16[8,8,8,768]{3,2,1,0:T(8,128)(2,1)S(1)}, u32[]{:S(2)}, u32[]{:S(2)}) async-start(bf16[8,8,8,768]{3,2,1,0:T(8,128)(2,1)} %copy_bitcast_fusion), calls=%async_computation.1 | async-start | bytes 1572864 | tf_op jit(solution)/shard_map/all_to_all | solution.py:1016
  138.0 24.3 %all-to-all-start = ((bf16[32,2,8,768]{3,2,1,0:T(8,128)(2,1)}), bf16[32,2,8,768]{3,2,1,0:T(8,128)(2,1)S(1)}, u32[]{:S(2)}, u32[]{:S(2)}) async-start(bf16[32,2,8,768]{3,2,1,0:T(8,128)(2,1)} %get-tuple-element.116), calls=%async_computation | async-start | bytes 1572864 | tf_op jit(solution)/shard_map/all_to_all | solution.py:999
  194.1 17.2 %collective-permute-start.12 = (bf16[16,192,768]{2,1,0:T(8,128)(2,1)}, bf16[16,192,768]{2,1,0:T(8,128)(2,1)S(1)}, u32[]{:S(2)}, u32[]{:S(2)}) collective-permute-start(bf16[16,192,768]{2,1,0:T(8,128)(2,1)} %bitcast.207), channel_id=1, source_target_pairs={{0,8},{8,0},{16,24},{24,16},{1,9},{9,1},{17,25},{25,17},{2,10},{10... | collective-permute-start | bytes 14155784 | tf_op jit(solution)/shard_map/ppermute | solution.py:28
  218.4 31.9 %collective-permute-start.13 = (bf16[2,4,96,768]{3,2,1,0:T(8,128)(2,1)}, bf16[2,4,96,768]{3,2,1,0:T(8,128)(2,1)}, u32[]{:S(2)}, u32[]{:S(2)}) collective-permute-start(bf16[2,4,96,768]{3,2,1,0:T(8,128)(2,1)} %get-tuple-element.128), channel_id=1, source_target_pairs={{0,16},{8,24},{16,0},{24,8},{1,17},{9,25},{17,1},{25,9},{2,18},{10... | collective-permute-start | bytes 3538952 | tf_op jit(solution)/shard_map/ppermute | solution.py:28
  219.8 35.4 %collective-permute-start.14 = (bf16[2,4,96,768]{3,2,1,0:T(8,128)(2,1)}, bf16[2,4,96,768]{3,2,1,0:T(8,128)(2,1)}, u32[]{:S(2)}, u32[]{:S(2)}) collective-permute-start(bf16[2,4,96,768]{3,2,1,0:T(8,128)(2,1)} %get-tuple-element.130), channel_id=1, source_target_pairs={{0,1},{1,0},{2,3},{3,2},{4,5},{5,4},{6,7},{7,6},{8,9},{9,8},{10,11... | collective-permute-start | bytes 3538952 | tf_op jit(solution)/shard_map/ppermute | solution.py:28
  221.3 35.3 %all-to-all-start.2 = ((bf16[8,8,8,768]{3,2,1,0:T(8,128)(2,1)}), bf16[8,8,8,768]{3,2,1,0:T(8,128)(2,1)S(1)}, u32[]{:S(2)}, u32[]{:S(2)}) async-start(bf16[8,8,8,768]{3,2,1,0:T(8,128)(2,1)} %bitcast.29), calls=%async_computation.2 | async-start | bytes 1572864 | tf_op jit(solution)/shard_map/all_to_all | solution.py:1024
  256.5 37.3 %collective-permute-start.15 = (bf16[16,96,768]{2,1,0:T(8,128)(2,1)}, bf16[16,96,768]{2,1,0:T(8,128)(2,1)}, u32[]{:S(2)}, u32[]{:S(2)}) collective-permute-start(bf16[16,96,768]{2,1,0:T(8,128)(2,1)} %bitcast.211), channel_id=1, source_target_pairs={{0,8},{8,0},{16,24},{24,16},{1,9},{9,1},{17,25},{25,17},{2,10},{10... | collective-permute-start | bytes 7077896 | tf_op jit(solution)/shard_map/ppermute | solution.py:28
  259.6 20.1 %collective-permute-start.16 = (bf16[4,96,768]{2,1,0:T(8,128)(2,1)}, bf16[4,96,768]{2,1,0:T(8,128)(2,1)}, u32[]{:S(2)}, u32[]{:S(2)}) collective-permute-start(bf16[4,96,768]{2,1,0:T(8,128)(2,1)} %slice_bitcast_fusion.12), channel_id=1, source_target_pairs={{0,1},{1,0},{2,3},{3,2},{4,5},{5,4},{6,7},{7,6},{8,9},{9,8},{10,11... | collective-permute-start | bytes 1769480 | tf_op jit(solution)/shard_map/ppermute | solution.py:28
  264.6 26.8 %collective-permute-start.17 = (bf16[4,96,768]{2,1,0:T(8,128)(2,1)}, bf16[4,96,768]{2,1,0:T(8,128)(2,1)}, u32[]{:S(2)}, u32[]{:S(2)}) collective-permute-start(bf16[4,96,768]{2,1,0:T(8,128)(2,1)} %slice_bitcast_fusion.10), channel_id=1, source_target_pairs={{0,16},{8,24},{16,0},{24,8},{1,17},{9,25},{17,1},{25,9},{2,18},{10... | collective-permute-start | bytes 1769480 | tf_op jit(solution)/shard_map/ppermute | solution.py:28
  265.2 33.3 %all-to-all-start.3 = ((bf16[32,2,8,768]{3,2,1,0:T(8,128)(2,1)}), bf16[32,2,8,768]{3,2,1,0:T(8,128)(2,1)S(1)}, u32[]{:S(2)}, u32[]{:S(2)}) async-start(bf16[32,2,8,768]{3,2,1,0:T(8,128)(2,1)} %get-tuple-element.146), calls=%async_computation.3 | async-start | bytes 1572864 | tf_op jit(solution)/shard_map/all_to_all | solution.py:999
  267.8 58.6 %all-gather.9.cloned.1.call-start = ((), (), s32[]{:S(2)}) async-start(), calls=%async_computation.5 | async-start | bytes 3932160 | tf_op jit(solution)/shard_map/all_gather | solution.py:1082
  268.6 145.5 %all-gather.11.cloned.1.call-start = ((), (), s32[]{:S(2)}) async-start(), calls=%async_computation.6 | async-start | bytes 3932160 | tf_op jit(solution)/shard_map/all_gather | solution.py:1111
  298.5 25.9 %collective-permute-start.20 = (bf16[192,768]{1,0:T(8,128)(2,1)}, bf16[192,768]{1,0:T(8,128)(2,1)S(1)}, u32[]{:S(2)}, u32[]{:S(2)}) collective-permute-start(bf16[192,768]{1,0:T(8,128)(2,1)} %get-tuple-element.152), channel_id=1, source_target_pairs={{0,4},{1,5},{2,6},{3,7},{4,0},{5,1},{6,2},{7,3},{8,12},{9,13},{10,... | collective-permute-start | bytes 884744 | tf_op jit(solution)/shard_map/ppermute | solution.py:35
  298.5 25.9 %collective-permute-start.21 = (bf16[192,768]{1,0:T(8,128)(2,1)}, bf16[192,768]{1,0:T(8,128)(2,1)S(1)}, u32[]{:S(2)}, u32[]{:S(2)}) collective-permute-start(bf16[192,768]{1,0:T(8,128)(2,1)} %get-tuple-element.153), channel_id=1, source_target_pairs={{0,2},{1,3},{2,0},{3,1},{4,6},{5,7},{6,4},{7,5},{8,10},{9,11},{10,... | collective-permute-start | bytes 884744 | tf_op jit(solution)/shard_map/ppermute | solution.py:35
  298.5 25.9 %collective-permute-start.22 = (bf16[192,768]{1,0:T(8,128)(2,1)}, bf16[192,768]{1,0:T(8,128)(2,1)S(1)}, u32[]{:S(2)}, u32[]{:S(2)}) collective-permute-start(bf16[192,768]{1,0:T(8,128)(2,1)} %get-tuple-element.154), channel_id=1, source_target_pairs={{0,6},{1,7},{2,4},{3,5},{4,2},{5,3},{6,0},{7,1},{8,14},{9,15},{10,... | collective-permute-start | bytes 884744 | tf_op jit(solution)/shard_map/ppermute | solution.py:35
  302.8 22.5 %collective-permute-start.19 = (bf16[2,4,48,768]{3,2,1,0:T(8,128)(2,1)}, bf16[2,4,48,768]{3,2,1,0:T(8,128)(2,1)S(1)}, u32[]{:S(2)}, u32[]{:S(2)}) collective-permute-start(bf16[2,4,48,768]{3,2,1,0:T(8,128)(2,1)} %get-tuple-element.150), channel_id=1, source_target_pairs={{0,1},{1,0},{2,3},{3,2},{4,5},{5,4},{6,7},{7,6},{8,9},{9,8},{10,11... | collective-permute-start | bytes 1769480 | tf_op jit(solution)/shard_map/ppermute | solution.py:28
  302.8 23.4 %collective-permute-start.18 = (bf16[2,4,48,768]{3,2,1,0:T(8,128)(2,1)}, bf16[2,4,48,768]{3,2,1,0:T(8,128)(2,1)S(1)}, u32[]{:S(2)}, u32[]{:S(2)}) collective-permute-start(bf16[2,4,48,768]{3,2,1,0:T(8,128)(2,1)} %get-tuple-element.148), channel_id=1, source_target_pairs={{0,16},{8,24},{16,0},{24,8},{1,17},{9,25},{17,1},{25,9},{2,18},{10... | collective-permute-start | bytes 1769480 | tf_op jit(solution)/shard_map/ppermute | solution.py:28
  340.7 15.4 %collective-permute-start.26 = (bf16[4,96,768]{2,1,0:T(8,128)(2,1)S(1)}, bf16[4,96,768]{2,1,0:T(8,128)(2,1)S(1)}, u32[]{:S(2)}, u32[]{:S(2)}) collective-permute-start(bf16[4,96,768]{2,1,0:T(8,128)(2,1)S(1)} %get-tuple-element.172), channel_id=1, source_target_pairs={{0,1},{1,0},{2,3},{3,2},{4,5},{5,4},{6,7},{7,6},{8,9},{9,8},{10,11... | collective-permute-start | bytes 1769480 | tf_op jit(solution)/shard_map/ppermute | solution.py:28
  341.0 16.3 %collective-permute-start.27 = (bf16[4,96,768]{2,1,0:T(8,128)(2,1)S(1)}, bf16[4,96,768]{2,1,0:T(8,128)(2,1)S(1)}, u32[]{:S(2)}, u32[]{:S(2)}) collective-permute-start(bf16[4,96,768]{2,1,0:T(8,128)(2,1)S(1)} %get-tuple-element.173), channel_id=1, source_target_pairs={{0,16},{8,24},{16,0},{24,8},{1,17},{9,25},{17,1},{25,9},{2,18},{10... | collective-permute-start | bytes 1769480 | tf_op jit(solution)/shard_map/ppermute | solution.py:28
  342.5 26.7 %collective-permute-start.28 = (bf16[4,96,768]{2,1,0:T(8,128)(2,1)S(1)}, bf16[4,96,768]{2,1,0:T(8,128)(2,1)S(1)}, u32[]{:S(2)}, u32[]{:S(2)}) collective-permute-start(bf16[4,96,768]{2,1,0:T(8,128)(2,1)S(1)} %get-tuple-element.174), channel_id=1, source_target_pairs={{0,17},{1,16},{2,19},{3,18},{4,21},{5,20},{6,23},{7,22},{8,25},{9,... | collective-permute-start | bytes 1769480 | tf_op jit(solution)/shard_map/ppermute | solution.py:42
  382.2 15.9 %collective-permute-start.33 = (bf16[1,96,768]{2,1,0:T(8,128)(2,1)S(1)}, bf16[1,96,768]{2,1,0:T(8,128)(2,1)S(1)}, u32[]{:S(2)}, u32[]{:S(2)}) collective-permute-start(bf16[1,96,768]{2,1,0:T(8,128)(2,1)S(1)} %bitcast.201), channel_id=1, source_target_pairs={{0,4},{1,5},{2,6},{3,7},{4,0},{5,1},{6,2},{7,3},{8,12},{9,13},{10,... | collective-permute-start | bytes 442376 | tf_op jit(solution)/shard_map/ppermute | solution.py:28
  (49 other events, 573.6 us)
Sparse Core Ops, SparseCore 0:
  15.4 132.5 all-gather.6
  270.2 38.3 all-gather.8
  370.4 26.8 all-gather.10
